TPU v7x, 256 devices: a whole 4x4x8 slice. The times are simulated.
256 devices in a mesh: dp: 16 (over z, core), expert: 16 (over y, x).
Axes of the slice: x: 4, y: 4, z: 8, core: 2. Of those that a mesh axis runs over, the one named last changes fastest.
Arguments:
- cotangent: bfloat16 [32768, 2048], P(('dp', 'expert')), may hold values from -6 to 6
- saved_gate_up: bfloat16 [32768, 8, 1536], P(('dp', 'expert')), may hold values from -6 to 6
- route_ids: int32 [32768, 8], P(('dp', 'expert')), may hold values from 0 to 31, all different within a row; in each aligned block of 128 rows (0 to 127, 128 to 255, ...) at most 64 rows name the same one
- route_weights: float32 [32768, 8], P(('dp', 'expert')), may hold values from 0.05 to 1
- w_down: bfloat16 [32, 768, 2048], P('expert', 'dp'), may hold values from -0.21875 to 0.21875
Outputs:
- grad_gate_up: bfloat16 [32768, 8, 1536], P(('dp', 'expert'))
- route_grad: float32 [32768, 8], P(('dp', 'expert'))
- grad_down: float32 [32, 768, 2048], P('expert', 'dp')
Inputs may be any that keep to these rules, and one draw needn't show every extreme that they name: `route_ids`: within the rows of one device (aligned blocks of 128 tokens), no expert is named by more than 64 routes, and in every draw some expert is named by exactly 64; the 8 experts of a token are distinct.
All inputs are finite; a program needn't handle non-finite values.
Results may differ from a plain program's by a relative error of at most 0.02.
Values may be sent and summed in bfloat16 or wider, within the bound.
A program may use at most 128 MiB of HBM per device.

v0:
```python
import jax
import jax.numpy as jnp
from jax import lax
from jax.sharding import PartitionSpec as P


def slot_positions(flat_ids, experts, capacity):
    onehot = (flat_ids[:, None] == jnp.arange(experts, dtype=jnp.int32)[None, :]).astype(jnp.int32)
    before = jnp.cumsum(onehot, axis=0) - onehot
    slot = jnp.sum(before * onehot, axis=1)
    return flat_ids * capacity + slot


def local(cotangent, saved_gate_up, route_ids, route_weights, w_down):
    tokens, top = route_ids.shape
    width = cotangent.shape[1]
    hidden_units = saved_gate_up.shape[2] // 2
    owners = lax.axis_size("expert")
    local_experts = w_down.shape[0]
    experts = local_experts * owners
    capacity = min(tokens, 2 * tokens * top // experts)
    routes = tokens * top
    gate = saved_gate_up[:, :, :hidden_units].astype(jnp.float32)
    up = saved_gate_up[:, :, hidden_units:].astype(jnp.float32)
    sig = jax.nn.sigmoid(gate)
    act = gate * sig
    hidden = (act * up).astype(jnp.bfloat16)
    weights = route_weights[:, :, None]
    scaled = (weights * hidden.astype(jnp.float32)).astype(jnp.bfloat16)
    flat_ids = route_ids.reshape(routes)
    position = slot_positions(flat_ids, experts, capacity)
    source = (
        jnp.full((experts * capacity,), routes, jnp.int32)
        .at[position]
        .set(jnp.arange(routes, dtype=jnp.int32))
    )
    dy_rows = jnp.concatenate([cotangent, jnp.zeros((1, width), cotangent.dtype)], 0)[source // top]
    h_rows = jnp.concatenate(
        [scaled.reshape(routes, hidden_units), jnp.zeros((1, hidden_units), jnp.bfloat16)], 0
    )[source]
    dy_send = dy_rows.reshape(owners, local_experts, capacity, width)
    h_send = h_rows.reshape(owners, local_experts, capacity, hidden_units)
    full_down = lax.all_gather(w_down, "dp", axis=1, tiled=True)
    dy_recv, h_recv = (
        lax.all_to_all(dy_send, "expert", split_axis=0, concat_axis=2, tiled=True),
        lax.all_to_all(h_send, "expert", split_axis=0, concat_axis=2, tiled=True),
    )
    dy_recv = dy_recv[0]
    h_recv = h_recv[0]
    grads = jnp.einsum(
        "jsd,jfd->jsf", dy_recv, full_down, preferred_element_type=jnp.float32
    ).astype(jnp.bfloat16)
    back = lax.all_to_all(
        grads.reshape(1, local_experts, owners * capacity, hidden_units),
        "expert",
        split_axis=2,
        concat_axis=0,
        tiled=True,
    )
    summed = lax.psum_scatter(
        jnp.einsum("jsn,jsd->njd", h_recv, dy_recv, preferred_element_type=jnp.float32).astype(
            jnp.bfloat16
        ),
        "dp",
        scatter_dimension=0,
        tiled=True,
    ).astype(jnp.float32)
    grad_down = jnp.transpose(summed, (1, 0, 2))
    returned_rows = back.reshape(experts * capacity, hidden_units)[position]
    qf = returned_rows.reshape(tokens, top, hidden_units).astype(jnp.float32)
    route_grad = jnp.sum(qf * hidden.astype(jnp.float32), -1)
    d_hidden = weights * qf
    d_gate = d_hidden * up * sig * (1.0 + gate * (1.0 - sig))
    d_up = d_hidden * act
    grad_gate_up = jnp.concatenate([d_gate, d_up], -1).astype(jnp.bfloat16)
    return (grad_gate_up, route_grad, grad_down)


def solution(mesh):
    return jax.shard_map(
        local,
        mesh=mesh,
        in_specs=(
            P(("dp", "expert"), None),
            P(("dp", "expert"), None, None),
            P(("dp", "expert"), None),
            P(("dp", "expert"), None),
            P("expert", "dp", None),
        ),
        out_specs=(
            P(("dp", "expert"), None, None),
            P(("dp", "expert"), None),
            P("expert", "dp", None),
        ),
        check_vma=False,
    )
```

profile of v0, /device:TPU:64, one launch (start us, length us, event | category | flops | bytes accessed | tf_op | source)
XLA Modules:
  0.0 443.5 jit_solution(13268947145808185518)
XLA Ops:
  7.2 0.0 all-gather.2.cloned.1.call-start
  7.2 0.7 all-gather.2.cloned.1.call-update
  7.9 0.8 copy.27
  8.7 0.1 eq.29
  8.8 0.1 eq.25
  8.9 0.7 broadcast_multiply_fusion
  9.6 0.1 copy.26
  9.7 0.1 mul.60
  9.8 9.0 %reduce-window.6 = s32[32,8,128]{2,1,0:T(8,128)S(1)} reduce-window(s32[32,8,128]{2,1,0:T(8,128)S(1)} %fusion.16, s32[]{:T(128)} %constant.16.clone.1), window={size=1x1x128 pad=0_0x0_0x127_0}, to_apply=%region_0.0 | reduce-window | flops 4161536 | bytes 262148 | tf_op jit(solution)/shard_map/reduce-window
  18.8 0.1 slice.22
  18.9 0.1 copy.29
  19.1 0.1 copy.30
  19.1 1.1 concatenate.10
  20.2 0.1 broadcast_add_fusion
  20.4 4.3 scatter_custom_fusion
  24.8 11.0 %gather_fusion = bf16[2048,2048]{1,0:T(8,128)(2,1)} fusion(bf16[129,2048]{1,0:T(8,128)(2,1)S(1)} %concatenate.10, s32[2048]{0:T(1024)S(1)} %get-tuple-element.19), kind=kCustom, calls=%fused_computation | custom fusion | bytes 16785408 | tf_op jit(solution)/shard_map/gather | solution.py:37
  35.8 102.9 %all_to_all.45 = bf16[16,2,64,2048]{3,2,1,0:T(8,128)(2,1)} all-to-all(bf16[16,2,64,2048]{3,2,1,0:T(8,128)(2,1)} %bitcast.53), channel_id=1, replica_groups=mesh['dp'=16,'expert'=16] {'expert'}, dimensions={0} | all-to-all | bytes 16777216 | tf_op jit(solution)/shard_map/all_to_all | solution.py:45
  138.7 8.3 %copy.31 = bf16[1,2,16,64,2048]{4,3,2,1,0:T(8,128)(2,1)} copy(bf16[1,2,16,64,2048]{4,3,1,2,0:T(8,128)(2,1)} %bitcast.54) | data formatting | bytes 16777216 | tf_op jit(solution)/shard_map/all_to_all | solution.py:45
  147.0 0.0 all-gather.2.cloned.1.call-done
  147.0 11.0 %convert_bitcast_fusion.1 = bf16[1,2,1024,768]{3,2,1,0:T(8,128)(2,1)S(1)} fusion(bf16[2,1024,2048]{2,1,0:T(8,128)(2,1)} %bitcast.58, bf16[2,768,2048]{2,1,0:T(8,128)(2,1)} %all-gather.2.cloned.1.call-done), kind=kOutput, calls=%fused_computation.26 | convolution fusion | flops 6444023808 | bytes 17825792 | tf_op jit(solution)/shard_map/jsd,jfd->jsf/dot_general | solution.py:50
  158.0 4.9 %copy.32 = bf16[1,2,1024,768]{3,1,0,2:T(2,128)(2,1)} copy(bf16[1,2,1024,768]{3,2,1,0:T(8,128)(2,1)S(1)} %convert_bitcast_fusion.1) | data formatting | bytes 6291456 | tf_op jit(solution)/shard_map/reshape | solution.py:54
  162.9 0.0 copy-start.2
  162.9 3.9 all-to-all-start.1
  166.8 0.2 all-reduce.5.cloned.1.call-start
  167.0 0.0 copy-done.2
  167.0 0.1 copy.25
  167.1 44.0 %all-to-all-done.1 = bf16[1,2,1024,768]{3,1,0,2:T(2,128)(2,1)S(1)} async-done(((bf16[1,2,1024,768]{3,1,0,2:T(2,128)(2,1)}), bf16[1,2,1024,768]{3,1,0,2:T(2,128)(2,1)S(1)}, u32[]{:S(2)}, u32[]{:S(2)}) %all-to-all-start.1) | async-done | bytes 3145760 | tf_op jit(solution)/shard_map/all_to_all | solution.py:53
  211.1 0.0 copy-start.1
  211.1 1.7 copy-done.1
  212.8 2.5 copy.33
  215.3 5.2 %gather_fusion.1 = bf16[1024,768]{1,0:T(8,128)(2,1)} fusion(bf16[2048,768]{1,0:T(8,128)(2,1)S(1)} %bitcast.52, s32[1024]{0:T(1024)S(1)} %broadcast_clamp_fusion), kind=kCustom, calls=%fused_computation.1 | custom fusion | bytes 3149824 | tf_op jit(solution)/shard_map/gather | solution.py:69
  220.5 5.0 %fusion.12 = (bf16[1024,768]{1,0:T(8,128)(2,1)S(1)}, bf16[128,8,768]{2,1,0:T(8,128)(2,1)S(1)}, bf16[128,8,768]{2,1,0:T(8,128)(2,1)}, bf16[128,8,768]{2,1,0:T(8,128)(2,1)}) fusion(f32[128,8]{1,0:T(8,128)S(1)} %copy.25, bf16[128,8,1536]{2,1,0:T(8,128)(2,1)} %param.6, bf16[1024,768]{1,0:T(8,128)(2,1)} %gather_fusion.1), kind=kLoop, calls=%fused_computation.27 | loop fusion | flops 17301504 | bytes 11014144 | tf_op jit(solution)/shard_map/reshape | solution.py:39
  225.5 0.1 concatenate.12
  225.6 9.4 %gather_fusion.2 = bf16[2048,768]{1,0:T(8,128)(2,1)} fusion(bf16[1025,768]{1,0:T(8,128)(2,1)S(1)} %concatenate.12, s32[2048]{0:T(1024)S(1)} %get-tuple-element.18), kind=kCustom, calls=%fused_computation.2 | custom fusion | bytes 6299648 | tf_op jit(solution)/shard_map/gather | solution.py:38
  235.0 43.2 %all_to_all.46 = bf16[16,2,64,768]{3,2,1,0:T(8,128)(2,1)S(1)} all-to-all(bf16[16,2,64,768]{3,2,1,0:T(8,128)(2,1)} %bitcast.57), channel_id=1, replica_groups=mesh['dp'=16,'expert'=16] {'expert'}, dimensions={0} | all-to-all | bytes 6291456 | tf_op jit(solution)/shard_map/all_to_all | solution.py:46
  278.2 0.2 copy.34
  278.4 15.2 %convert_bitcast_fusion = bf16[768,2,2048]{0,2,1:T(8,128)(2,1)} fusion(bf16[2,1024,2048]{2,1,0:T(8,128)(2,1)} %bitcast.59, bf16[2,1024,768]{2,1,0:T(8,128)(2,1)S(1)} %bitcast.60), kind=kOutput, calls=%fused_computation.4 | convolution fusion | flops 6445596672 | bytes 17825792 | tf_op jit(solution)/shard_map/jsn,jsd->njd/dot_general | solution.py:61
  293.6 16.4 %copy.36 = bf16[768,2,2048]{2,1,0:T(2,128)(2,1)} copy(bf16[768,2,2048]{0,2,1:T(8,128)(2,1)} %convert_bitcast_fusion) | data formatting | bytes 12582912 | tf_op jit(solution)/shard_map/convert_element_type | solution.py:61
  310.0 0.0 copy-start.3
  310.0 0.0 copy-start
  310.0 0.0 all-reduce.5.cloned.1.call-update
  310.0 0.6 copy-done.3
  310.7 0.6 dynamic-slice
  311.9 0.0 copy-done
  311.9 0.5 fusion.7
  312.4 0.7 copy.37
  313.1 3.8 pad_maximum_fusion
  316.8 117.0 %all-reduce.5.cloned.1.call-done = bf16[768,2,2048]{2,1,0:T(2,128)(2,1)} async-done(((bf16[768,2,2048]{2,1,0:T(2,128)(2,1)}), bf16[768,2,2048]{2,1,0:T(2,128)(2,1)}) %all-reduce.5.cloned.1.call-update) | async-done | bytes 6291472
  433.9 1.4 convert_bitcast_fusion.2
  435.3 1.3 copy.38
  (8 shorter events, 0.1 us)
Async XLA Ops:
  7.2 139.8 %all-gather.2.cloned.1.call-start = ((), (), s32[]{:S(2)}) async-start(), calls=%async_computation.3 | async-start | bytes 6684672 | tf_op jit(solution)/shard_map/all_gather | solution.py:43
  162.9 4.1 copy-start.2
  162.9 48.2 %all-to-all-start.1 = ((bf16[1,2,1024,768]{3,1,0,2:T(2,128)(2,1)}), bf16[1,2,1024,768]{3,1,0,2:T(2,128)(2,1)S(1)}, u32[]{:S(2)}, u32[]{:S(2)}) async-start(bf16[1,2,1024,768]{3,1,0,2:T(2,128)(2,1)} %copy.32), calls=%async_computation.1 | async-start | bytes 6291456 | tf_op jit(solution)/shard_map/all_to_all | solution.py:53
  166.8 267.1 %all-reduce.5.cloned.1.call-start = ((), (), s32[]{:S(2)}) async-start(), calls=%async_computation.4 | async-start | bytes 12582912
  211.1 1.7 copy-start.1
  310.0 0.7 copy-start.3
  310.0 1.9 copy-start
Sparse Core Ops, SparseCore 0:
  9.8 47.6 all-gather.1
  310.2 123.6 all-reduce.4
where the time goes:
time: 448 us; the launch traced here: 443 us
  waiting for transfers between devices  162 us (36%)
  blocking collectives  146 us (33%)
  local copies, waits for them, and re-layouts  69.9 us (16%)
  matrix products  26.2 us (6%)
  other arithmetic  20.6 us (5%)
  between operations  14.8 us (3%)
    unnamed x3, waiting for transfers between devices  118 us
    all_to_all x1, blocking collectives, local(): lax.all_to_all(dy_send, 'expert', split_axis=0, concat_axis=2, tiled=True)  103 us
    all_to_all x1, waiting for transfers between devices, local(): lax.all_to_all(grads.reshape(1, local_experts, owners * capacity, hidden_...  44 us
    all_to_all x1, blocking collectives, local(): lax.all_to_all(h_send, 'expert', split_axis=0, concat_axis=2, tiled=True)  43.2 us
    convert_element_type x1, local copies, waits for them, and re-layouts, local(): jnp.einsum('jsn,jsd->njd', h_recv, dy_recv, preferred_element_type=jnp.fl...  16.4 us
    dot_general x1, matrix products, local(): jnp.einsum('jsn,jsd->njd', h_recv, dy_recv, preferred_element_type=jnp.fl...  15.2 us
    gather x1, local copies, waits for them, and re-layouts, local(): jnp.concatenate([cotangent, jnp.zeros((1, width), cotangent.dtype)], 0)  11 us
    dot_general x1, matrix products, local(): jnp.einsum('jsd,jfd->jsf', dy_recv, full_down, preferred_element_type=jnp...  11 us
  transfers between devices with their start and end apart: 3, of which 2 were waited for; matrix products, arithmetic and copies ran while one was open for 9% of the time, Pallas kernels for 0%

commit v1 on v0

v1 whole, which is shorter than its diff:
```python
import jax
import jax.numpy as jnp
from jax import lax
from jax.sharding import PartitionSpec as P


def slot_counts(ids, experts):
    routes = ids.shape[-1]
    onehot = (ids[..., None] == jnp.arange(experts, dtype=jnp.int32)).astype(jnp.bfloat16)
    lower = (jnp.arange(routes)[:, None] > jnp.arange(routes)[None, :]).astype(jnp.bfloat16)
    before = jnp.einsum("rq,...qe->...re", lower, onehot, preferred_element_type=jnp.float32)
    return jnp.sum(before * onehot.astype(jnp.float32), axis=-1).astype(jnp.int32)


def local(cotangent, saved_gate_up, route_ids, route_weights, w_down):
    tokens, top = route_ids.shape
    width = cotangent.shape[1]
    hidden_units = saved_gate_up.shape[2] // 2
    owners = lax.axis_size("expert")
    replicas = lax.axis_size("dp")
    me = lax.axis_index("expert")
    local_experts = w_down.shape[0]
    experts = local_experts * owners
    capacity = min(tokens, 2 * tokens * top // experts)
    routes = tokens * top

    cot_group = lax.all_gather(cotangent, "expert", axis=0, tiled=True)
    ids_group = lax.all_gather(route_ids.reshape(1, routes), "expert", axis=0, tiled=True)
    full_down = lax.all_gather(w_down, "dp", axis=1, tiled=True)

    gate = saved_gate_up[:, :, :hidden_units].astype(jnp.float32)
    up = saved_gate_up[:, :, hidden_units:].astype(jnp.float32)
    sig = jax.nn.sigmoid(gate)
    act = gate * sig
    hidden = (act * up).astype(jnp.bfloat16)
    weights = route_weights[:, :, None]
    scaled = (weights * hidden.astype(jnp.float32)).astype(jnp.bfloat16)

    flat_ids = route_ids.reshape(routes)
    slot = slot_counts(flat_ids, experts)
    position = flat_ids * capacity + slot
    slot_ids = jnp.arange(experts * capacity, dtype=jnp.int32)
    match = position[None, :] == slot_ids[:, None]
    route_of_slot = jnp.sum(jnp.where(match, jnp.arange(routes, dtype=jnp.int32)[None, :], 0), axis=1)
    filled = jnp.any(match, axis=1)
    h_rows = jnp.where(filled[:, None], scaled.reshape(routes, hidden_units)[route_of_slot], jnp.zeros((), jnp.bfloat16))
    h_send = h_rows.reshape(owners, local_experts, capacity, hidden_units)

    slot_all = slot_counts(ids_group, experts)
    mine = me * local_experts + jnp.arange(local_experts, dtype=jnp.int32)
    pos_all = ids_group * capacity + slot_all
    want = (mine[:, None] * capacity + jnp.arange(capacity, dtype=jnp.int32)[None, :]).reshape(-1)
    hit = pos_all[:, None, :] == want[None, :, None]
    token_of = jnp.sum(jnp.where(hit, (jnp.arange(routes, dtype=jnp.int32) // top)[None, None, :], 0), axis=2)
    rows = (jnp.arange(owners, dtype=jnp.int32)[:, None] * tokens + token_of).reshape(owners, local_experts, capacity)
    rows = jnp.transpose(rows, (1, 0, 2)).reshape(local_experts, owners * capacity)
    dy_recv = cot_group[rows]

    h_recv = lax.all_to_all(h_send, "expert", split_axis=0, concat_axis=2, tiled=True)[0]
    grads = jnp.einsum(
        "jsd,jfd->jsf", dy_recv, full_down, preferred_element_type=jnp.float32
    ).astype(jnp.bfloat16)
    back = lax.all_to_all(
        grads.reshape(1, local_experts, owners * capacity, hidden_units),
        "expert",
        split_axis=2,
        concat_axis=0,
        tiled=True,
    )
    parts = []
    for j in range(local_experts):
        part = jnp.einsum(
            "sf,sd->fd", h_recv[j], dy_recv[j], preferred_element_type=jnp.float32
        ).astype(jnp.bfloat16)
        parts.append(lax.psum_scatter(part, "dp", scatter_dimension=0, tiled=True).astype(jnp.float32))
    grad_down = jnp.stack(parts)
    returned_rows = back.reshape(experts * capacity, hidden_units)[position]
    qf = returned_rows.reshape(tokens, top, hidden_units).astype(jnp.float32)
    route_grad = jnp.sum(qf * hidden.astype(jnp.float32), -1)
    d_hidden = weights * qf
    d_gate = d_hidden * up * sig * (1.0 + gate * (1.0 - sig))
    d_up = d_hidden * act
    grad_gate_up = jnp.concatenate([d_gate, d_up], -1).astype(jnp.bfloat16)
    return (grad_gate_up, route_grad, grad_down)


def solution(mesh):
    return jax.shard_map(
        local,
        mesh=mesh,
        in_specs=(
            P(("dp", "expert"), None),
            P(("dp", "expert"), None, None),
            P(("dp", "expert"), None),
            P(("dp", "expert"), None),
            P("expert", "dp", None),
        ),
        out_specs=(
            P(("dp", "expert"), None, None),
            P(("dp", "expert"), None),
            P("expert", "dp", None),
        ),
        check_vma=False,
    )
```

time: 448 us -> 410 us (0.915)
  blocking collectives: 146 us -> 67.7 us
  waiting for transfers between devices: 162 us -> 224 us
  local copies, waits for them, and re-layouts: 69.9 us -> 48.4 us
    unnamed x3 -> x4, waiting for transfers between devices: 118 us -> 1.41 us
    all_to_all x2 -> x1, blocking collectives: 146 us -> 43.6 us  [local(): lax.all_to_all(h_send, 'expert', split_axis=0, concat_axis=2, tiled=True)[0]]
    reduce_scatter x0 -> x2, waiting for transfers between devices: none -> 99.2 us  [local(): lax.psum_scatter(part, 'dp', scatter_dimension=0, tiled=True)]
    all_gather x0 -> x1, waiting for transfers between devices: none -> 52.1 us  [local(): cot_group = lax.all_gather(cotangent, 'expert', axis=0, tiled=True)]
    all_gather x1, waiting for transfers between devices: 0.01 us -> 26.2 us  [local(): full_down = lax.all_gather(w_down, 'dp', axis=1, tiled=True)]
    all_gather x0 -> x1, blocking collectives: none -> 24.1 us  [local(): lax.all_gather(route_ids.reshape(1, routes), 'expert', axis=0, tiled=True)]
    convert_element_type x1 -> x0, local copies, waits for them, and re-layouts: 16.4 us -> none  [local(): jnp.einsum('jsn,jsd->njd', h_recv, dy_recv, preferred_element_type=jnp.fl...]
    gather x2, local copies, waits for them, and re-layouts: 20.4 us -> 30.2 us  [the longest x1 20.8 us: local(): dy_recv = cot_group[rows]]
  transfers between devices with their start and end apart: 3 -> 5, of which waited for: 2 -> 5; matrix products, arithmetic and copies ran while one was open for 9% -> 10% of each run, Pallas kernels for 0% -> 0%
where the time goes in v1:
time: 410 us; the launch traced here: 403 us
  waiting for transfers between devices  224 us (55%)
  blocking collectives  67.7 us (17%)
  local copies, waits for them, and re-layouts  48.4 us (12%)
  matrix products  24.9 us (6%)
  other arithmetic  16.6 us (4%)
  between operations  14 us (3%)
  starting transfers between devices  7.1 us (2%)
    reduce_scatter x2, waiting for transfers between devices, local(): lax.psum_scatter(part, 'dp', scatter_dimension=0, tiled=True)  99.2 us
    all_gather x1, waiting for transfers between devices, local(): cot_group = lax.all_gather(cotangent, 'expert', axis=0, tiled=True)  52.1 us
    all_to_all x1, waiting for transfers between devices, local(): lax.all_to_all(grads.reshape(1, local_experts, owners * capacity, hidden_...  45.5 us
    all_to_all x1, blocking collectives, local(): lax.all_to_all(h_send, 'expert', split_axis=0, concat_axis=2, tiled=True)[0]  43.6 us
    all_gather x1, waiting for transfers between devices, local(): full_down = lax.all_gather(w_down, 'dp', axis=1, tiled=True)  26.2 us
    all_gather x1, blocking collectives, local(): lax.all_gather(route_ids.reshape(1, routes), 'expert', axis=0, tiled=True)  24.1 us
    gather x1, local copies, waits for them, and re-layouts, local(): dy_recv = cot_group[rows]  20.8 us
    dot_general x2, matrix products, local(): jnp.einsum('sf,sd->fd', h_recv[j], dy_recv[j], preferred_element_type=jnp...  11.9 us
  transfers between devices with their start and end apart: 5, of which 5 were waited for; matrix products, arithmetic and copies ran while one was open for 10% of the time, Pallas kernels for 0%

profile of v1, /device:TPU:64, one launch (start us, length us, event | category | flops | bytes accessed | tf_op | source)
XLA Modules:
  0.0 403.0 jit_solution(11496074652841021074)
XLA Ops:
  7.2 0.0 all-gather.4.cloned.1.call-start
  7.2 0.7 all-gather.4.cloned.1.call-update
  7.9 0.0 all-gather.6.cloned.1.call-start
  7.9 0.7 all-gather.6.cloned.1.call-update
  8.7 0.8 copy.30
  9.4 0.1 reshape.205
  9.5 24.1 %all-gather = s32[16,1,1024]{2,1,0:T(1,128)S(1)} all-gather(s32[1,1,1024]{2,1,0:T(1,128)S(1)} %reshape.205), channel_id=1, replica_groups=mesh['dp'=16,'expert'=16] {'expert'}, dimensions={0}, use_global_device_ids=true | all-gather | bytes 69632 | tf_op jit(solution)/shard_map/all_gather | solution.py:28
  33.6 0.1 iota_add_fusion
  33.7 0.1 add.119
  33.8 1.4 fusion.27
  35.2 1.0 select_reduce_fusion.1
  36.2 0.1 reduce_sum.51
  36.3 0.1 add_bitcast_fusion
  36.4 0.1 reshape.171
  36.5 52.1 %all-gather.4.cloned.1.call-done = bf16[2048,2048]{1,0:T(8,128)(2,1)} async-done(((bf16[128,2048]{1,0:T(8,128)(2,1)}), bf16[2048,2048]{1,0:T(8,128)(2,1)}) %all-gather.4.cloned.1.call-update) | async-done | bytes 8388624 | tf_op jit(solution)/shard_map/all_gather | solution.py:27
  88.6 20.8 %gather_fusion = bf16[2048,2048]{1,0:T(8,128)(2,1)} fusion(bf16[2048,2048]{1,0:T(8,128)(2,1)} %all-gather.4.cloned.1.call-done, s32[2048]{0:T(1024)S(1)} %bitcast_clamp_fusion), kind=kCustom, calls=%fused_computation | custom fusion | bytes 16785408 | tf_op jit(solution)/shard_map/gather | solution.py:57
  109.4 26.2 %all-gather.6.cloned.1.call-done = bf16[2,768,2048]{2,1,0:T(8,128)(2,1)} async-done(((bf16[2,48,2048]{2,1,0:T(8,128)(2,1)}), bf16[2,768,2048]{2,1,0:T(8,128)(2,1)}) %all-gather.6.cloned.1.call-update) | async-done | bytes 6291472 | tf_op jit(solution)/shard_map/all_gather | solution.py:29
  135.6 11.0 %convert_bitcast_fusion = bf16[1,2,1024,768]{3,2,1,0:T(8,128)(2,1)S(1)} fusion(bf16[2,1024,2048]{2,1,0:T(8,128)(2,1)} %bitcast.55, bf16[2,768,2048]{2,1,0:T(8,128)(2,1)} %all-gather.6.cloned.1.call-done), kind=kOutput, calls=%fused_computation.38 | convolution fusion | flops 6444023808 | bytes 17825792 | tf_op jit(solution)/shard_map/jsd,jfd->jsf/dot_general | solution.py:60
  146.6 4.9 %copy.32 = bf16[1,2,1024,768]{3,1,0,2:T(2,128)(2,1)} copy(bf16[1,2,1024,768]{3,2,1,0:T(8,128)(2,1)S(1)} %convert_bitcast_fusion) | data formatting | bytes 6291456 | tf_op jit(solution)/shard_map/reshape | solution.py:64
  151.5 0.0 copy-start.3
  151.5 0.0 copy-start.2
  151.5 6.9 %all-to-all-start = ((bf16[1,2,1024,768]{3,1,0,2:T(2,128)(2,1)}), bf16[1,2,1024,768]{3,1,0,2:T(2,128)(2,1)S(1)}, u32[]{:S(2)}, u32[]{:S(2)}) async-start(bf16[1,2,1024,768]{3,1,0,2:T(2,128)(2,1)} %copy.32), calls=%async_computation | async-start | bytes 6291456 | tf_op jit(solution)/shard_map/all_to_all | solution.py:63
  158.4 0.0 reduce-scatter.5.cloned.1.call-start
  158.5 0.1 eq.60
  158.6 0.0 copy-done.3
  158.6 0.1 copy.29
  158.7 0.0 copy-done.2
  158.7 0.1 copy.34
  158.8 0.1 mul.102
  158.9 0.5 fusion.31
  159.5 1.0 fusion
  160.5 0.1 broadcast_in_dim.36
  160.6 0.9 select_reduce_fusion
  161.6 45.5 %all-to-all-done = bf16[1,2,1024,768]{3,1,0,2:T(2,128)(2,1)S(1)} async-done(((bf16[1,2,1024,768]{3,1,0,2:T(2,128)(2,1)}), bf16[1,2,1024,768]{3,1,0,2:T(2,128)(2,1)S(1)}, u32[]{:S(2)}, u32[]{:S(2)}) %all-to-all-start) | async-done | bytes 3145760 | tf_op jit(solution)/shard_map/all_to_all | solution.py:63
  207.0 0.0 copy-start.1
  207.1 1.7 copy-done.1
  208.7 2.5 copy.33
  211.2 5.2 %gather_fusion.1 = bf16[1024,768]{1,0:T(8,128)(2,1)} fusion(bf16[2048,768]{1,0:T(8,128)(2,1)S(1)} %bitcast.51, s32[1024]{0:T(1024)S(1)} %broadcast_clamp_fusion.1), kind=kCustom, calls=%fused_computation.1 | custom fusion | bytes 3149824 | tf_op jit(solution)/shard_map/gather | solution.py:77
  216.5 5.0 %fusion.29 = (bf16[1024,768]{1,0:T(8,128)(2,1)S(1)}, bf16[128,8,768]{2,1,0:T(8,128)(2,1)S(1)}, bf16[128,8,768]{2,1,0:T(8,128)(2,1)}, bf16[128,8,768]{2,1,0:T(8,128)(2,1)}) fusion(f32[128,8]{1,0:T(8,128)S(1)} %copy.29, bf16[128,8,1536]{2,1,0:T(8,128)(2,1)} %param.6, bf16[1024,768]{1,0:T(8,128)(2,1)} %gather_fusion.1), kind=kLoop, calls=%fused_computation.44 | loop fusion | flops 17301504 | bytes 11014144 | tf_op jit(solution)/shard_map/reshape | solution.py:46
  221.4 9.4 %gather_fusion.2 = bf16[2048,768]{1,0:T(8,128)(2,1)} fusion(bf16[1024,768]{1,0:T(8,128)(2,1)S(1)} %get-tuple-element.9, s32[2048]{0:T(1024)S(1)} %broadcast_clamp_fusion), kind=kCustom, calls=%fused_computation.2 | custom fusion | bytes 6299648 | tf_op jit(solution)/shard_map/gather | solution.py:46
  230.8 0.0 slice-start
  230.8 2.3 broadcast_select_fusion
  233.1 0.0 slice-start.1
  233.1 43.6 %all_to_all.30 = bf16[16,2,64,768]{3,2,1,0:T(8,128)(2,1)S(1)} all-to-all(bf16[16,2,64,768]{3,2,1,0:T(8,128)(2,1)S(1)} %broadcast_select_fusion), channel_id=1, replica_groups=mesh['dp'=16,'expert'=16] {'expert'}, dimensions={0} | all-to-all | bytes 6291456 | tf_op jit(solution)/shard_map/all_to_all | solution.py:59
  276.7 0.2 fusion.42
  277.0 0.0 slice-done
  277.0 0.0 slice-done.1
  277.0 4.9 %fusion.13 = bf16[768,2048]{1,0:T(8,128)(2,1)} fusion(bf16[1024,768]{1,0:T(8,128)(2,1)S(1)} %bitcast.59, bf16[2048,2048]{1,0:T(8,128)(2,1)S(1)} %bitcast.57), kind=kOutput, calls=%fused_computation.25 | convolution fusion | flops 3222798336 | bytes 8912896 | tf_op jit(solution)/shard_map/sf,sd->fd/dot_general | solution.py:72
  281.9 0.0 reduce-scatter.5.cloned.1.call-update
  281.9 0.0 reduce-scatter.3.cloned.1.call-start
  282.0 7.0 %fusion.10 = bf16[768,2048]{1,0:T(8,128)(2,1)} fusion(bf16[1024,768]{1,0:T(8,128)(2,1)S(1)} %bitcast.58, bf16[2048,2048]{1,0:T(8,128)(2,1)} %gather_fusion), kind=kOutput, calls=%fused_computation.24 | convolution fusion | flops 3222798336 | bytes 8912896 | tf_op jit(solution)/shard_map/sf,sd->fd/dot_general | solution.py:72
  289.0 0.0 copy-start
  289.0 0.0 reduce-scatter.3.cloned.1.call-update
  289.0 1.4 copy-done
  290.4 0.5 fusion.22
  290.9 0.7 copy.36
  291.6 3.8 pad_maximum_fusion
  295.4 37.5 %reduce-scatter.5.cloned.1.call-done = bf16[48,2048]{1,0:T(8,128)(2,1)} async-done(((bf16[768,2048]{1,0:T(8,128)(2,1)}), bf16[48,2048]{1,0:T(8,128)(2,1)}) %reduce-scatter.5.cloned.1.call-update) | async-done | bytes 196624 | tf_op jit(solution)/shard_map/reduce_scatter | solution.py:75
  332.8 61.7 %reduce-scatter.3.cloned.1.call-done = bf16[48,2048]{1,0:T(8,128)(2,1)} async-done(((bf16[768,2048]{1,0:T(8,128)(2,1)}), bf16[48,2048]{1,0:T(8,128)(2,1)}) %reduce-scatter.3.cloned.1.call-update) | async-done | bytes 196624 | tf_op jit(solution)/shard_map/reduce_scatter | solution.py:75
  394.5 2.0 maximum_convert_fusion
  (16 shorter events, 0.1 us)
Async XLA Ops:
  7.2 81.4 %all-gather.4.cloned.1.call-start = ((), (), s32[]{:S(2)}) async-start(), calls=%async_computation.4 | async-start | bytes 8912896 | tf_op jit(solution)/shard_map/all_gather | solution.py:27
  7.9 127.7 %all-gather.6.cloned.1.call-start = ((), (), s32[]{:S(2)}) async-start(), calls=%async_computation.5 | async-start | bytes 6684672 | tf_op jit(solution)/shard_map/all_gather | solution.py:29
  151.5 7.1 %copy-start.3 = (f32[128,8]{0,1:T(8,128)S(1)}, f32[128,8]{0,1:T(8,128)}, u32[]{:S(2)}) copy-start(f32[128,8]{0,1:T(8,128)} %param.8) | copy-start | bytes 12292
  151.5 7.2 %copy-start.2 = (s32[128,8]{0,1:T(8,128)S(1)}, s32[128,8]{0,1:T(8,128)}, u32[]{:S(2)}) copy-start(s32[128,8]{0,1:T(8,128)} %param.7) | copy-start | bytes 12292
  151.5 55.6 %all-to-all-start = ((bf16[1,2,1024,768]{3,1,0,2:T(2,128)(2,1)}), bf16[1,2,1024,768]{3,1,0,2:T(2,128)(2,1)S(1)}, u32[]{:S(2)}, u32[]{:S(2)}) async-start(bf16[1,2,1024,768]{3,1,0,2:T(2,128)(2,1)} %copy.32), calls=%async_computation | async-start | bytes 6291456 | tf_op jit(solution)/shard_map/all_to_all | solution.py:63
  158.4 174.4 %reduce-scatter.5.cloned.1.call-start = ((), (), s32[]{:S(2)}) async-start(), calls=%async_computation.7 | async-start | bytes 3342336 | tf_op jit(solution)/shard_map/reduce_scatter | solution.py:75
  207.0 1.7 copy-start.1
  230.8 46.2 %slice-start = ((s8[8388608]{0:T(1024)(128)(4,1)}), s8[4194304]{0:T(1024)(128)(4,1)S(1)}, s32[]{:S(2)}) async-start(s8[8388608]{0:T(1024)(128)(4,1)} %bitcast.56), calls=%async_computation.8 | async-start | bytes 8388608
  233.1 43.9 %slice-start.1 = ((s8[8388608]{0:T(1024)(128)(4,1)}), s8[4194304]{0:T(1024)(128)(4,1)S(1)}, s32[]{:S(2)}) async-start(s8[8388608]{0:T(1024)(128)(4,1)} %bitcast.56), calls=%async_computation.9 | async-start | bytes 8388608
  281.9 112.6 %reduce-scatter.3.cloned.1.call-start = ((), (), s32[]{:S(2)}) async-start(), calls=%async_computation.6 | async-start | bytes 3342336 | tf_op jit(solution)/shard_map/reduce_scatter | solution.py:75
  289.0 1.4 copy-start
Sparse Core Ops, SparseCore 0:
  10.4 78.0 all-gather.3
  90.4 45.1 all-gather.5
  282.0 50.7 reduce-scatter.4
  335.2 59.2 reduce-scatter.2

commit v2 on v1

--- a/solution.py
+++ b/solution.py
@@ -54,9 +54,10 @@
     token_of = jnp.sum(jnp.where(hit, (jnp.arange(routes, dtype=jnp.int32) // top)[None, None, :], 0), axis=2)
     rows = (jnp.arange(owners, dtype=jnp.int32)[:, None] * tokens + token_of).reshape(owners, local_experts, capacity)
     rows = jnp.transpose(rows, (1, 0, 2)).reshape(local_experts, owners * capacity)
+    h_recv = lax.all_to_all(h_send, "expert", split_axis=0, concat_axis=2, tiled=True)[0]
+    h_recv, cot_group = lax.optimization_barrier((h_recv, cot_group))
     dy_recv = cot_group[rows]
 
-    h_recv = lax.all_to_all(h_send, "expert", split_axis=0, concat_axis=2, tiled=True)[0]
     grads = jnp.einsum(
         "jsd,jfd->jsf", dy_recv, full_down, preferred_element_type=jnp.float32
     ).astype(jnp.bfloat16)
@@ -72,8 +73,9 @@
         part = jnp.einsum(
             "sf,sd->fd", h_recv[j], dy_recv[j], preferred_element_type=jnp.float32
         ).astype(jnp.bfloat16)
-        parts.append(lax.psum_scatter(part, "dp", scatter_dimension=0, tiled=True).astype(jnp.float32))
-    grad_down = jnp.stack(parts)
+        parts.append(part.reshape(replicas, hidden_units // replicas, width))
+    summed = lax.psum_scatter(jnp.stack(parts, axis=1), "dp", scatter_dimension=0, tiled=True)
+    grad_down = summed[0].astype(jnp.float32)
     returned_rows = back.reshape(experts * capacity, hidden_units)[position]
     qf = returned_rows.reshape(tokens, top, hidden_units).astype(jnp.float32)
     route_grad = jnp.sum(qf * hidden.astype(jnp.float32), -1)

time: 410 us -> 259 us (0.63); the launches traced: 403 us -> 257 us
  waiting for transfers between devices: 224 us -> 63.9 us
  starting transfers between devices: 7.1 us -> 14.1 us
  other arithmetic: 16.6 us -> 21.3 us
    reduce_scatter x2 -> x1, waiting for transfers between devices: 99.2 us -> 0.01 us  [local(): lax.psum_scatter(jnp.stack(parts, axis=1), 'dp', scatter_dimension=0, til...]
    all_gather x1, waiting for transfers between devices: 52.1 us -> 2.47 us  [local(): cot_group = lax.all_gather(cotangent, 'expert', axis=0, tiled=True)]
    all_gather x1, blocking collectives: 24.1 us -> 71.6 us  [local(): lax.all_gather(route_ids.reshape(1, routes), 'expert', axis=0, tiled=True)]
    all_to_all x1 -> x0, blocking collectives: 43.6 us -> none  [local(): lax.all_to_all(h_send, 'expert', split_axis=0, concat_axis=2, tiled=True)[0]]
    all_gather x1, waiting for transfers between devices: 26.2 us -> 11.7 us  [local(): full_down = lax.all_gather(w_down, 'dp', axis=1, tiled=True)]
    all_to_all x0 -> x1, starting transfers between devices: none -> 7.04 us  [local(): lax.all_to_all(h_send, 'expert', split_axis=0, concat_axis=2, tiled=True)[0]]
    another operation x1 -> x2, other arithmetic: 1.95 us -> 7.53 us  [local(): grad_down = jnp.stack(parts)]
  transfers between devices with their start and end apart: 5 -> 5, of which waited for: 5 -> 3; matrix products, arithmetic and copies ran while one was open for 10% -> 35% of each run, Pallas kernels for 0% -> 0%
where the time goes in v2:
time: 259 us; the launch traced here: 257 us
  blocking collectives  71.6 us (28%)
  waiting for transfers between devices  63.9 us (25%)
  local copies, waits for them, and re-layouts  49.7 us (19%)
  matrix products  22.8 us (9%)
  other arithmetic  21.3 us (8%)
  starting transfers between devices  14.1 us (5%)
  between operations  14 us (5%)
    all_gather x1, blocking collectives, local(): lax.all_gather(route_ids.reshape(1, routes), 'expert', axis=0, tiled=True)  71.6 us
    all_to_all x1, waiting for transfers between devices, local(): lax.all_to_all(grads.reshape(1, local_experts, owners * capacity, hidden_...  48.3 us
    gather x1, local copies, waits for them, and re-layouts, local(): dy_recv = cot_group[rows]  21.1 us
    all_gather x1, waiting for transfers between devices, local(): full_down = lax.all_gather(w_down, 'dp', axis=1, tiled=True)  11.7 us
    dot_general x1, matrix products, local(): jnp.einsum('jsd,jfd->jsf', dy_recv, full_down, preferred_element_type=jnp...  11 us
    dot_general x2, matrix products, local(): jnp.einsum('sf,sd->fd', h_recv[j], dy_recv[j], preferred_element_type=jnp...  9.81 us
    gather x1, local copies, waits for them, and re-layouts, local(): scaled.reshape(routes, hidden_units)[route_of_slot]  9.4 us
    all_to_all x1, starting transfers between devices, local(): lax.all_to_all(h_send, 'expert', split_axis=0, concat_axis=2, tiled=True)[0]  7.04 us
  transfers between devices with their start and end apart: 5, of which 3 were waited for; matrix products, arithmetic and copies ran while one was open for 35% of the time, Pallas kernels for 0%

profile of v2, /device:TPU:64, one launch (start us, length us, event | category | flops | bytes accessed | tf_op | source)
XLA Modules:
  0.0 257.4 jit_solution(17816790262172470901)
XLA Ops:
  7.2 0.0 all-gather.4.cloned.1.call-start
  7.2 0.7 all-gather.4.cloned.1.call-update
  7.9 0.0 all-gather.6.cloned.1.call-start
  7.9 0.7 all-gather.6.cloned.1.call-update
  8.6 0.8 copy.43
  9.4 0.1 reshape.170
  9.5 0.8 copy.42
  10.3 0.5 fusion.35
  10.9 1.0 fusion
  11.9 0.1 broadcast_in_dim.34
  12.0 0.9 select_reduce_fusion.1
  12.9 3.4 %fusion.29 = (bf16[1024,768]{1,0:T(8,128)(2,1)S(1)}, bf16[128,8,768]{2,1,0:T(8,128)(2,1)}) fusion(f32[128,8]{1,0:T(8,128)S(1)} %copy.42, bf16[128,8,1536]{2,1,0:T(8,128)(2,1)} %param.6), kind=kLoop, calls=%fused_computation.45 | loop fusion | flops 8650752 | bytes 6295552 | tf_op jit(solution)/shard_map/reshape | solution.py:46
  16.3 9.4 %gather_fusion = bf16[2048,768]{1,0:T(8,128)(2,1)} fusion(bf16[1024,768]{1,0:T(8,128)(2,1)S(1)} %get-tuple-element.13, s32[2048]{0:T(1024)S(1)} %broadcast_clamp_fusion), kind=kCustom, calls=%fused_computation | custom fusion | bytes 6299648 | tf_op jit(solution)/shard_map/gather | solution.py:46
  25.7 3.4 %broadcast_select_fusion = bf16[16,2,64,768]{3,2,1,0:T(8,128)(2,1)} fusion(bf16[16,2,64,768]{3,2,1,0:T(8,128)(2,1)} %bitcast.64, pred[16,2,64]{2,1,0:T(4,128)(4,1)S(1)} %broadcast_in_dim.34), kind=kLoop, calls=%fused_computation.40 | loop fusion | flops 1572864 | bytes 6293504 | tf_op jit(solution)/shard_map/jit(_where)/select_n | solution.py:46
  29.1 7.0 %all-to-all-start = ((bf16[16,2,64,768]{3,2,1,0:T(8,128)(2,1)}), bf16[16,2,64,768]{3,2,1,0:T(8,128)(2,1)S(1)}, u32[]{:S(2)}, u32[]{:S(2)}) async-start(bf16[16,2,64,768]{3,2,1,0:T(8,128)(2,1)} %broadcast_select_fusion), calls=%async_computation | async-start | bytes 6291456 | tf_op jit(solution)/shard_map/all_to_all | solution.py:57
  36.2 0.0 reduce-scatter.2.cloned.1.call-start
  36.2 0.1 reshape.207
  36.3 71.6 %all-gather = s32[16,1,1024]{2,1,0:T(1,128)S(1)} all-gather(s32[1,1,1024]{2,1,0:T(1,128)S(1)} %reshape.207), channel_id=1, replica_groups=mesh['dp'=16,'expert'=16] {'expert'}, dimensions={0}, use_global_device_ids=true | all-gather | bytes 69632 | tf_op jit(solution)/shard_map/all_gather | solution.py:28
  108.0 0.1 iota_add_fusion
  108.1 0.1 add.121
  108.2 1.4 fusion.27
  109.6 1.0 select_reduce_fusion
  110.6 0.1 reduce_sum.54
  110.7 0.1 add_bitcast_fusion
  110.8 0.1 reshape.173
  110.9 0.0 all-to-all-done
  110.9 1.9 copy.44
  112.8 2.5 all-gather.4.cloned.1.call-done
  115.2 0.0 copy-start.2
  115.2 21.1 %gather_fusion.1 = bf16[2048,2048]{1,0:T(8,128)(2,1)} fusion(bf16[2048,2048]{1,0:T(8,128)(2,1)} %all-gather.4.cloned.1.call-done, s32[2048]{0:T(1024)S(1)} %bitcast_clamp_fusion), kind=kCustom, calls=%fused_computation.1 | custom fusion | bytes 16785408 | tf_op jit(solution)/shard_map/gather | solution.py:59
  136.4 0.0 copy-done.2
  136.4 0.0 copy-start.1
  136.4 6.1 %fusion.10 = bf16[768,2048]{1,0:T(8,128)(2,1)S(1)} fusion(bf16[2048,2048]{1,0:T(8,128)(2,1)} %gather_fusion.1, bf16[2,1024,768]{2,1,0:T(8,128)(2,1)S(1)} %bitcast.66), kind=kOutput, calls=%fused_computation.25 | convolution fusion | flops 3222798336 | bytes 8912896 | tf_op jit(solution)/shard_map/sf,sd->fd/dot_general | solution.py:73
  142.5 0.0 copy-done.1
  142.5 3.7 %fusion.13 = bf16[768,2048]{1,0:T(8,128)(2,1)S(1)} fusion(bf16[2048,2048]{1,0:T(8,128)(2,1)S(1)} %copy-done.1, bf16[2,1024,768]{2,1,0:T(8,128)(2,1)S(1)} %bitcast.67), kind=kOutput, calls=%fused_computation.26 | convolution fusion | flops 3222798336 | bytes 8912896 | tf_op jit(solution)/shard_map/sf,sd->fd/dot_general | solution.py:73
  146.2 3.3 %pad_maximum_fusion = bf16[16,2,48,2048]{3,2,1,0:T(8,128)(2,1)} fusion(bf16[16,1,48,2048]{3,2,1,0:T(8,128)(2,1)S(1)} %bitcast.69, bf16[16,1,48,2048]{3,2,1,0:T(8,128)(2,1)S(1)} %bitcast.68), kind=kLoop, calls=%fused_computation.7 | loop fusion | flops 3145728 | bytes 12582912 | tf_op jit(solution)/shard_map/stack | solution.py:77
  149.5 0.0 reduce-scatter.2.cloned.1.call-update
  149.5 11.7 %all-gather.6.cloned.1.call-done = bf16[2,768,2048]{2,1,0:T(8,128)(2,1)} async-done(((bf16[2,48,2048]{2,1,0:T(8,128)(2,1)}), bf16[2,768,2048]{2,1,0:T(8,128)(2,1)}) %all-gather.6.cloned.1.call-update) | async-done | bytes 6291472 | tf_op jit(solution)/shard_map/all_gather | solution.py:29
  161.2 11.0 %convert_bitcast_fusion = bf16[1,2,1024,768]{3,2,1,0:T(8,128)(2,1)S(1)} fusion(bf16[2,1024,2048]{2,1,0:T(8,128)(2,1)} %bitcast.65, bf16[2,768,2048]{2,1,0:T(8,128)(2,1)} %all-gather.6.cloned.1.call-done), kind=kOutput, calls=%fused_computation.39 | convolution fusion | flops 6444023808 | bytes 17825792 | tf_op jit(solution)/shard_map/jsd,jfd->jsf/dot_general | solution.py:61
  172.2 4.9 %copy.47 = bf16[1,2,1024,768]{3,1,0,2:T(2,128)(2,1)} copy(bf16[1,2,1024,768]{3,2,1,0:T(8,128)(2,1)S(1)} %convert_bitcast_fusion) | data formatting | bytes 6291456 | tf_op jit(solution)/shard_map/reshape | solution.py:65
  177.1 0.0 copy-start.3
  177.1 6.9 %all-to-all-start.1 = ((bf16[1,2,1024,768]{3,1,0,2:T(2,128)(2,1)}), bf16[1,2,1024,768]{3,1,0,2:T(2,128)(2,1)S(1)}, u32[]{:S(2)}, u32[]{:S(2)}) async-start(bf16[1,2,1024,768]{3,1,0,2:T(2,128)(2,1)} %copy.47), calls=%async_computation.1 | async-start | bytes 6291456 | tf_op jit(solution)/shard_map/all_to_all | solution.py:64
  184.1 0.0 copy-done.3
  184.1 0.1 copy.49
  184.2 0.1 mul.108
  184.3 48.3 %all-to-all-done.1 = bf16[1,2,1024,768]{3,1,0,2:T(2,128)(2,1)S(1)} async-done(((bf16[1,2,1024,768]{3,1,0,2:T(2,128)(2,1)}), bf16[1,2,1024,768]{3,1,0,2:T(2,128)(2,1)S(1)}, u32[]{:S(2)}, u32[]{:S(2)}) %all-to-all-start.1) | async-done | bytes 3145760 | tf_op jit(solution)/shard_map/all_to_all | solution.py:64
  232.7 0.0 copy-start
  232.7 1.7 copy-done
  234.3 2.5 copy.48
  236.9 5.2 %gather_fusion.2 = bf16[1024,768]{1,0:T(8,128)(2,1)} fusion(bf16[2048,768]{1,0:T(8,128)(2,1)S(1)} %bitcast.62, s32[1024]{0:T(1024)S(1)} %broadcast_clamp_fusion.1), kind=kCustom, calls=%fused_computation.2 | custom fusion | bytes 3149824 | tf_op jit(solution)/shard_map/gather | solution.py:79
  242.1 4.2 %fusion.20 = (bf16[128,8,768]{2,1,0:T(8,128)(2,1)S(1)}, bf16[128,8,768]{2,1,0:T(8,128)(2,1)S(1)}, f32[128,8]{1,0:T(8,128)S(1)}) fusion(bf16[1024,768]{1,0:T(8,128)(2,1)} %gather_fusion.2, f32[128,8]{1,0:T(8,128)S(1)} %copy.42, bf16[128,8,1536]{2,1,0:T(8,128)(2,1)} %param.6, bf16[128,8,768]{2,1,0:T(8,128)(2,1)} %get-tuple-element.14), kind=kLoop, calls=%fused_computation.31 | loop fusion | flops 15727616 | bytes 9445376 | tf_op jit(solution)/shard_map/convert.2
  246.3 0.7 copy.52
  247.0 1.9 pad_maximum_fusion.1
  248.9 0.0 reduce-scatter.2.cloned.1.call-done
  248.9 1.9 bitcast_convert_fusion
  (15 shorter events, 0.1 us)
Async XLA Ops:
  7.2 108.1 %all-gather.4.cloned.1.call-start = ((), (), s32[]{:S(2)}) async-start(), calls=%async_computation.3 | async-start | bytes 8912896 | tf_op jit(solution)/shard_map/all_gather | solution.py:27
  7.9 153.3 %all-gather.6.cloned.1.call-start = ((), (), s32[]{:S(2)}) async-start(), calls=%async_computation.4 | async-start | bytes 6684672 | tf_op jit(solution)/shard_map/all_gather | solution.py:29
  29.1 81.7 %all-to-all-start = ((bf16[16,2,64,768]{3,2,1,0:T(8,128)(2,1)}), bf16[16,2,64,768]{3,2,1,0:T(8,128)(2,1)S(1)}, u32[]{:S(2)}, u32[]{:S(2)}) async-start(bf16[16,2,64,768]{3,2,1,0:T(8,128)(2,1)} %broadcast_select_fusion), calls=%async_computation | async-start | bytes 6291456 | tf_op jit(solution)/shard_map/all_to_all | solution.py:57
  36.2 212.7 %reduce-scatter.2.cloned.1.call-start = ((), (), s32[]{:S(2)}) async-start(), calls=%async_computation.5 | async-start | bytes 6684672 | tf_op jit(solution)/shard_map/reduce_scatter | solution.py:77
  115.2 21.1 %copy-start.2 = (bf16[16,2,64,768]{3,2,0,1:T(8,128)(2,1)S(1)}, bf16[16,2,64,768]{3,2,0,1:T(8,128)(2,1)}, u32[]{:S(2)}) copy-start(bf16[16,2,64,768]{3,2,0,1:T(8,128)(2,1)} %copy.44) | copy-start | bytes 9437188
  136.4 6.1 %copy-start.1 = (bf16[2048,2048]{1,0:T(8,128)(2,1)S(1)}, bf16[2048,2048]{1,0:T(8,128)(2,1)}, u32[]{:S(2)}) copy-start(bf16[2048,2048]{1,0:T(8,128)(2,1)} %gather_fusion.1) | copy-start | bytes 25165828
  177.1 7.0 %copy-start.3 = (s32[128,8]{0,1:T(8,128)S(1)}, s32[128,8]{0,1:T(8,128)}, u32[]{:S(2)}) copy-start(s32[128,8]{0,1:T(8,128)} %param.7) | copy-start | bytes 12292
  177.1 55.6 %all-to-all-start.1 = ((bf16[1,2,1024,768]{3,1,0,2:T(2,128)(2,1)}), bf16[1,2,1024,768]{3,1,0,2:T(2,128)(2,1)S(1)}, u32[]{:S(2)}, u32[]{:S(2)}) async-start(bf16[1,2,1024,768]{3,1,0,2:T(2,128)(2,1)} %copy.47), calls=%async_computation.1 | async-start | bytes 6291456 | tf_op jit(solution)/shard_map/all_to_all | solution.py:64
  232.7 1.7 copy-start
Sparse Core Ops, SparseCore 0:
  10.4 104.7 all-gather.3
  117.1 44.0 all-gather.5
  163.8 60.7 reduce-scatter.1

commit v3 on v2

--- a/solution.py
+++ b/solution.py
@@ -1,7 +1,78 @@
 import jax
 import jax.numpy as jnp
 from jax import lax
+from jax.experimental import pallas as pl
+from jax.experimental.pallas import tpu as pltpu
 from jax.sharding import PartitionSpec as P
+
+MESH = pl.DeviceIdType.MESH
+
+
+def ring_dp(pos, replicas):
+    pos = lax.rem(pos + 2 * replicas, replicas)
+    z = pos // 2
+    core = lax.rem(pos, 2)
+    core = jnp.where(lax.rem(z, 2) == 0, core, 1 - core)
+    return z * 2 + core
+
+
+def ring_pos(dp):
+    z = dp // 2
+    core = lax.rem(dp, 2)
+    return z * 2 + jnp.where(lax.rem(z, 2) == 0, core, 1 - core)
+
+
+def gather_kernel(replicas, w_ref, o_ref, own_sem, send_sem, recv_sem):
+    me = lax.axis_index("dp")
+    col = lax.axis_index("expert")
+    pos = ring_pos(me)
+    right = ring_dp(pos + 1, replicas)
+    left = ring_dp(pos - 1, replicas)
+
+    barrier = pltpu.get_barrier_semaphore()
+    for neighbour in (left, right):
+        pl.semaphore_signal(barrier, inc=1, device_id=(neighbour, col), device_id_type=MESH)
+    pl.semaphore_wait(barrier, 2)
+
+    own = pltpu.make_async_copy(w_ref, o_ref.at[me], own_sem)
+    own.start()
+    for step in range(replicas - 1):
+        copies = []
+        for j, (target, origin) in enumerate(((right, pos - step), (left, pos + step))):
+            block = ring_dp(origin, replicas)
+            src = w_ref.at[j] if step == 0 else o_ref.at[block, j]
+            copy = pltpu.make_async_remote_copy(
+                src_ref=src,
+                dst_ref=o_ref.at[block, j],
+                send_sem=send_sem.at[j, step],
+                recv_sem=recv_sem.at[j, step],
+                device_id=(target, col),
+                device_id_type=MESH,
+            )
+            copy.start()
+            copies.append(copy)
+        for copy in copies:
+            copy.wait()
+    own.wait()
+
+
+def gather_down(w_down, replicas):
+    local_experts, rows, width = w_down.shape
+    return pl.pallas_call(
+        lambda *refs: gather_kernel(replicas, *refs),
+        out_shape=jax.ShapeDtypeStruct((replicas, local_experts, rows, width), w_down.dtype),
+        in_specs=[pl.BlockSpec(memory_space=pl.ANY)],
+        out_specs=pl.BlockSpec(memory_space=pl.ANY),
+        scratch_shapes=[
+            pltpu.SemaphoreType.DMA(()),
+            pltpu.SemaphoreType.DMA((2, replicas - 1)),
+            pltpu.SemaphoreType.DMA((2, replicas - 1)),
+        ],
+        compiler_params=pltpu.CompilerParams(collective_id=0, has_side_effects=True),
+        cost_estimate=pl.CostEstimate(
+            flops=0, bytes_accessed=2 * replicas * w_down.size * 2, transcendentals=0
+        ),
+    )(w_down)
 
 
 def slot_counts(ids, experts):
@@ -26,7 +97,7 @@
 
     cot_group = lax.all_gather(cotangent, "expert", axis=0, tiled=True)
     ids_group = lax.all_gather(route_ids.reshape(1, routes), "expert", axis=0, tiled=True)
-    full_down = lax.all_gather(w_down, "dp", axis=1, tiled=True)
+    full_down = gather_down(w_down, replicas)
 
     gate = saved_gate_up[:, :, :hidden_units].astype(jnp.float32)
     up = saved_gate_up[:, :, hidden_units:].astype(jnp.float32)
@@ -54,13 +125,14 @@
     token_of = jnp.sum(jnp.where(hit, (jnp.arange(routes, dtype=jnp.int32) // top)[None, None, :], 0), axis=2)
     rows = (jnp.arange(owners, dtype=jnp.int32)[:, None] * tokens + token_of).reshape(owners, local_experts, capacity)
     rows = jnp.transpose(rows, (1, 0, 2)).reshape(local_experts, owners * capacity)
+    full_down, h_send = lax.optimization_barrier((full_down, h_send))
     h_recv = lax.all_to_all(h_send, "expert", split_axis=0, concat_axis=2, tiled=True)[0]
     h_recv, cot_group = lax.optimization_barrier((h_recv, cot_group))
     dy_recv = cot_group[rows]
 
     grads = jnp.einsum(
-        "jsd,jfd->jsf", dy_recv, full_down, preferred_element_type=jnp.float32
-    ).astype(jnp.bfloat16)
+        "jsd,qjid->jsqi", dy_recv, full_down, preferred_element_type=jnp.float32
+    ).astype(jnp.bfloat16).reshape(local_experts, owners * capacity, hidden_units)
     back = lax.all_to_all(
         grads.reshape(1, local_experts, owners * capacity, hidden_units),
         "expert",

time: 259 us -> 299 us (1.15)
  Pallas kernels: 0 us -> 79.1 us
  waiting for transfers between devices: 63.9 us -> 40.7 us
  blocking collectives: 71.6 us -> 60.7 us
    pallas_call x0 -> x1, Pallas kernels: none -> 79.1 us  [gather_down(): pl.pallas_call(lambda *refs: gather_kernel(replicas, *refs), out_shape=ja...]
    all_gather x1 -> x0, waiting for transfers between devices: 11.7 us -> none  [local(): full_down = lax.all_gather(w_down, 'dp', axis=1, tiled=True)]
    all_gather x1, blocking collectives: 71.6 us -> 60.7 us  [local(): lax.all_gather(route_ids.reshape(1, routes), 'expert', axis=0, tiled=True)]
    all_to_all x1, waiting for transfers between devices: 48.3 us -> 40 us  [local(): lax.all_to_all(grads.reshape(1, local_experts, owners * capacity, hidden_...]
    another operation x0 -> x1, local copies, waits for them, and re-layouts: none -> 5.64 us  [local(): grads.reshape(1, local_experts, owners * capacity, hidden_units)]
    reshape x1 -> x0, local copies, waits for them, and re-layouts: 4.9 us -> none  [local(): grads.reshape(1, local_experts, owners * capacity, hidden_units)]
  transfers between devices with their start and end apart: 5 -> 4, of which waited for: 3 -> 1; matrix products, arithmetic and copies ran while one was open for 35% -> 18% of each run, Pallas kernels for 0% -> 27%
where the time goes in v3:
time: 299 us; the launch traced here: 297 us
  Pallas kernels  79.1 us (26%)
  blocking collectives  60.7 us (20%)
  local copies, waits for them, and re-layouts  46.8 us (16%)
  waiting for transfers between devices  40.7 us (14%)
  matrix products  22.9 us (8%)
  other arithmetic  21.2 us (7%)
  between operations  14.3 us (5%)
  starting transfers between devices  11.5 us (4%)
    pallas_call x1, Pallas kernels, gather_down(): pl.pallas_call(lambda *refs: gather_kernel(replicas, *refs), out_shape=ja...  79.1 us
    all_gather x1, blocking collectives, local(): lax.all_gather(route_ids.reshape(1, routes), 'expert', axis=0, tiled=True)  60.7 us
    all_to_all x1, waiting for transfers between devices, local(): lax.all_to_all(grads.reshape(1, local_experts, owners * capacity, hidden_...  40 us
    gather x1, local copies, waits for them, and re-layouts, local(): dy_recv = cot_group[rows]  21.1 us
    dot_general x1, matrix products, local(): jnp.einsum('jsd,qjid->jsqi', dy_recv, full_down, preferred_element_type=j...  11.2 us
    dot_general x2, matrix products, local(): jnp.einsum('sf,sd->fd', h_recv[j], dy_recv[j], preferred_element_type=jnp...  9.73 us
    gather x1, local copies, waits for them, and re-layouts, local(): scaled.reshape(routes, hidden_units)[route_of_slot]  9.4 us
    all_to_all x1, starting transfers between devices, local(): lax.all_to_all(h_send, 'expert', split_axis=0, concat_axis=2, tiled=True)[0]  7.03 us
  transfers between devices with their start and end apart: 4, of which 1 were waited for; matrix products, arithmetic and copies ran while one was open for 18% of the time, Pallas kernels for 27%

profile of v3, /device:TPU:64, one launch (start us, length us, event | category | flops | bytes accessed | tf_op | source)
XLA Modules:
  0.0 297.3 jit_solution(3524422067617023224)
XLA Ops:
  7.2 0.0 all-gather.3.cloned.1.call-start
  7.2 0.7 all-gather.3.cloned.1.call-update
  7.9 0.8 copy.49
  8.7 0.8 copy.50
  9.5 0.1 reshape.167
  9.6 0.5 fusion.40
  10.1 1.0 fusion
  11.1 0.1 broadcast_in_dim.34
  11.2 79.1 %shard_map.76 = bf16[16,2,48,2048]{3,2,1,0:T(8,128)(2,1)} custom-call(bf16[2,48,2048]{2,1,0:T(8,128)(2,1)} %refs_0_.1), custom_call_target="tpu_custom_call" | custom-call | bytes 12582912 | tf_op jit(solution)/shard_map/pallas_call | solution.py:61
  90.4 0.9 select_reduce_fusion.1
  91.3 3.4 %fusion.34 = (bf16[1024,768]{1,0:T(8,128)(2,1)S(1)}, bf16[128,8,768]{2,1,0:T(8,128)(2,1)}) fusion(f32[128,8]{1,0:T(8,128)S(1)} %copy.49, bf16[128,8,1536]{2,1,0:T(8,128)(2,1)} %param.6), kind=kLoop, calls=%fused_computation.47 | loop fusion | flops 8650752 | bytes 6295552 | tf_op jit(solution)/shard_map/reshape | solution.py:117
  94.7 9.4 %gather_fusion = bf16[2048,768]{1,0:T(8,128)(2,1)} fusion(bf16[1024,768]{1,0:T(8,128)(2,1)S(1)} %get-tuple-element.17, s32[2048]{0:T(1024)S(1)} %broadcast_clamp_fusion), kind=kCustom, calls=%fused_computation | custom fusion | bytes 6299648 | tf_op jit(solution)/shard_map/gather | solution.py:117
  104.1 3.3 %broadcast_select_fusion = bf16[16,2,64,768]{3,2,1,0:T(8,128)(2,1)} fusion(bf16[16,2,64,768]{3,2,1,0:T(8,128)(2,1)} %bitcast.66, pred[16,2,64]{2,1,0:T(4,128)(4,1)S(1)} %broadcast_in_dim.34), kind=kLoop, calls=%fused_computation.41 | loop fusion | flops 1572864 | bytes 6293504 | tf_op jit(solution)/shard_map/jit(_where)/select_n | solution.py:117
  107.4 7.0 %all-to-all-start = ((bf16[16,2,64,768]{3,2,1,0:T(8,128)(2,1)}), bf16[16,2,64,768]{3,2,1,0:T(8,128)(2,1)S(1)}, u32[]{:S(2)}, u32[]{:S(2)}) async-start(bf16[16,2,64,768]{3,2,1,0:T(8,128)(2,1)} %broadcast_select_fusion), calls=%async_computation | async-start | bytes 6291456 | tf_op jit(solution)/shard_map/all_to_all | solution.py:129
  114.4 0.0 reduce-scatter.2.cloned.1.call-start
  114.5 0.1 reshape.203
  114.6 0.1 iota_add_fusion
  114.6 0.1 add.121
  114.7 60.7 %all-gather = s32[16,1,1024]{2,1,0:T(1,128)S(1)} all-gather(s32[1,1,1024]{2,1,0:T(1,128)S(1)} %reshape.203), channel_id=1, replica_groups=mesh['dp'=16,'expert'=16] {'expert'}, dimensions={0}, use_global_device_ids=true | all-gather | bytes 69632 | tf_op jit(solution)/shard_map/all_gather | solution.py:99
  175.5 1.4 fusion.32
  176.9 1.0 select_reduce_fusion
  177.9 0.1 reduce_sum.54
  178.0 0.1 add_bitcast_fusion
  178.1 0.1 reshape.170
  178.2 0.0 all-to-all-done
  178.2 1.9 copy.51
  180.1 0.0 all-gather.3.cloned.1.call-done
  180.1 0.0 copy-start.1
  180.1 21.1 %gather_fusion.1 = bf16[2048,2048]{1,0:T(8,128)(2,1)} fusion(bf16[2048,2048]{1,0:T(8,128)(2,1)} %all-gather.3.cloned.1.call-done, s32[2048]{0:T(1024)S(1)} %bitcast_clamp_fusion), kind=kCustom, calls=%fused_computation.1 | custom fusion | bytes 16785408 | tf_op jit(solution)/shard_map/gather | solution.py:131
  201.2 0.0 copy-done.1
  201.2 0.0 copy-start
  201.2 6.0 %fusion.15 = bf16[768,2048]{1,0:T(8,128)(2,1)S(1)} fusion(bf16[2048,2048]{1,0:T(8,128)(2,1)} %gather_fusion.1, bf16[2,1024,768]{2,1,0:T(8,128)(2,1)S(1)} %bitcast.68), kind=kOutput, calls=%fused_computation.28 | convolution fusion | flops 3222798336 | bytes 8912896 | tf_op jit(solution)/shard_map/sf,sd->fd/dot_general | solution.py:145
  207.3 0.0 copy-done
  207.3 3.7 %fusion.12 = bf16[768,2048]{1,0:T(8,128)(2,1)S(1)} fusion(bf16[2048,2048]{1,0:T(8,128)(2,1)S(1)} %copy-done, bf16[2,1024,768]{2,1,0:T(8,128)(2,1)S(1)} %bitcast.69), kind=kOutput, calls=%fused_computation.27 | convolution fusion | flops 3222798336 | bytes 8912896 | tf_op jit(solution)/shard_map/sf,sd->fd/dot_general | solution.py:145
  211.0 3.3 %pad_maximum_fusion = bf16[16,2,48,2048]{3,2,1,0:T(8,128)(2,1)} fusion(bf16[16,1,48,2048]{3,2,1,0:T(8,128)(2,1)S(1)} %bitcast.71, bf16[16,1,48,2048]{3,2,1,0:T(8,128)(2,1)S(1)} %bitcast.72), kind=kLoop, calls=%fused_computation.7 | loop fusion | flops 3145728 | bytes 12582912 | tf_op jit(solution)/shard_map/stack | solution.py:149
  214.3 0.0 reduce-scatter.2.cloned.1.call-update
  214.3 11.2 %fusion.29 = bf16[2,1024,16,48]{1,3,2,0:T(8,128)(2,1)S(1)} fusion(bf16[2,1024,2048,1]{2,1,3,0:T(8,128)(2,1)} %bitcast.67, bf16[16,2,48,2048]{3,2,1,0:T(8,128)(2,1)} %shard_map.76), kind=kOutput, calls=%fused_computation.42 | convolution fusion | flops 6444023808 | bytes 17825792 | tf_op jit(solution)/shard_map/jsd,qjid->jsqi/dot_general | solution.py:133
  225.5 5.6 %copy.55 = bf16[1,2,1024,768]{3,1,0,2:T(2,128)(2,1)} copy(bf16[1,2,1024,768]{2,3,1,0:T(8,128)(2,1)S(1)} %bitcast.70) | data formatting | bytes 6291456 | tf_op jit(solution)/shard_map/reshape;reshape | solution.py:137
  231.2 0.0 copy-start.2
  231.2 4.4 %all-to-all-start.1 = ((bf16[1,2,1024,768]{3,1,0,2:T(2,128)(2,1)}), bf16[1,2,1024,768]{3,1,0,2:T(2,128)(2,1)S(1)}, u32[]{:S(2)}, u32[]{:S(2)}) async-start(bf16[1,2,1024,768]{3,1,0,2:T(2,128)(2,1)} %copy.55), calls=%async_computation.1 | async-start | bytes 6291456 | tf_op jit(solution)/shard_map/all_to_all | solution.py:136
  235.5 0.0 copy-done.2
  235.6 0.1 copy.58
  235.7 0.1 mul.108
  235.8 40.0 %all-to-all-done.1 = bf16[1,2,1024,768]{3,1,0,2:T(2,128)(2,1)S(1)} async-done(((bf16[1,2,1024,768]{3,1,0,2:T(2,128)(2,1)}), bf16[1,2,1024,768]{3,1,0,2:T(2,128)(2,1)S(1)}, u32[]{:S(2)}, u32[]{:S(2)}) %all-to-all-start.1) | async-done | bytes 3145760 | tf_op jit(solution)/shard_map/all_to_all | solution.py:136
  275.8 0.4 copy.56
  276.2 0.2 copy.57
  276.4 5.2 %gather_fusion.2 = bf16[1024,768]{1,0:T(8,128)(2,1)} fusion(bf16[2048,768]{1,0:T(8,128)(2,1)S(1)} %bitcast.64, s32[1024]{0:T(1024)S(1)} %broadcast_clamp_fusion.1), kind=kCustom, calls=%fused_computation.2 | custom fusion | bytes 3149824 | tf_op jit(solution)/shard_map/gather | solution.py:151
  281.7 4.2 %fusion.22 = (bf16[128,8,768]{2,1,0:T(8,128)(2,1)S(1)}, bf16[128,8,768]{2,1,0:T(8,128)(2,1)S(1)}, f32[128,8]{1,0:T(8,128)S(1)}) fusion(bf16[1024,768]{1,0:T(8,128)(2,1)} %gather_fusion.2, f32[128,8]{1,0:T(8,128)S(1)} %copy.49, bf16[128,8,1536]{2,1,0:T(8,128)(2,1)} %param.6, bf16[128,8,768]{2,1,0:T(8,128)(2,1)} %get-tuple-element.18), kind=kLoop, calls=%fused_computation.33 | loop fusion | flops 15727616 | bytes 9445376 | tf_op jit(solution)/shard_map/convert.2
  285.9 0.7 copy.61
  286.6 1.9 pad_maximum_fusion.1
  288.5 0.0 reduce-scatter.2.cloned.1.call-done
  288.5 1.9 bitcast_convert_fusion
  (15 shorter events, 0.1 us)
Async XLA Ops:
  7.2 172.9 %all-gather.3.cloned.1.call-start = ((), (), s32[]{:S(2)}) async-start(), calls=%async_computation.3 | async-start | bytes 8912896 | tf_op jit(solution)/shard_map/all_gather | solution.py:98
  107.4 70.8 %all-to-all-start = ((bf16[16,2,64,768]{3,2,1,0:T(8,128)(2,1)}), bf16[16,2,64,768]{3,2,1,0:T(8,128)(2,1)S(1)}, u32[]{:S(2)}, u32[]{:S(2)}) async-start(bf16[16,2,64,768]{3,2,1,0:T(8,128)(2,1)} %broadcast_select_fusion), calls=%async_computation | async-start | bytes 6291456 | tf_op jit(solution)/shard_map/all_to_all | solution.py:129
  114.4 174.1 %reduce-scatter.2.cloned.1.call-start = ((), (), s32[]{:S(2)}) async-start(), calls=%async_computation.4 | async-start | bytes 6684672 | tf_op jit(solution)/shard_map/reduce_scatter | solution.py:149
  180.1 21.1 %copy-start.1 = (bf16[16,2,64,768]{3,2,0,1:T(8,128)(2,1)S(1)}, bf16[16,2,64,768]{3,2,0,1:T(8,128)(2,1)}, u32[]{:S(2)}) copy-start(bf16[16,2,64,768]{3,2,0,1:T(8,128)(2,1)} %copy.51) | copy-start | bytes 9437188
  201.2 6.0 %copy-start = (bf16[2048,2048]{1,0:T(8,128)(2,1)S(1)}, bf16[2048,2048]{1,0:T(8,128)(2,1)}, u32[]{:S(2)}) copy-start(bf16[2048,2048]{1,0:T(8,128)(2,1)} %gather_fusion.1) | copy-start | bytes 25165828
  231.2 4.4 %copy-start.2 = (s32[128,8]{0,1:T(8,128)S(1)}, s32[128,8]{0,1:T(8,128)}, u32[]{:S(2)}) copy-start(s32[128,8]{0,1:T(8,128)} %param.7) | copy-start | bytes 12292
  231.2 44.7 %all-to-all-start.1 = ((bf16[1,2,1024,768]{3,1,0,2:T(2,128)(2,1)}), bf16[1,2,1024,768]{3,1,0,2:T(2,128)(2,1)S(1)}, u32[]{:S(2)}, u32[]{:S(2)}) async-start(bf16[1,2,1024,768]{3,1,0,2:T(2,128)(2,1)} %copy.55), calls=%async_computation.1 | async-start | bytes 6291456 | tf_op jit(solution)/shard_map/all_to_all | solution.py:136
Sparse Core Ops, SparseCore 0:
  10.4 77.9 all-gather.2
  214.4 58.2 reduce-scatter.1

commit v4 on v3

--- a/solution.py
+++ b/solution.py
@@ -22,12 +22,13 @@
     return z * 2 + jnp.where(lax.rem(z, 2) == 0, core, 1 - core)
 
 
-def gather_kernel(replicas, w_ref, o_ref, own_sem, send_sem, recv_sem):
+def gather_kernel(replicas, pieces, w_ref, o_ref, own_sem, send_sem, recv_sem):
     me = lax.axis_index("dp")
     col = lax.axis_index("expert")
     pos = ring_pos(me)
     right = ring_dp(pos + 1, replicas)
     left = ring_dp(pos - 1, replicas)
+    cols = w_ref.shape[2] // pieces
 
     barrier = pltpu.get_barrier_semaphore()
     for neighbour in (left, right):
@@ -36,37 +37,42 @@
 
     own = pltpu.make_async_copy(w_ref, o_ref.at[me], own_sem)
     own.start()
-    for step in range(replicas - 1):
+    hops = (replicas // 2, replicas - 1 - replicas // 2)
+    for step in range(hops[0]):
         copies = []
-        for j, (target, origin) in enumerate(((right, pos - step), (left, pos + step))):
-            block = ring_dp(origin, replicas)
-            src = w_ref.at[j] if step == 0 else o_ref.at[block, j]
-            copy = pltpu.make_async_remote_copy(
-                src_ref=src,
-                dst_ref=o_ref.at[block, j],
-                send_sem=send_sem.at[j, step],
-                recv_sem=recv_sem.at[j, step],
-                device_id=(target, col),
-                device_id_type=MESH,
-            )
-            copy.start()
-            copies.append(copy)
+        for way, (target, sign) in enumerate(((right, -1), (left, 1))):
+            if step >= hops[way]:
+                continue
+            block = ring_dp(pos + sign * step, replicas)
+            for piece in range(pieces):
+                part = pl.ds(piece * cols, cols)
+                src = w_ref.at[:, :, part] if step == 0 else o_ref.at[block, :, :, part]
+                copy = pltpu.make_async_remote_copy(
+                    src_ref=src,
+                    dst_ref=o_ref.at[block, :, :, part],
+                    send_sem=send_sem.at[way, step, piece],
+                    recv_sem=recv_sem.at[way, step, piece],
+                    device_id=(target, col),
+                    device_id_type=MESH,
+                )
+                copy.start()
+                copies.append(copy)
         for copy in copies:
             copy.wait()
     own.wait()
 
 
-def gather_down(w_down, replicas):
+def gather_down(w_down, replicas, pieces=4):
     local_experts, rows, width = w_down.shape
     return pl.pallas_call(
-        lambda *refs: gather_kernel(replicas, *refs),
+        lambda *refs: gather_kernel(replicas, pieces, *refs),
         out_shape=jax.ShapeDtypeStruct((replicas, local_experts, rows, width), w_down.dtype),
         in_specs=[pl.BlockSpec(memory_space=pl.ANY)],
         out_specs=pl.BlockSpec(memory_space=pl.ANY),
         scratch_shapes=[
             pltpu.SemaphoreType.DMA(()),
-            pltpu.SemaphoreType.DMA((2, replicas - 1)),
-            pltpu.SemaphoreType.DMA((2, replicas - 1)),
+            pltpu.SemaphoreType.DMA((2, replicas // 2, pieces)),
+            pltpu.SemaphoreType.DMA((2, replicas // 2, pieces)),
         ],
         compiler_params=pltpu.CompilerParams(collective_id=0, has_side_effects=True),
         cost_estimate=pl.CostEstimate(
@@ -95,8 +101,13 @@
     capacity = min(tokens, 2 * tokens * top // experts)
     routes = tokens * top
 
-    cot_group = lax.all_gather(cotangent, "expert", axis=0, tiled=True)
-    ids_group = lax.all_gather(route_ids.reshape(1, routes), "expert", axis=0, tiled=True)
+    lanes = 128
+    ids_cols = jnp.pad(route_ids.astype(jnp.bfloat16), ((0, 0), (0, lanes - top)))
+    cot_ext = lax.all_gather(
+        jnp.concatenate([cotangent, ids_cols], axis=1), "expert", axis=0, tiled=True
+    )
+    ids_group = cot_ext[:, width:width + top].astype(jnp.int32).reshape(owners, routes)
+    cot_group = cot_ext[:, :width]
     full_down = gather_down(w_down, replicas)
 
     gate = saved_gate_up[:, :, :hidden_units].astype(jnp.float32)

time: 299 us -> 281 us (0.940)
  the two profiles are of different devices: /device:TPU:64 before, /device:TPU:33 now
where the time goes in v4:
time: 281 us
  waiting for transfers between devices  91.2 us (32%)
  Pallas kernels  61.2 us (22%)
  local copies, waits for them, and re-layouts  55.6 us (20%)
  other arithmetic  25 us (9%)
  matrix products  22.9 us (8%)
  between operations  14.2 us (5%)
  starting transfers between devices  10.6 us (4%)
    pallas_call x1, Pallas kernels, gather_down(): pl.pallas_call(lambda *refs: gather_kernel(replicas, pieces, *refs), out_...  61.2 us
    all_to_all x1, waiting for transfers between devices, local(): lax.all_to_all(grads.reshape(1, local_experts, owners * capacity, hidden_...  47.4 us
    all_to_all x1, waiting for transfers between devices, local(): lax.all_to_all(h_send, 'expert', split_axis=0, concat_axis=2, tiled=True)[0]  43.7 us
    gather x1, local copies, waits for them, and re-layouts, local(): dy_recv = cot_group[rows]  21.1 us
    dot_general x1, matrix products, local(): jnp.einsum('jsd,qjid->jsqi', dy_recv, full_down, preferred_element_type=j...  11.2 us
    dot_general x2, matrix products, local(): jnp.einsum('sf,sd->fd', h_recv[j], dy_recv[j], preferred_element_type=jnp...  9.73 us
    gather x1, local copies, waits for them, and re-layouts, local(): scaled.reshape(routes, hidden_units)[route_of_slot]  9.4 us
    slice x1, local copies, waits for them, and re-layouts, local(): cot_group = cot_ext[:, :width]  8.27 us
  transfers between devices with their start and end apart: 4, of which 2 were waited for; matrix products, arithmetic and copies ran while one was open for 19% of the time, Pallas kernels for 22%

profile of v4, /device:TPU:33, one launch (start us, length us, event | category | flops | bytes accessed | tf_op | source)
XLA Modules:
  0.0 280.8 jit_solution(795166418756804255)
XLA Ops:
  7.2 0.0 all-gather.2.cloned.1.call-start
  7.2 0.8 broadcast_multiply_fusion
  8.0 0.1 copy.77
  8.1 1.9 fusion.45
  10.0 0.0 all-gather.2.cloned.1.call-update
  10.0 0.8 copy.64
  10.8 0.8 copy.63
  11.6 0.1 reshape.178
  11.7 0.5 fusion.40
  12.2 1.0 fusion
  13.3 0.1 broadcast_in_dim.34
  13.3 61.2 %shard_map.76 = bf16[16,2,48,2048]{3,2,1,0:T(8,128)(2,1)} custom-call(bf16[2,48,2048]{2,1,0:T(8,128)(2,1)} %refs_0_.1), custom_call_target="tpu_custom_call" | custom-call | bytes 12582912 | tf_op jit(solution)/shard_map/pallas_call | solution.py:67
  74.5 0.9 select_reduce_fusion.1
  75.5 3.4 %fusion.34 = (bf16[1024,768]{1,0:T(8,128)(2,1)S(1)}, bf16[128,8,768]{2,1,0:T(8,128)(2,1)}) fusion(f32[128,8]{1,0:T(8,128)S(1)} %copy.63, bf16[128,8,1536]{2,1,0:T(8,128)(2,1)} %param.6), kind=kLoop, calls=%fused_computation.47 | loop fusion | flops 8650752 | bytes 6295552 | tf_op jit(solution)/shard_map/reshape | solution.py:128
  78.9 9.4 %gather_fusion = bf16[2048,768]{1,0:T(8,128)(2,1)} fusion(bf16[1024,768]{1,0:T(8,128)(2,1)S(1)} %get-tuple-element.20, s32[2048]{0:T(1024)S(1)} %broadcast_clamp_fusion), kind=kCustom, calls=%fused_computation | custom fusion | bytes 6299648 | tf_op jit(solution)/shard_map/gather | solution.py:128
  88.3 3.3 %broadcast_select_fusion = bf16[16,2,64,768]{3,2,1,0:T(8,128)(2,1)} fusion(bf16[16,2,64,768]{3,2,1,0:T(8,128)(2,1)} %bitcast.61, pred[16,2,64]{2,1,0:T(4,128)(4,1)S(1)} %broadcast_in_dim.34), kind=kLoop, calls=%fused_computation.41 | loop fusion | flops 1572864 | bytes 6293504 | tf_op jit(solution)/shard_map/jit(_where)/select_n | solution.py:128
  91.6 6.8 %all-to-all-start = ((bf16[16,2,64,768]{3,2,1,0:T(8,128)(2,1)}), bf16[16,2,64,768]{3,2,1,0:T(8,128)(2,1)S(1)}, u32[]{:S(2)}, u32[]{:S(2)}) async-start(bf16[16,2,64,768]{3,2,1,0:T(8,128)(2,1)} %broadcast_select_fusion), calls=%async_computation | async-start | bytes 6291456 | tf_op jit(solution)/shard_map/all_to_all | solution.py:140
  98.4 0.0 reduce-scatter.2.cloned.1.call-start
  98.4 0.1 iota_add_fusion
  98.5 0.1 add.127
  98.6 43.7 %all-to-all-done = bf16[16,2,64,768]{3,2,1,0:T(8,128)(2,1)S(1)} async-done(((bf16[16,2,64,768]{3,2,1,0:T(8,128)(2,1)}), bf16[16,2,64,768]{3,2,1,0:T(8,128)(2,1)S(1)}, u32[]{:S(2)}, u32[]{:S(2)}) %all-to-all-start) | async-done | bytes 3145760 | tf_op jit(solution)/shard_map/all_to_all | solution.py:140
  142.3 1.9 copy.65
  144.2 0.0 all-gather.2.cloned.1.call-done
  144.2 1.1 slice_convert_fusion
  145.4 0.5 reshape.185
  145.9 1.4 fusion.32
  147.3 1.0 select_reduce_fusion
  148.3 0.1 reduce_sum.54
  148.4 0.1 add_bitcast_fusion
  148.5 0.1 reshape.182
  148.6 8.3 %slice.40 = bf16[2048,2048]{1,0:T(8,128)(2,1)} slice(bf16[2048,2176]{1,0:T(8,128)(2,1)} %all-gather.2.cloned.1.call-done), slice={[0:2048], [0:2048]} | slice | bytes 16777216 | tf_op jit(solution)/shard_map/slice | solution.py:110
  156.9 0.0 copy-start.1
  156.9 21.1 %gather_fusion.1 = bf16[2048,2048]{1,0:T(8,128)(2,1)} fusion(bf16[2048,2048]{1,0:T(8,128)(2,1)} %slice.40, s32[2048]{0:T(1024)S(1)} %bitcast_clamp_fusion), kind=kCustom, calls=%fused_computation.1 | custom fusion | bytes 16785408 | tf_op jit(solution)/shard_map/gather | solution.py:142
  178.0 0.0 copy-done.1
  178.0 0.0 copy-start
  178.0 6.0 %fusion.15 = bf16[768,2048]{1,0:T(8,128)(2,1)S(1)} fusion(bf16[2048,2048]{1,0:T(8,128)(2,1)} %gather_fusion.1, bf16[2,1024,768]{2,1,0:T(8,128)(2,1)S(1)} %bitcast.63), kind=kOutput, calls=%fused_computation.28 | convolution fusion | flops 3222798336 | bytes 8912896 | tf_op jit(solution)/shard_map/sf,sd->fd/dot_general | solution.py:156
  184.0 0.0 copy-done
  184.0 3.7 %fusion.12 = bf16[768,2048]{1,0:T(8,128)(2,1)S(1)} fusion(bf16[2048,2048]{1,0:T(8,128)(2,1)S(1)} %copy-done, bf16[2,1024,768]{2,1,0:T(8,128)(2,1)S(1)} %bitcast.64), kind=kOutput, calls=%fused_computation.27 | convolution fusion | flops 3222798336 | bytes 8912896 | tf_op jit(solution)/shard_map/sf,sd->fd/dot_general | solution.py:156
  187.7 3.3 %pad_maximum_fusion = bf16[16,2,48,2048]{3,2,1,0:T(8,128)(2,1)} fusion(bf16[16,1,48,2048]{3,2,1,0:T(8,128)(2,1)S(1)} %bitcast.66, bf16[16,1,48,2048]{3,2,1,0:T(8,128)(2,1)S(1)} %bitcast.67), kind=kLoop, calls=%fused_computation.7 | loop fusion | flops 3145728 | bytes 12582912 | tf_op jit(solution)/shard_map/stack | solution.py:160
  191.0 0.0 reduce-scatter.2.cloned.1.call-update
  191.1 11.2 %fusion.29 = bf16[2,1024,16,48]{1,3,2,0:T(8,128)(2,1)S(1)} fusion(bf16[2,1024,2048,1]{2,1,3,0:T(8,128)(2,1)} %bitcast.62, bf16[16,2,48,2048]{3,2,1,0:T(8,128)(2,1)} %shard_map.76), kind=kOutput, calls=%fused_computation.42 | convolution fusion | flops 6444023808 | bytes 17825792 | tf_op jit(solution)/shard_map/jsd,qjid->jsqi/dot_general | solution.py:144
  202.3 5.6 %copy.69 = bf16[1,2,1024,768]{3,1,0,2:T(2,128)(2,1)} copy(bf16[1,2,1024,768]{2,3,1,0:T(8,128)(2,1)S(1)} %bitcast.65) | data formatting | bytes 6291456 | tf_op jit(solution)/shard_map/reshape;reshape | solution.py:148
  207.9 3.7 %all-to-all-start.1 = ((bf16[1,2,1024,768]{3,1,0,2:T(2,128)(2,1)}), bf16[1,2,1024,768]{3,1,0,2:T(2,128)(2,1)S(1)}, u32[]{:S(2)}, u32[]{:S(2)}) async-start(bf16[1,2,1024,768]{3,1,0,2:T(2,128)(2,1)} %copy.69), calls=%async_computation.1 | async-start | bytes 6291456 | tf_op jit(solution)/shard_map/all_to_all | solution.py:147
  211.7 0.1 copy.72
  211.8 0.1 mul.112
  211.9 47.4 %all-to-all-done.1 = bf16[1,2,1024,768]{3,1,0,2:T(2,128)(2,1)S(1)} async-done(((bf16[1,2,1024,768]{3,1,0,2:T(2,128)(2,1)}), bf16[1,2,1024,768]{3,1,0,2:T(2,128)(2,1)S(1)}, u32[]{:S(2)}, u32[]{:S(2)}) %all-to-all-start.1) | async-done | bytes 3145760 | tf_op jit(solution)/shard_map/all_to_all | solution.py:147
  259.3 0.4 copy.70
  259.7 0.2 copy.71
  260.0 5.2 %gather_fusion.2 = bf16[1024,768]{1,0:T(8,128)(2,1)} fusion(bf16[2048,768]{1,0:T(8,128)(2,1)S(1)} %bitcast.59, s32[1024]{0:T(1024)S(1)} %broadcast_clamp_fusion.1), kind=kCustom, calls=%fused_computation.2 | custom fusion | bytes 3149824 | tf_op jit(solution)/shard_map/gather | solution.py:162
  265.2 4.2 %fusion.22 = (bf16[128,8,768]{2,1,0:T(8,128)(2,1)S(1)}, bf16[128,8,768]{2,1,0:T(8,128)(2,1)S(1)}, f32[128,8]{1,0:T(8,128)S(1)}) fusion(bf16[1024,768]{1,0:T(8,128)(2,1)} %gather_fusion.2, f32[128,8]{1,0:T(8,128)S(1)} %copy.63, bf16[128,8,1536]{2,1,0:T(8,128)(2,1)} %param.6, bf16[128,8,768]{2,1,0:T(8,128)(2,1)} %get-tuple-element.21), kind=kLoop, calls=%fused_computation.33 | loop fusion | flops 15727616 | bytes 9445376 | tf_op jit(solution)/shard_map/convert.3
  269.4 0.7 copy.75
  270.1 1.9 pad_maximum_fusion.1
  272.0 0.0 reduce-scatter.2.cloned.1.call-done
  272.0 1.9 bitcast_convert_fusion
  (13 shorter events, 0.1 us)
Async XLA Ops:
  7.2 137.1 %all-gather.2.cloned.1.call-start = ((), (), s32[]{:S(2)}) async-start(), calls=%async_computation.3 | async-start | bytes 9469952 | tf_op jit(solution)/shard_map/all_gather | solution.py:106
  91.6 50.8 %all-to-all-start = ((bf16[16,2,64,768]{3,2,1,0:T(8,128)(2,1)}), bf16[16,2,64,768]{3,2,1,0:T(8,128)(2,1)S(1)}, u32[]{:S(2)}, u32[]{:S(2)}) async-start(bf16[16,2,64,768]{3,2,1,0:T(8,128)(2,1)} %broadcast_select_fusion), calls=%async_computation | async-start | bytes 6291456 | tf_op jit(solution)/shard_map/all_to_all | solution.py:140
  98.4 173.6 %reduce-scatter.2.cloned.1.call-start = ((), (), s32[]{:S(2)}) async-start(), calls=%async_computation.4 | async-start | bytes 6684672 | tf_op jit(solution)/shard_map/reduce_scatter | solution.py:160
  156.9 21.1 %copy-start.1 = (bf16[16,2,64,768]{3,2,0,1:T(8,128)(2,1)S(1)}, bf16[16,2,64,768]{3,2,0,1:T(8,128)(2,1)}, u32[]{:S(2)}) copy-start(bf16[16,2,64,768]{3,2,0,1:T(8,128)(2,1)} %copy.65) | copy-start | bytes 9437188
  178.0 6.0 %copy-start = (bf16[2048,2048]{1,0:T(8,128)(2,1)S(1)}, bf16[2048,2048]{1,0:T(8,128)(2,1)}, u32[]{:S(2)}) copy-start(bf16[2048,2048]{1,0:T(8,128)(2,1)} %gather_fusion.1) | copy-start | bytes 25165828
  207.9 51.4 %all-to-all-start.1 = ((bf16[1,2,1024,768]{3,1,0,2:T(2,128)(2,1)}), bf16[1,2,1024,768]{3,1,0,2:T(2,128)(2,1)S(1)}, u32[]{:S(2)}, u32[]{:S(2)}) async-start(bf16[1,2,1024,768]{3,1,0,2:T(2,128)(2,1)} %copy.69), calls=%async_computation.1 | async-start | bytes 6291456 | tf_op jit(solution)/shard_map/all_to_all | solution.py:147
Sparse Core Ops, SparseCore 0:
  11.0 80.7 all-gather.1
  191.2 58.3 reduce-scatter.1

commit v5 on v4

--- a/solution.py
+++ b/solution.py
@@ -22,7 +22,8 @@
     return z * 2 + jnp.where(lax.rem(z, 2) == 0, core, 1 - core)
 
 
-def gather_kernel(replicas, pieces, w_ref, o_ref, own_sem, send_sem, recv_sem):
+def exchange_kernel(replicas, owners, pieces, w_ref, h_ref, o_ref, g_ref, sems, send_sem, recv_sem,
+                    h_send_sem, h_recv_sem):
     me = lax.axis_index("dp")
     col = lax.axis_index("expert")
     pos = ring_pos(me)
@@ -33,10 +34,29 @@
     barrier = pltpu.get_barrier_semaphore()
     for neighbour in (left, right):
         pl.semaphore_signal(barrier, inc=1, device_id=(neighbour, col), device_id_type=MESH)
-    pl.semaphore_wait(barrier, 2)
-
-    own = pltpu.make_async_copy(w_ref, o_ref.at[me], own_sem)
+    for peer in range(owners - 1):
+        other = lax.rem(col + 1 + peer, owners)
+        pl.semaphore_signal(barrier, inc=1, device_id=(me, other), device_id_type=MESH)
+    pl.semaphore_wait(barrier, 2 + owners - 1)
+
+    own = pltpu.make_async_copy(w_ref, o_ref.at[me], sems.at[0])
     own.start()
+    own_h = pltpu.make_async_copy(h_ref.at[col], g_ref.at[col], sems.at[1])
+    own_h.start()
+    outgoing = []
+    for peer in range(owners - 1):
+        other = lax.rem(col + 1 + peer, owners)
+        copy = pltpu.make_async_remote_copy(
+            src_ref=h_ref.at[other],
+            dst_ref=g_ref.at[col],
+            send_sem=h_send_sem.at[other],
+            recv_sem=h_recv_sem.at[col],
+            device_id=(me, other),
+            device_id_type=MESH,
+        )
+        copy.start()
+        outgoing.append(copy)
+
     hops = (replicas // 2, replicas - 1 - replicas // 2)
     for step in range(hops[0]):
         copies = []
@@ -59,26 +79,47 @@
                 copies.append(copy)
         for copy in copies:
             copy.wait()
+
+    for copy in outgoing:
+        copy.wait_send()
+    for peer in range(owners - 1):
+        source = lax.rem(col + 1 + peer, owners)
+        incoming = pltpu.make_async_remote_copy(
+            src_ref=h_ref.at[source],
+            dst_ref=g_ref.at[source],
+            send_sem=h_send_sem.at[source],
+            recv_sem=h_recv_sem.at[source],
+            device_id=(me, source),
+            device_id_type=MESH,
+        )
+        incoming.wait_recv()
     own.wait()
-
-
-def gather_down(w_down, replicas, pieces=4):
-    local_experts, rows, width = w_down.shape
+    own_h.wait()
+
+
+def exchange(w_down, h_send, replicas, owners, pieces=4):
     return pl.pallas_call(
-        lambda *refs: gather_kernel(replicas, pieces, *refs),
-        out_shape=jax.ShapeDtypeStruct((replicas, local_experts, rows, width), w_down.dtype),
-        in_specs=[pl.BlockSpec(memory_space=pl.ANY)],
-        out_specs=pl.BlockSpec(memory_space=pl.ANY),
+        lambda *refs: exchange_kernel(replicas, owners, pieces, *refs),
+        out_shape=(
+            jax.ShapeDtypeStruct((replicas,) + w_down.shape, w_down.dtype),
+            jax.ShapeDtypeStruct(h_send.shape, h_send.dtype),
+        ),
+        in_specs=[pl.BlockSpec(memory_space=pl.ANY)] * 2,
+        out_specs=(pl.BlockSpec(memory_space=pl.ANY), pl.BlockSpec(memory_space=pl.ANY)),
         scratch_shapes=[
-            pltpu.SemaphoreType.DMA(()),
+            pltpu.SemaphoreType.DMA((2,)),
             pltpu.SemaphoreType.DMA((2, replicas // 2, pieces)),
             pltpu.SemaphoreType.DMA((2, replicas // 2, pieces)),
+            pltpu.SemaphoreType.DMA((owners,)),
+            pltpu.SemaphoreType.DMA((owners,)),
         ],
         compiler_params=pltpu.CompilerParams(collective_id=0, has_side_effects=True),
         cost_estimate=pl.CostEstimate(
-            flops=0, bytes_accessed=2 * replicas * w_down.size * 2, transcendentals=0
-        ),
-    )(w_down)
+            flops=0,
+            bytes_accessed=2 * replicas * w_down.size * 2 + 2 * h_send.size * 2,
+            transcendentals=0,
+        ),
+    )(w_down, h_send)
 
 
 def slot_counts(ids, experts):
@@ -108,7 +149,6 @@
     )
     ids_group = cot_ext[:, width:width + top].astype(jnp.int32).reshape(owners, routes)
     cot_group = cot_ext[:, :width]
-    full_down = gather_down(w_down, replicas)
 
     gate = saved_gate_up[:, :, :hidden_units].astype(jnp.float32)
     up = saved_gate_up[:, :, hidden_units:].astype(jnp.float32)
@@ -136,8 +176,8 @@
     token_of = jnp.sum(jnp.where(hit, (jnp.arange(routes, dtype=jnp.int32) // top)[None, None, :], 0), axis=2)
     rows = (jnp.arange(owners, dtype=jnp.int32)[:, None] * tokens + token_of).reshape(owners, local_experts, capacity)
     rows = jnp.transpose(rows, (1, 0, 2)).reshape(local_experts, owners * capacity)
-    full_down, h_send = lax.optimization_barrier((full_down, h_send))
-    h_recv = lax.all_to_all(h_send, "expert", split_axis=0, concat_axis=2, tiled=True)[0]
+    full_down, h_got = exchange(w_down, h_send, replicas, owners)
+    h_recv = jnp.transpose(h_got, (1, 0, 2, 3)).reshape(local_experts, owners * capacity, hidden_units)
     h_recv, cot_group = lax.optimization_barrier((h_recv, cot_group))
     dy_recv = cot_group[rows]
 

time: 281 us -> 264 us (0.940)
  the two profiles are of different devices: /device:TPU:33 before, /device:TPU:64 now
where the time goes in v5:
time: 264 us; the launch traced here: 262 us
  waiting for transfers between devices  70 us (27%)
  Pallas kernels  67.9 us (26%)
  local copies, waits for them, and re-layouts  57.5 us (22%)
  other arithmetic  25.2 us (10%)
  matrix products  23.1 us (9%)
  between operations  14.2 us (5%)
  starting transfers between devices  3.94 us (1%)
    pallas_call x1, Pallas kernels, exchange(): pl.pallas_call(lambda *refs: exchange_kernel(replicas, owners, pieces, *r...  67.9 us
    all_to_all x1, waiting for transfers between devices, local(): lax.all_to_all(grads.reshape(1, local_experts, owners * capacity, hidden_...  48.2 us
    all_gather x1, waiting for transfers between devices, local(): lax.all_gather(jnp.concatenate([cotangent, ids_cols], axis=1), 'expert',...  21.8 us
    gather x1, local copies, waits for them, and re-layouts, local(): dy_recv = cot_group[rows]  20.9 us
    dot_general x1, matrix products, local(): jnp.einsum('jsd,qjid->jsqi', dy_recv, full_down, preferred_element_type=j...  11.2 us
    dot_general x2, matrix products, local(): jnp.einsum('sf,sd->fd', h_recv[j], dy_recv[j], preferred_element_type=jnp...  9.96 us
    gather x1, local copies, waits for them, and re-layouts, local(): scaled.reshape(routes, hidden_units)[route_of_slot]  9.4 us
    slice x1, local copies, waits for them, and re-layouts, local(): cot_group = cot_ext[:, :width]  8.27 us
  transfers between devices with their start and end apart: 3, of which 2 were waited for; matrix products, arithmetic and copies ran while one was open for 21% of the time, Pallas kernels for 26%

profile of v5, /device:TPU:64, one launch (start us, length us, event | category | flops | bytes accessed | tf_op | source)
XLA Modules:
  0.0 261.9 jit_solution(18231834956399788937)
XLA Ops:
  7.2 0.0 all-gather.2.cloned.1.call-start
  7.2 0.8 broadcast_multiply_fusion
  8.0 0.1 copy.75
  8.1 1.9 fusion.45
  10.0 0.0 all-gather.2.cloned.1.call-update
  10.0 0.0 reduce-scatter.2.cloned.1.call-start
  10.1 0.8 copy.62
  10.9 0.1 iota_add_fusion
  10.9 0.1 add.127
  11.0 0.8 copy.61
  11.8 0.1 reshape.180
  11.9 0.5 fusion.40
  12.5 1.0 fusion
  13.5 0.1 broadcast_in_dim.34
  13.6 0.9 select_reduce_fusion.1
  14.5 3.6 %fusion.34 = (bf16[1024,768]{1,0:T(8,128)(2,1)S(1)}, bf16[128,8,768]{2,1,0:T(8,128)(2,1)}) fusion(f32[128,8]{1,0:T(8,128)S(1)} %copy.61, bf16[128,8,1536]{2,1,0:T(8,128)(2,1)} %param.6), kind=kLoop, calls=%fused_computation.47 | loop fusion | flops 8650752 | bytes 6295552 | tf_op jit(solution)/shard_map/reshape | solution.py:168
  18.1 9.4 %gather_fusion = bf16[2048,768]{1,0:T(8,128)(2,1)} fusion(bf16[1024,768]{1,0:T(8,128)(2,1)S(1)} %get-tuple-element.20, s32[2048]{0:T(1024)S(1)} %broadcast_clamp_fusion), kind=kCustom, calls=%fused_computation | custom fusion | bytes 6299648 | tf_op jit(solution)/shard_map/gather | solution.py:168
  27.5 3.3 %broadcast_select_fusion.refs_1_ = bf16[16,2,64,768]{3,2,1,0:T(8,128)(2,1)} fusion(bf16[16,2,64,768]{3,2,1,0:T(8,128)(2,1)} %bitcast.58, pred[16,2,64]{2,1,0:T(4,128)(4,1)S(1)} %broadcast_in_dim.34), kind=kLoop, calls=%fused_computation.41 | loop fusion | flops 1572864 | bytes 6293504 | tf_op jit(solution)/shard_map/jit(_where)/select_n | solution.py:168
  30.8 67.9 %shard_map.76 = (bf16[16,2,48,2048]{3,2,1,0:T(8,128)(2,1)}, bf16[16,2,64,768]{3,2,1,0:T(8,128)(2,1)}) custom-call(bf16[2,48,2048]{2,1,0:T(8,128)(2,1)} %refs_0_.1, bf16[16,2,64,768]{3,2,1,0:T(8,128)(2,1)} %broadcast_select_fusion.refs_1_), custom_call_target="tpu_custom_call" | custom-call | bytes 18874368 | tf_op jit(solution)/shard_map/pallas_call | solution.py:101
  98.7 3.9 %copy.63 = bf16[2,16,64,768]{3,2,1,0:T(8,128)(2,1)} copy(bf16[2,16,64,768]{3,2,0,1:T(8,128)(2,1)} %bitcast.62) | data formatting | bytes 6291456 | tf_op jit(solution)/shard_map/transpose | solution.py:180
  102.6 21.8 %all-gather.2.cloned.1.call-done = bf16[2048,2176]{1,0:T(8,128)(2,1)} async-done(((bf16[128,2176]{1,0:T(8,128)(2,1)}), bf16[2048,2176]{1,0:T(8,128)(2,1)}) %all-gather.2.cloned.1.call-update) | async-done | bytes 8912912 | tf_op jit(solution)/shard_map/all_gather | solution.py:147
  124.4 1.1 slice_convert_fusion
  125.5 0.5 reshape.188
  126.0 1.4 fusion.32
  127.5 1.0 select_reduce_fusion
  128.4 0.1 reduce_sum.54
  128.5 0.1 add_bitcast_fusion
  128.6 0.1 reshape.185
  128.7 8.3 %slice.40 = bf16[2048,2048]{1,0:T(8,128)(2,1)} slice(bf16[2048,2176]{1,0:T(8,128)(2,1)} %all-gather.2.cloned.1.call-done), slice={[0:2048], [0:2048]} | slice | bytes 16777216 | tf_op jit(solution)/shard_map/slice | solution.py:151
  137.0 0.0 copy-start.1
  137.0 20.9 %gather_fusion.1 = bf16[2048,2048]{1,0:T(8,128)(2,1)} fusion(bf16[2048,2048]{1,0:T(8,128)(2,1)} %slice.40, s32[2048]{0:T(1024)S(1)} %bitcast_clamp_fusion), kind=kCustom, calls=%fused_computation.1 | custom fusion | bytes 16785408 | tf_op jit(solution)/shard_map/gather | solution.py:182
  158.0 0.0 copy-done.1
  158.0 0.0 copy-start
  158.0 6.0 %fusion.15 = bf16[768,2048]{1,0:T(8,128)(2,1)S(1)} fusion(bf16[2048,2048]{1,0:T(8,128)(2,1)} %gather_fusion.1, bf16[2,1024,768]{2,1,0:T(8,128)(2,1)S(1)} %bitcast.60), kind=kOutput, calls=%fused_computation.28 | convolution fusion | flops 3222798336 | bytes 8912896 | tf_op jit(solution)/shard_map/sf,sd->fd/dot_general | solution.py:196
  164.0 0.0 copy-done
  164.0 3.9 %fusion.12 = bf16[768,2048]{1,0:T(8,128)(2,1)S(1)} fusion(bf16[2048,2048]{1,0:T(8,128)(2,1)S(1)} %copy-done, bf16[2,1024,768]{2,1,0:T(8,128)(2,1)S(1)} %bitcast.61), kind=kOutput, calls=%fused_computation.27 | convolution fusion | flops 3222798336 | bytes 8912896 | tf_op jit(solution)/shard_map/sf,sd->fd/dot_general | solution.py:196
  167.9 3.3 %pad_maximum_fusion = bf16[16,2,48,2048]{3,2,1,0:T(8,128)(2,1)} fusion(bf16[16,1,48,2048]{3,2,1,0:T(8,128)(2,1)S(1)} %bitcast.64, bf16[16,1,48,2048]{3,2,1,0:T(8,128)(2,1)S(1)} %bitcast.65), kind=kLoop, calls=%fused_computation.7 | loop fusion | flops 3145728 | bytes 12582912 | tf_op jit(solution)/shard_map/stack | solution.py:200
  171.2 0.0 reduce-scatter.2.cloned.1.call-update
  171.3 11.2 %fusion.29 = bf16[2,1024,16,48]{1,3,2,0:T(8,128)(2,1)S(1)} fusion(bf16[2,1024,2048,1]{2,1,3,0:T(8,128)(2,1)} %bitcast.59, bf16[16,2,48,2048]{3,2,1,0:T(8,128)(2,1)} %get-tuple-element.9), kind=kOutput, calls=%fused_computation.42 | convolution fusion | flops 6444023808 | bytes 17825792 | tf_op jit(solution)/shard_map/jsd,qjid->jsqi/dot_general | solution.py:184
  182.5 5.6 %copy.67 = bf16[1,2,1024,768]{3,1,0,2:T(2,128)(2,1)} copy(bf16[1,2,1024,768]{2,3,1,0:T(8,128)(2,1)S(1)} %bitcast.63) | data formatting | bytes 6291456 | tf_op jit(solution)/shard_map/reshape;reshape | solution.py:188
  188.1 3.9 %all-to-all-start = ((bf16[1,2,1024,768]{3,1,0,2:T(2,128)(2,1)}), bf16[1,2,1024,768]{3,1,0,2:T(2,128)(2,1)S(1)}, u32[]{:S(2)}, u32[]{:S(2)}) async-start(bf16[1,2,1024,768]{3,1,0,2:T(2,128)(2,1)} %copy.67), calls=%async_computation | async-start | bytes 6291456 | tf_op jit(solution)/shard_map/all_to_all | solution.py:187
  192.0 0.1 copy.70
  192.1 0.1 mul.112
  192.2 48.2 %all-to-all-done = bf16[1,2,1024,768]{3,1,0,2:T(2,128)(2,1)S(1)} async-done(((bf16[1,2,1024,768]{3,1,0,2:T(2,128)(2,1)}), bf16[1,2,1024,768]{3,1,0,2:T(2,128)(2,1)S(1)}, u32[]{:S(2)}, u32[]{:S(2)}) %all-to-all-start) | async-done | bytes 3145760 | tf_op jit(solution)/shard_map/all_to_all | solution.py:187
  240.4 0.4 copy.68
  240.8 0.2 copy.69
  241.0 5.2 %gather_fusion.2 = bf16[1024,768]{1,0:T(8,128)(2,1)} fusion(bf16[2048,768]{1,0:T(8,128)(2,1)S(1)} %bitcast.56, s32[1024]{0:T(1024)S(1)} %broadcast_clamp_fusion.1), kind=kCustom, calls=%fused_computation.2 | custom fusion | bytes 3149824 | tf_op jit(solution)/shard_map/gather | solution.py:202
  246.3 4.2 %fusion.22 = (bf16[128,8,768]{2,1,0:T(8,128)(2,1)S(1)}, bf16[128,8,768]{2,1,0:T(8,128)(2,1)S(1)}, f32[128,8]{1,0:T(8,128)S(1)}) fusion(bf16[1024,768]{1,0:T(8,128)(2,1)} %gather_fusion.2, f32[128,8]{1,0:T(8,128)S(1)} %copy.61, bf16[128,8,1536]{2,1,0:T(8,128)(2,1)} %param.6, bf16[128,8,768]{2,1,0:T(8,128)(2,1)} %get-tuple-element.21), kind=kLoop, calls=%fused_computation.33 | loop fusion | flops 15727616 | bytes 9445376 | tf_op jit(solution)/shard_map/convert.3
  250.5 0.7 copy.73
  251.2 1.9 pad_maximum_fusion.1
  253.1 0.0 reduce-scatter.2.cloned.1.call-done
  253.1 1.9 bitcast_convert_fusion
  (13 shorter events, 0.1 us)
Async XLA Ops:
  7.2 117.2 %all-gather.2.cloned.1.call-start = ((), (), s32[]{:S(2)}) async-start(), calls=%async_computation.2 | async-start | bytes 9469952 | tf_op jit(solution)/shard_map/all_gather | solution.py:147
  10.0 243.1 %reduce-scatter.2.cloned.1.call-start = ((), (), s32[]{:S(2)}) async-start(), calls=%async_computation.3 | async-start | bytes 6684672 | tf_op jit(solution)/shard_map/reduce_scatter | solution.py:200
  137.0 20.9 %copy-start.1 = (bf16[2,16,64,768]{3,2,1,0:T(8,128)(2,1)S(1)}, bf16[2,16,64,768]{3,2,1,0:T(8,128)(2,1)}, u32[]{:S(2)}) copy-start(bf16[2,16,64,768]{3,2,1,0:T(8,128)(2,1)} %copy.63) | copy-start | bytes 9437188
  158.0 6.0 %copy-start = (bf16[2048,2048]{1,0:T(8,128)(2,1)S(1)}, bf16[2048,2048]{1,0:T(8,128)(2,1)}, u32[]{:S(2)}) copy-start(bf16[2048,2048]{1,0:T(8,128)(2,1)} %gather_fusion.1) | copy-start | bytes 25165828
  188.1 52.3 %all-to-all-start = ((bf16[1,2,1024,768]{3,1,0,2:T(2,128)(2,1)}), bf16[1,2,1024,768]{3,1,0,2:T(2,128)(2,1)S(1)}, u32[]{:S(2)}, u32[]{:S(2)}) async-start(bf16[1,2,1024,768]{3,1,0,2:T(2,128)(2,1)} %copy.67), calls=%async_computation | async-start | bytes 6291456 | tf_op jit(solution)/shard_map/all_to_all | solution.py:187
Sparse Core Ops, SparseCore 0:
  11.0 113.3 all-gather.1
  171.4 61.7 reduce-scatter.1

commit v6 on v5

--- a/solution.py
+++ b/solution.py
@@ -22,8 +22,8 @@
     return z * 2 + jnp.where(lax.rem(z, 2) == 0, core, 1 - core)
 
 
-def exchange_kernel(replicas, owners, pieces, w_ref, h_ref, o_ref, g_ref, sems, send_sem, recv_sem,
-                    h_send_sem, h_recv_sem):
+def exchange_kernel(replicas, owners, pieces, w_ref, h_ref, t_ref, o_ref, g_ref, u_ref, sems, send_sem,
+                    recv_sem, h_send_sem, h_recv_sem, t_send_sem, t_recv_sem):
     me = lax.axis_index("dp")
     col = lax.axis_index("expert")
     pos = ring_pos(me)
@@ -39,23 +39,26 @@
         pl.semaphore_signal(barrier, inc=1, device_id=(me, other), device_id_type=MESH)
     pl.semaphore_wait(barrier, 2 + owners - 1)
 
-    own = pltpu.make_async_copy(w_ref, o_ref.at[me], sems.at[0])
+    own = pltpu.make_async_copy(w_ref, o_ref.at[:, me], sems.at[0])
     own.start()
     own_h = pltpu.make_async_copy(h_ref.at[col], g_ref.at[col], sems.at[1])
     own_h.start()
+    own_t = pltpu.make_async_copy(t_ref.at[col], u_ref.at[col], sems.at[2])
+    own_t.start()
     outgoing = []
     for peer in range(owners - 1):
         other = lax.rem(col + 1 + peer, owners)
-        copy = pltpu.make_async_remote_copy(
-            src_ref=h_ref.at[other],
-            dst_ref=g_ref.at[col],
-            send_sem=h_send_sem.at[other],
-            recv_sem=h_recv_sem.at[col],
-            device_id=(me, other),
-            device_id_type=MESH,
-        )
-        copy.start()
-        outgoing.append(copy)
+        for src, dst, ssem, rsem in ((h_ref, g_ref, h_send_sem, h_recv_sem), (t_ref, u_ref, t_send_sem, t_recv_sem)):
+            copy = pltpu.make_async_remote_copy(
+                src_ref=src.at[other],
+                dst_ref=dst.at[col],
+                send_sem=ssem.at[other],
+                recv_sem=rsem.at[col],
+                device_id=(me, other),
+                device_id_type=MESH,
+            )
+            copy.start()
+            outgoing.append(copy)
 
     hops = (replicas // 2, replicas - 1 - replicas // 2)
     for step in range(hops[0]):
@@ -66,10 +69,10 @@
             block = ring_dp(pos + sign * step, replicas)
             for piece in range(pieces):
                 part = pl.ds(piece * cols, cols)
-                src = w_ref.at[:, :, part] if step == 0 else o_ref.at[block, :, :, part]
+                src = w_ref.at[:, :, part] if step == 0 else o_ref.at[:, block, :, part]
                 copy = pltpu.make_async_remote_copy(
                     src_ref=src,
-                    dst_ref=o_ref.at[block, :, :, part],
+                    dst_ref=o_ref.at[:, block, :, part],
                     send_sem=send_sem.at[way, step, piece],
                     recv_sem=recv_sem.at[way, step, piece],
                     device_id=(target, col),
@@ -84,32 +87,38 @@
         copy.wait_send()
     for peer in range(owners - 1):
         source = lax.rem(col + 1 + peer, owners)
-        incoming = pltpu.make_async_remote_copy(
-            src_ref=h_ref.at[source],
-            dst_ref=g_ref.at[source],
-            send_sem=h_send_sem.at[source],
-            recv_sem=h_recv_sem.at[source],
-            device_id=(me, source),
-            device_id_type=MESH,
-        )
-        incoming.wait_recv()
+        for src, dst, ssem, rsem in ((h_ref, g_ref, h_send_sem, h_recv_sem), (t_ref, u_ref, t_send_sem, t_recv_sem)):
+            incoming = pltpu.make_async_remote_copy(
+                src_ref=src.at[source],
+                dst_ref=dst.at[source],
+                send_sem=ssem.at[source],
+                recv_sem=rsem.at[source],
+                device_id=(me, source),
+                device_id_type=MESH,
+            )
+            incoming.wait_recv()
     own.wait()
     own_h.wait()
-
-
-def exchange(w_down, h_send, replicas, owners, pieces=4):
+    own_t.wait()
+
+
+def exchange(w_down, h_send, t_send, replicas, owners, pieces=4):
+    local_experts, rows, width = w_down.shape
     return pl.pallas_call(
         lambda *refs: exchange_kernel(replicas, owners, pieces, *refs),
         out_shape=(
-            jax.ShapeDtypeStruct((replicas,) + w_down.shape, w_down.dtype),
+            jax.ShapeDtypeStruct((local_experts, replicas, rows, width), w_down.dtype),
             jax.ShapeDtypeStruct(h_send.shape, h_send.dtype),
-        ),
-        in_specs=[pl.BlockSpec(memory_space=pl.ANY)] * 2,
-        out_specs=(pl.BlockSpec(memory_space=pl.ANY), pl.BlockSpec(memory_space=pl.ANY)),
+            jax.ShapeDtypeStruct(t_send.shape, t_send.dtype),
+        ),
+        in_specs=[pl.BlockSpec(memory_space=pl.ANY)] * 3,
+        out_specs=(pl.BlockSpec(memory_space=pl.ANY),) * 3,
         scratch_shapes=[
-            pltpu.SemaphoreType.DMA((2,)),
+            pltpu.SemaphoreType.DMA((3,)),
             pltpu.SemaphoreType.DMA((2, replicas // 2, pieces)),
             pltpu.SemaphoreType.DMA((2, replicas // 2, pieces)),
+            pltpu.SemaphoreType.DMA((owners,)),
+            pltpu.SemaphoreType.DMA((owners,)),
             pltpu.SemaphoreType.DMA((owners,)),
             pltpu.SemaphoreType.DMA((owners,)),
         ],
@@ -119,7 +128,7 @@
             bytes_accessed=2 * replicas * w_down.size * 2 + 2 * h_send.size * 2,
             transcendentals=0,
         ),
-    )(w_down, h_send)
+    )(w_down, h_send, t_send)
 
 
 def slot_counts(ids, experts):
@@ -142,13 +151,7 @@
     capacity = min(tokens, 2 * tokens * top // experts)
     routes = tokens * top
 
-    lanes = 128
-    ids_cols = jnp.pad(route_ids.astype(jnp.bfloat16), ((0, 0), (0, lanes - top)))
-    cot_ext = lax.all_gather(
-        jnp.concatenate([cotangent, ids_cols], axis=1), "expert", axis=0, tiled=True
-    )
-    ids_group = cot_ext[:, width:width + top].astype(jnp.int32).reshape(owners, routes)
-    cot_group = cot_ext[:, :width]
+    cot_group = lax.all_gather(cotangent, "expert", axis=0, tiled=True)
 
     gate = saved_gate_up[:, :, :hidden_units].astype(jnp.float32)
     up = saved_gate_up[:, :, hidden_units:].astype(jnp.float32)
@@ -168,33 +171,26 @@
     h_rows = jnp.where(filled[:, None], scaled.reshape(routes, hidden_units)[route_of_slot], jnp.zeros((), jnp.bfloat16))
     h_send = h_rows.reshape(owners, local_experts, capacity, hidden_units)
 
-    slot_all = slot_counts(ids_group, experts)
-    mine = me * local_experts + jnp.arange(local_experts, dtype=jnp.int32)
-    pos_all = ids_group * capacity + slot_all
-    want = (mine[:, None] * capacity + jnp.arange(capacity, dtype=jnp.int32)[None, :]).reshape(-1)
-    hit = pos_all[:, None, :] == want[None, :, None]
-    token_of = jnp.sum(jnp.where(hit, (jnp.arange(routes, dtype=jnp.int32) // top)[None, None, :], 0), axis=2)
-    rows = (jnp.arange(owners, dtype=jnp.int32)[:, None] * tokens + token_of).reshape(owners, local_experts, capacity)
-    rows = jnp.transpose(rows, (1, 0, 2)).reshape(local_experts, owners * capacity)
-    full_down, h_got = exchange(w_down, h_send, replicas, owners)
-    h_recv = jnp.transpose(h_got, (1, 0, 2, 3)).reshape(local_experts, owners * capacity, hidden_units)
-    h_recv, cot_group = lax.optimization_barrier((h_recv, cot_group))
-    dy_recv = cot_group[rows]
+    t_send = jnp.where(filled, route_of_slot // top, -1).reshape(owners, 1, local_experts * capacity)
+    full_down, h_got, t_got = exchange(w_down, h_send, t_send, replicas, owners)
+    h_got, t_got, cot_group = lax.optimization_barrier((h_got, t_got, cot_group))
+    pick = (t_got.reshape(owners, local_experts * capacity, 1)
+            == jnp.arange(tokens, dtype=jnp.int32)[None, None, :]).astype(jnp.bfloat16)
+    dy = jnp.einsum(
+        "sct,std->scd", pick, cot_group.reshape(owners, tokens, width),
+        preferred_element_type=jnp.bfloat16,
+    ).reshape(owners, local_experts, capacity, width)
 
     grads = jnp.einsum(
-        "jsd,qjid->jsqi", dy_recv, full_down, preferred_element_type=jnp.float32
-    ).astype(jnp.bfloat16).reshape(local_experts, owners * capacity, hidden_units)
-    back = lax.all_to_all(
-        grads.reshape(1, local_experts, owners * capacity, hidden_units),
-        "expert",
-        split_axis=2,
-        concat_axis=0,
-        tiled=True,
-    )
+        "sjcd,jfd->sjcf", dy, full_down.reshape(local_experts, hidden_units, width),
+        preferred_element_type=jnp.float32,
+    ).astype(jnp.bfloat16)
+    grads, dy, h_got = lax.optimization_barrier((grads, dy, h_got))
+    back = lax.all_to_all(grads, "expert", split_axis=0, concat_axis=0, tiled=True)
     parts = []
     for j in range(local_experts):
         part = jnp.einsum(
-            "sf,sd->fd", h_recv[j], dy_recv[j], preferred_element_type=jnp.float32
+            "scf,scd->fd", h_got[:, j], dy[:, j], preferred_element_type=jnp.float32
         ).astype(jnp.bfloat16)
         parts.append(part.reshape(replicas, hidden_units // replicas, width))
     summed = lax.psum_scatter(jnp.stack(parts, axis=1), "dp", scatter_dimension=0, tiled=True)

time: 264 us -> 231 us (0.88)
  local copies, waits for them, and re-layouts: 57.5 us -> 19.1 us
  matrix products: 23.1 us -> 29.9 us
  starting transfers between devices: 3.94 us -> 9.55 us
  other arithmetic: 25.2 us -> 21 us
    gather x1 -> x0, local copies, waits for them, and re-layouts: 20.9 us -> none  [local(): dy_recv = cot_group[rows]]
    slice x1 -> x0, local copies, waits for them, and re-layouts: 8.27 us -> none  [local(): cot_group = cot_ext[:, :width]]
    dot_general x3 -> x4, matrix products: 21.2 us -> 29.4 us  [the longest x1 11.1 us: local(): jnp.einsum('sjcd,jfd->sjcf', dy, full_down.reshape(local_experts, hidden_...]
    another operation x1 -> x0, local copies, waits for them, and re-layouts: 5.64 us -> none  [local(): grads.reshape(1, local_experts, owners * capacity, hidden_units)]
    all_to_all x1, starting transfers between devices: 3.86 us -> 9.47 us  [local(): lax.all_to_all(grads, 'expert', split_axis=0, concat_axis=0, tiled=True)]
    transpose x2 -> x0, local copies, waits for them, and re-layouts: 3.92 us -> none  [the longest x1 3.91 us: local(): jnp.transpose(h_got, (1, 0, 2, 3))]
    all_gather x1, waiting for transfers between devices: 21.8 us -> 19.1 us  [local(): cot_group = lax.all_gather(cotangent, 'expert', axis=0, tiled=True)]
  transfers between devices with their start and end apart: 3 -> 3, of which waited for: 2 -> 2; matrix products, arithmetic and copies ran while one was open for 21% -> 15% of each run, Pallas kernels for 26% -> 30%
where the time goes in v6:
time: 231 us
  Pallas kernels  69.6 us (30%)
  waiting for transfers between devices  67.6 us (29%)
  matrix products  29.9 us (13%)
  other arithmetic  21 us (9%)
  local copies, waits for them, and re-layouts  19.1 us (8%)
  between operations  14.2 us (6%)
  starting transfers between devices  9.55 us (4%)
    pallas_call x1, Pallas kernels, exchange(): pl.pallas_call(lambda *refs: exchange_kernel(replicas, owners, pieces, *r...  69.6 us
    all_to_all x1, waiting for transfers between devices, local(): lax.all_to_all(grads, 'expert', split_axis=0, concat_axis=0, tiled=True)  47.8 us
    all_gather x1, waiting for transfers between devices, local(): cot_group = lax.all_gather(cotangent, 'expert', axis=0, tiled=True)  19.1 us
    dot_general x1, matrix products, local(): jnp.einsum('sjcd,jfd->sjcf', dy, full_down.reshape(local_experts, hidden_...  11.1 us
    dot_general x2, matrix products, local(): jnp.einsum('scf,scd->fd', h_got[:, j], dy[:, j], preferred_element_type=j...  10.2 us
    all_to_all x1, starting transfers between devices, local(): lax.all_to_all(grads, 'expert', split_axis=0, concat_axis=0, tiled=True)  9.47 us
    gather x1, local copies, waits for them, and re-layouts, local(): scaled.reshape(routes, hidden_units)[route_of_slot]  9.4 us
    dot_general x1, matrix products, local(): jnp.einsum('sct,std->scd', pick, cot_group.reshape(owners, tokens, width)...  8.06 us
  transfers between devices with their start and end apart: 3, of which 2 were waited for; matrix products, arithmetic and copies ran while one was open for 15% of the time, Pallas kernels for 30%

profile of v6, /device:TPU:64, one launch (start us, length us, event | category | flops | bytes accessed | tf_op | source)
XLA Modules:
  0.0 231.0 jit_solution(15655780218111324165)
XLA Ops:
  7.2 0.0 all-gather.2.cloned.1.call-start
  7.2 0.7 all-gather.2.cloned.1.call-update
  7.9 0.0 reduce-scatter.2.cloned.1.call-start
  7.9 0.8 copy.35
  8.7 0.8 copy.36
  9.5 0.1 reshape.176
  9.6 0.5 fusion.26
  10.2 1.0 fusion.2
  11.2 0.1 broadcast_in_dim.28
  11.3 0.9 select_reduce_fusion
  12.2 3.6 %fusion.20 = (bf16[1024,768]{1,0:T(8,128)(2,1)S(1)}, bf16[128,8,768]{2,1,0:T(8,128)(2,1)}) fusion(f32[128,8]{1,0:T(8,128)S(1)} %copy.35, bf16[128,8,1536]{2,1,0:T(8,128)(2,1)} %param.6), kind=kLoop, calls=%fused_computation.39 | loop fusion | flops 8650752 | bytes 6295552 | tf_op jit(solution)/shard_map/reshape | solution.py:171
  15.8 9.4 %gather_fusion = bf16[2048,768]{1,0:T(8,128)(2,1)} fusion(bf16[1024,768]{1,0:T(8,128)(2,1)S(1)} %get-tuple-element.27, s32[2048]{0:T(1024)S(1)} %broadcast_clamp_fusion), kind=kCustom, calls=%fused_computation | custom fusion | bytes 6299648 | tf_op jit(solution)/shard_map/gather | solution.py:171
  25.2 0.6 copy_select_fusion.refs_2_
  25.9 3.4 %broadcast_select_fusion.refs_1_ = bf16[16,2,64,768]{3,2,1,0:T(8,128)(2,1)} fusion(bf16[16,2,64,768]{3,2,1,0:T(8,128)(2,1)} %bitcast.63, pred[16,2,64]{2,1,0:T(4,128)(4,1)S(1)} %broadcast_in_dim.28), kind=kLoop, calls=%fused_computation.38 | loop fusion | flops 1572864 | bytes 6293504 | tf_op jit(solution)/shard_map/jit(_where)/select_n | solution.py:171
  29.3 69.6 %shard_map.76 = (bf16[2,16,48,2048]{3,2,1,0:T(8,128)(2,1)}, bf16[16,2,64,768]{3,2,1,0:T(8,128)(2,1)}, s32[16,1,128]{2,1,0:T(1,128)}) custom-call(bf16[2,48,2048]{2,1,0:T(8,128)(2,1)} %refs_0_.1, bf16[16,2,64,768]{3,2,1,0:T(8,128)(2,1)} %broadcast_select_fusion.refs_1_, s32[16,1,128]{2,1,0:T(1,128)} %copy_select_fusion.refs_2_), custom_call_target="tpu_custom_call" | custom-call | bytes 18874368 | tf_op jit(solution)/shard_map/pallas_call | solution.py:107
  98.9 19.1 %all-gather.2.cloned.1.call-done = bf16[2048,2048]{1,0:T(8,128)(2,1)} async-done(((bf16[128,2048]{1,0:T(8,128)(2,1)}), bf16[2048,2048]{1,0:T(8,128)(2,1)}) %all-gather.2.cloned.1.call-update) | async-done | bytes 8388624 | tf_op jit(solution)/shard_map/all_gather | solution.py:154
  118.0 8.1 %fusion.27 = bf16[16,128,2048]{2,1,0:T(8,128)(2,1)} fusion(bf16[16,128,2048]{2,1,0:T(8,128)(2,1)} %bitcast.57, s32[16,128]{1,0:T(8,128)} %bitcast.66), kind=kOutput, calls=%fused_computation.47 | convolution fusion | flops 1074003968 | bytes 16785408 | tf_op jit(solution)/shard_map/sct,std->scd/dot_general | solution.py:179
  126.1 0.0 slice-start
  126.1 11.1 %convert_bitcast_fusion = bf16[16,2,64,768]{3,2,0,1:T(8,128)(2,1)S(1)} fusion(bf16[2,768,2048,1]{2,1,3,0:T(8,128)(2,1)} %bitcast.73, bf16[16,2,64,2048]{3,2,1,0:T(8,128)(2,1)} %bitcast.58), kind=kOutput, calls=%fused_computation.37 | convolution fusion | flops 6444023808 | bytes 17825792 | tf_op jit(solution)/shard_map/sjcd,jfd->sjcf/dot_general | solution.py:184
  137.2 0.0 slice-start.1
  137.2 0.0 copy-start.1
  137.2 6.3 %bitcast_convert_fusion = bf16[768,2048]{1,0:T(8,128)(2,1)S(1)} fusion(bf16[16,2,64,768]{3,2,1,0:T(8,128)(2,1)} %get-tuple-element.19, bf16[16,2,64,2048]{3,2,1,0:T(8,128)(2,1)} %bitcast.59), kind=kOutput, calls=%fused_computation.8 | convolution fusion | flops 3222798336 | bytes 8912896 | tf_op jit(solution)/shard_map/scf,scd->fd/dot_general | solution.py:192
  143.5 0.0 slice-done
  143.5 0.0 slice-done.1
  143.5 0.0 copy-done.1
  143.6 3.9 %bitcast_convert_fusion.1 = bf16[768,2048]{1,0:T(8,128)(2,1)S(1)} fusion(bf16[16,2,64,768]{3,2,1,0:T(8,128)(2,1)S(1)} %copy-done.1, bf16[16,2,64,2048]{3,2,1,0:T(8,128)(2,1)S(1)} %bitcast.62), kind=kOutput, calls=%fused_computation.9 | convolution fusion | flops 3222798336 | bytes 8912896 | tf_op jit(solution)/shard_map/scf,scd->fd/dot_general | solution.py:192
  147.5 3.2 %pad_maximum_fusion = bf16[16,2,48,2048]{3,2,1,0:T(8,128)(2,1)} fusion(bf16[16,1,48,2048]{3,2,1,0:T(8,128)(2,1)S(1)} %bitcast.64, bf16[16,1,48,2048]{3,2,1,0:T(8,128)(2,1)S(1)} %bitcast.65), kind=kLoop, calls=%fused_computation.7 | loop fusion | flops 3145728 | bytes 12582912 | tf_op jit(solution)/shard_map/stack | solution.py:196
  150.7 0.0 reduce-scatter.2.cloned.1.call-update
  150.7 1.9 copy.39
  152.6 0.0 copy-start
  152.6 9.5 %all-to-all-start = ((bf16[16,2,64,768]{3,2,1,0:T(8,128)(2,1)}), bf16[16,2,64,768]{3,2,1,0:T(8,128)(2,1)S(1)}, u32[]{:S(2)}, u32[]{:S(2)}) async-start(bf16[16,2,64,768]{3,2,1,0:T(8,128)(2,1)} %copy.39), calls=%async_computation | async-start | bytes 6291456 | tf_op jit(solution)/shard_map/all_to_all | solution.py:189
  162.1 0.0 copy-done
  162.1 0.1 copy.40
  162.2 0.1 mul.74
  162.4 47.8 %all-to-all-done = bf16[16,2,64,768]{3,2,1,0:T(8,128)(2,1)S(1)} async-done(((bf16[16,2,64,768]{3,2,1,0:T(8,128)(2,1)}), bf16[16,2,64,768]{3,2,1,0:T(8,128)(2,1)S(1)}, u32[]{:S(2)}, u32[]{:S(2)}) %all-to-all-start) | async-done | bytes 3145760 | tf_op jit(solution)/shard_map/all_to_all | solution.py:189
  210.2 5.2 %gather_fusion.1 = bf16[1024,768]{1,0:T(8,128)(2,1)} fusion(bf16[2048,768]{1,0:T(8,128)(2,1)S(1)} %bitcast.56, s32[1024]{0:T(1024)S(1)} %broadcast_clamp_fusion.1), kind=kCustom, calls=%fused_computation.1 | custom fusion | bytes 3149824 | tf_op jit(solution)/shard_map/gather | solution.py:198
  215.4 4.2 %fusion.11 = (bf16[128,8,768]{2,1,0:T(8,128)(2,1)S(1)}, bf16[128,8,768]{2,1,0:T(8,128)(2,1)S(1)}, f32[128,8]{1,0:T(8,128)S(1)}) fusion(bf16[1024,768]{1,0:T(8,128)(2,1)} %gather_fusion.1, f32[128,8]{1,0:T(8,128)S(1)} %copy.35, bf16[128,8,1536]{2,1,0:T(8,128)(2,1)} %param.6, bf16[128,8,768]{2,1,0:T(8,128)(2,1)} %get-tuple-element.28), kind=kLoop, calls=%fused_computation.29 | loop fusion | flops 15727616 | bytes 9445376 | tf_op jit(solution)/shard_map/convert.2
  219.7 0.7 copy.45
  220.3 1.9 pad_maximum_fusion.1
  222.2 0.0 reduce-scatter.2.cloned.1.call-done
  222.2 1.9 bitcast_convert_fusion.2
  (8 shorter events, 0.0 us)
Async XLA Ops:
  7.2 110.9 %all-gather.2.cloned.1.call-start = ((), (), s32[]{:S(2)}) async-start(), calls=%async_computation.2 | async-start | bytes 8912896 | tf_op jit(solution)/shard_map/all_gather | solution.py:154
  7.9 214.3 %reduce-scatter.2.cloned.1.call-start = ((), (), s32[]{:S(2)}) async-start(), calls=%async_computation.3 | async-start | bytes 6684672 | tf_op jit(solution)/shard_map/reduce_scatter | solution.py:196
  126.1 17.4 %slice-start = ((s8[8388608]{0:T(1024)(128)(4,1)}), s8[4194304]{0:T(1024)(128)(4,1)S(1)}, s32[]{:S(2)}) async-start(s8[8388608]{0:T(1024)(128)(4,1)} %bitcast.60), calls=%async_computation.4 | async-start | bytes 8388608
  137.2 6.3 %slice-start.1 = ((s8[8388608]{0:T(1024)(128)(4,1)}), s8[4194304]{0:T(1024)(128)(4,1)S(1)}, s32[]{:S(2)}) async-start(s8[8388608]{0:T(1024)(128)(4,1)} %bitcast.60), calls=%async_computation.5 | async-start | bytes 8388608
  137.2 6.3 %copy-start.1 = (bf16[16,2,64,768]{3,2,1,0:T(8,128)(2,1)S(1)}, bf16[16,2,64,768]{3,2,1,0:T(8,128)(2,1)}, u32[]{:S(2)}) copy-start(bf16[16,2,64,768]{3,2,1,0:T(8,128)(2,1)} %get-tuple-element.19) | copy-start | bytes 9437188
  152.6 9.5 %copy-start = (s32[128,8]{0,1:T(8,128)S(1)}, s32[128,8]{0,1:T(8,128)}, u32[]{:S(2)}) copy-start(s32[128,8]{0,1:T(8,128)} %param.7) | copy-start | bytes 12292
  152.6 57.6 %all-to-all-start = ((bf16[16,2,64,768]{3,2,1,0:T(8,128)(2,1)}), bf16[16,2,64,768]{3,2,1,0:T(8,128)(2,1)S(1)}, u32[]{:S(2)}, u32[]{:S(2)}) async-start(bf16[16,2,64,768]{3,2,1,0:T(8,128)(2,1)} %copy.39), calls=%async_computation | async-start | bytes 6291456 | tf_op jit(solution)/shard_map/all_to_all | solution.py:189
Sparse Core Ops, SparseCore 0:
  10.4 107.5 all-gather.1
  150.9 64.0 reduce-scatter.1

commit v7 on v6

--- a/solution.py
+++ b/solution.py
@@ -131,6 +131,81 @@
     )(w_down, h_send, t_send)
 
 
+def return_kernel(owners, dy_ref, w_ref, back_ref, gbuf, own_sem, send_sem, recv_sem):
+    me = lax.axis_index("dp")
+    col = lax.axis_index("expert")
+
+    barrier = pltpu.get_barrier_semaphore()
+    for peer in range(owners - 1):
+        other = lax.rem(col + 1 + peer, owners)
+        pl.semaphore_signal(barrier, inc=1, device_id=(me, other), device_id_type=MESH)
+    pl.semaphore_wait(barrier, owners - 1)
+
+    def send(source):
+        return pltpu.make_async_remote_copy(
+            src_ref=gbuf.at[source],
+            dst_ref=back_ref.at[col],
+            send_sem=send_sem.at[source],
+            recv_sem=recv_sem.at[col],
+            device_id=(me, source),
+            device_id_type=MESH,
+        )
+
+    previous = None
+    for step in range(owners):
+        source = lax.rem(col + 1 + step, owners)
+        for j in range(w_ref.shape[0]):
+            gbuf[source, j] = lax.dot_general(
+                dy_ref[source, j], w_ref[j], (((1,), (1,)), ((), ())),
+                preferred_element_type=jnp.float32,
+            ).astype(gbuf.dtype)
+        if previous is not None:
+            send(previous).start()
+        previous = source
+    own = pltpu.make_async_copy(gbuf.at[col], back_ref.at[col], own_sem)
+    own.start()
+
+    for peer in range(owners - 1):
+        send(lax.rem(col + 1 + peer, owners)).wait_send()
+    for peer in range(owners - 1):
+        source = lax.rem(col + 1 + peer, owners)
+        pltpu.make_async_remote_copy(
+            src_ref=gbuf.at[source],
+            dst_ref=back_ref.at[source],
+            send_sem=send_sem.at[source],
+            recv_sem=recv_sem.at[source],
+            device_id=(me, source),
+            device_id_type=MESH,
+        ).wait_recv()
+    own.wait()
+
+
+def give_back(dy, full_down, owners):
+    sources, local_experts, capacity, width = dy.shape
+    hidden_units = full_down.shape[1]
+    shape = (sources, local_experts, capacity, hidden_units)
+    return pl.pallas_call(
+        lambda *refs: return_kernel(owners, *refs),
+        out_shape=jax.ShapeDtypeStruct(shape, dy.dtype),
+        in_specs=[pl.BlockSpec(memory_space=pltpu.VMEM)] * 2,
+        out_specs=pl.BlockSpec(memory_space=pl.ANY),
+        scratch_shapes=[
+            pltpu.VMEM(shape, dy.dtype),
+            pltpu.SemaphoreType.DMA(()),
+            pltpu.SemaphoreType.DMA((owners,)),
+            pltpu.SemaphoreType.DMA((owners,)),
+        ],
+        compiler_params=pltpu.CompilerParams(
+            collective_id=1, has_side_effects=True, vmem_limit_bytes=48 * 1024 * 1024
+        ),
+        cost_estimate=pl.CostEstimate(
+            flops=2 * sources * local_experts * capacity * width * hidden_units,
+            bytes_accessed=(dy.size + full_down.size + 2 * sources * local_experts * capacity * hidden_units) * 2,
+            transcendentals=0,
+        ),
+    )(dy, full_down)
+
+
 def slot_counts(ids, experts):
     routes = ids.shape[-1]
     onehot = (ids[..., None] == jnp.arange(experts, dtype=jnp.int32)).astype(jnp.bfloat16)
@@ -181,20 +256,17 @@
         preferred_element_type=jnp.bfloat16,
     ).reshape(owners, local_experts, capacity, width)
 
-    grads = jnp.einsum(
-        "sjcd,jfd->sjcf", dy, full_down.reshape(local_experts, hidden_units, width),
-        preferred_element_type=jnp.float32,
-    ).astype(jnp.bfloat16)
-    grads, dy, h_got = lax.optimization_barrier((grads, dy, h_got))
-    back = lax.all_to_all(grads, "expert", split_axis=0, concat_axis=0, tiled=True)
     parts = []
     for j in range(local_experts):
         part = jnp.einsum(
             "scf,scd->fd", h_got[:, j], dy[:, j], preferred_element_type=jnp.float32
         ).astype(jnp.bfloat16)
         parts.append(part.reshape(replicas, hidden_units // replicas, width))
-    summed = lax.psum_scatter(jnp.stack(parts, axis=1), "dp", scatter_dimension=0, tiled=True)
+    stacked = jnp.stack(parts, axis=1)
+    stacked, dy = lax.optimization_barrier((stacked, dy))
+    summed = lax.psum_scatter(stacked, "dp", scatter_dimension=0, tiled=True)
     grad_down = summed[0].astype(jnp.float32)
+    back = give_back(dy, full_down.reshape(local_experts, hidden_units, width), owners)
     returned_rows = back.reshape(experts * capacity, hidden_units)[position]
     qf = returned_rows.reshape(tokens, top, hidden_units).astype(jnp.float32)
     route_grad = jnp.sum(qf * hidden.astype(jnp.float32), -1)

time: 231 us -> 225 us (0.974); the launches traced: 231 us -> 222 us
  Pallas kernels: 69.6 us -> 134 us
  waiting for transfers between devices: 67.6 us -> 21.2 us
  matrix products: 29.9 us -> 14.4 us
  starting transfers between devices: 9.55 us -> 0.08 us
    pallas_call x0 -> x1, Pallas kernels: none -> 65.2 us  [give_back(): pl.pallas_call(lambda *refs: return_kernel(owners, *refs), out_shape=jax....]
    all_to_all x1 -> x0, waiting for transfers between devices: 47.8 us -> none  [local(): lax.all_to_all(grads, 'expert', split_axis=0, concat_axis=0, tiled=True)]
    dot_general x1 -> x0, matrix products: 11.1 us -> none  [local(): jnp.einsum('sjcd,jfd->sjcf', dy, full_down.reshape(local_experts, hidden_...]
    all_to_all x1 -> x0, starting transfers between devices: 9.47 us -> none  [local(): lax.all_to_all(grads, 'expert', split_axis=0, concat_axis=0, tiled=True)]
    dot_general x2, matrix products: 10.2 us -> 7.64 us  [local(): jnp.einsum('scf,scd->fd', h_got[:, j], dy[:, j], preferred_element_type=j...]
  transfers between devices with their start and end apart: 3 -> 2, of which waited for: 2 -> 1; matrix products, arithmetic and copies ran while one was open for 15% -> 15% of each run, Pallas kernels for 30% -> 60%
where the time goes in v7:
time: 225 us; the launch traced here: 222 us
  Pallas kernels  134 us (60%)
  waiting for transfers between devices  21.2 us (9%)
  other arithmetic  20.7 us (9%)
  local copies, waits for them, and re-layouts  17.9 us (8%)
  matrix products  14.4 us (6%)
  between operations  14.2 us (6%)
    pallas_call x1, Pallas kernels, exchange(): pl.pallas_call(lambda *refs: exchange_kernel(replicas, owners, pieces, *r...  68.3 us
    pallas_call x1, Pallas kernels, give_back(): pl.pallas_call(lambda *refs: return_kernel(owners, *refs), out_shape=jax....  65.2 us
    all_gather x1, waiting for transfers between devices, local(): cot_group = lax.all_gather(cotangent, 'expert', axis=0, tiled=True)  20.5 us
    gather x1, local copies, waits for them, and re-layouts, local(): scaled.reshape(routes, hidden_units)[route_of_slot]  9.4 us
    dot_general x2, matrix products, local(): jnp.einsum('scf,scd->fd', h_got[:, j], dy[:, j], preferred_element_type=j...  7.64 us
    dot_general x1, matrix products, local(): jnp.einsum('sct,std->scd', pick, cot_group.reshape(owners, tokens, width)...  6.24 us
    gather x1, local copies, waits for them, and re-layouts, local(): returned_rows = back.reshape(experts * capacity, hidden_units)[position]  5.21 us
  transfers between devices with their start and end apart: 2, of which 1 were waited for; matrix products, arithmetic and copies ran while one was open for 15% of the time, Pallas kernels for 60%

profile of v7, /device:TPU:64, one launch (start us, length us, event | category | flops | bytes accessed | tf_op | source)
XLA Modules:
  0.0 222.0 jit_solution(12150534198145852812)
XLA Ops:
  7.2 0.0 all-gather.2.cloned.1.call-start
  7.2 0.7 all-gather.2.cloned.1.call-update
  7.9 0.0 reduce-scatter.2.cloned.1.call-start
  7.9 0.8 copy.24
  8.7 0.8 copy.25
  9.5 0.1 reshape.176
  9.6 0.5 fusion.22
  10.2 1.0 fusion
  11.2 0.1 broadcast_in_dim.28
  11.3 0.9 select_reduce_fusion
  12.2 3.4 %fusion.16 = (bf16[1024,768]{1,0:T(8,128)(2,1)S(1)}, bf16[128,8,768]{2,1,0:T(8,128)(2,1)}) fusion(f32[128,8]{1,0:T(8,128)S(1)} %copy.24, bf16[128,8,1536]{2,1,0:T(8,128)(2,1)} %param.6), kind=kLoop, calls=%fused_computation.36 | loop fusion | flops 8650752 | bytes 6295552 | tf_op jit(solution)/shard_map/reshape | solution.py:246
  15.7 9.4 %gather_fusion = bf16[2048,768]{1,0:T(8,128)(2,1)} fusion(bf16[1024,768]{1,0:T(8,128)(2,1)S(1)} %get-tuple-element.25, s32[2048]{0:T(1024)S(1)} %broadcast_clamp_fusion), kind=kCustom, calls=%fused_computation | custom fusion | bytes 6299648 | tf_op jit(solution)/shard_map/gather | solution.py:246
  25.0 0.6 copy_select_fusion.refs_2_
  25.7 3.4 %broadcast_select_fusion.refs_1_ = bf16[16,2,64,768]{3,2,1,0:T(8,128)(2,1)} fusion(bf16[16,2,64,768]{3,2,1,0:T(8,128)(2,1)} %bitcast.54, pred[16,2,64]{2,1,0:T(4,128)(4,1)S(1)} %broadcast_in_dim.28), kind=kLoop, calls=%fused_computation.35 | loop fusion | flops 1572864 | bytes 6293504 | tf_op jit(solution)/shard_map/jit(_where)/select_n | solution.py:246
  29.1 68.3 %shard_map.76 = (bf16[2,16,48,2048]{3,2,1,0:T(8,128)(2,1)}, bf16[16,2,64,768]{3,2,1,0:T(8,128)(2,1)}, s32[16,1,128]{2,1,0:T(1,128)}) custom-call(bf16[2,48,2048]{2,1,0:T(8,128)(2,1)} %refs_0_.1, bf16[16,2,64,768]{3,2,1,0:T(8,128)(2,1)} %broadcast_select_fusion.refs_1_, s32[16,1,128]{2,1,0:T(1,128)} %copy_select_fusion.refs_2_), custom_call_target="tpu_custom_call" | custom-call | bytes 18874368 | tf_op jit(solution)/shard_map/pallas_call | solution.py:107
  97.5 20.5 %all-gather.2.cloned.1.call-done = bf16[2048,2048]{1,0:T(8,128)(2,1)} async-done(((bf16[128,2048]{1,0:T(8,128)(2,1)}), bf16[2048,2048]{1,0:T(8,128)(2,1)}) %all-gather.2.cloned.1.call-update) | async-done | bytes 8388624 | tf_op jit(solution)/shard_map/all_gather | solution.py:229
  118.0 0.0 copy-start.2
  118.0 6.2 %fusion.23 = bf16[16,128,2048]{2,1,0:T(8,128)(2,1)S(1)} fusion(bf16[16,128,2048]{2,1,0:T(8,128)(2,1)} %bitcast.50, s32[16,128]{1,0:T(8,128)} %bitcast.57), kind=kOutput, calls=%fused_computation.44 | convolution fusion | flops 1074003968 | bytes 16785408 | tf_op jit(solution)/shard_map/sct,std->scd/dot_general | solution.py:254
  124.3 0.0 copy-start
  124.3 0.0 copy-done.2
  124.3 3.7 %bitcast_convert_fusion = bf16[768,2048]{1,0:T(8,128)(2,1)S(1)} fusion(bf16[16,2,64,2048]{3,2,1,0:T(8,128)(2,1)S(1)} %bitcast.51, bf16[16,2,64,768]{3,2,1,0:T(8,128)(2,1)S(1)} %copy-done.2), kind=kOutput, calls=%fused_computation.6 | convolution fusion | flops 3222798336 | bytes 8912896 | tf_op jit(solution)/shard_map/scf,scd->fd/dot_general | solution.py:261
  128.0 0.0 copy-done
  128.0 3.9 %bitcast_convert_fusion.1 = bf16[768,2048]{1,0:T(8,128)(2,1)S(1)} fusion(bf16[16,2,64,2048]{3,2,1,0:T(8,128)(2,1)S(1)} %bitcast.52, bf16[16,2,64,768]{3,2,1,0:T(8,128)(2,1)S(1)} %copy-done.2), kind=kOutput, calls=%fused_computation.7 | convolution fusion | flops 3222798336 | bytes 8912896 | tf_op jit(solution)/shard_map/scf,scd->fd/dot_general | solution.py:261
  131.9 3.1 %pad_maximum_fusion = bf16[16,2,48,2048]{3,2,1,0:T(8,128)(2,1)} fusion(bf16[16,1,48,2048]{3,2,1,0:T(8,128)(2,1)S(1)} %bitcast.55, bf16[16,1,48,2048]{3,2,1,0:T(8,128)(2,1)S(1)} %bitcast.56), kind=kLoop, calls=%fused_computation.5 | loop fusion | flops 3145728 | bytes 12582912 | tf_op jit(solution)/shard_map/stack | solution.py:265
  135.1 0.0 copy-start.1
  135.1 0.0 reduce-scatter.2.cloned.1.call-update
  135.1 0.6 copy-done.1
  135.8 0.1 copy.29
  135.9 0.1 mul.74
  136.0 65.2 %shard_map.77 = bf16[16,2,64,768]{3,2,1,0:T(8,128)(2,1)S(1)} custom-call(bf16[16,2,64,2048]{3,2,1,0:T(8,128)(2,1)} %bitcast.53, bf16[2,768,2048]{2,1,0:T(8,128)(2,1)} %bitcast.64), custom_call_target="tpu_custom_call" | custom-call | flops 6442450944 | bytes 20971520 | tf_op jit(solution)/shard_map/pallas_call | solution.py:187
  201.2 5.2 %gather_fusion.1 = bf16[1024,768]{1,0:T(8,128)(2,1)} fusion(bf16[2048,768]{1,0:T(8,128)(2,1)S(1)} %bitcast.49, s32[1024]{0:T(1024)S(1)} %broadcast_clamp_fusion.1), kind=kCustom, calls=%fused_computation.1 | custom fusion | bytes 3149824 | tf_op jit(solution)/shard_map/gather | solution.py:270
  206.4 4.2 %fusion.9 = (bf16[128,8,768]{2,1,0:T(8,128)(2,1)S(1)}, bf16[128,8,768]{2,1,0:T(8,128)(2,1)S(1)}, f32[128,8]{1,0:T(8,128)S(1)}) fusion(bf16[1024,768]{1,0:T(8,128)(2,1)} %gather_fusion.1, f32[128,8]{1,0:T(8,128)S(1)} %copy.24, bf16[128,8,1536]{2,1,0:T(8,128)(2,1)} %param.6, bf16[128,8,768]{2,1,0:T(8,128)(2,1)} %get-tuple-element.26), kind=kLoop, calls=%fused_computation.27 | loop fusion | flops 15727616 | bytes 9445376 | tf_op jit(solution)/shard_map/convert.2
  210.7 0.7 copy.30
  211.4 1.9 pad_maximum_fusion.1
  213.3 0.0 reduce-scatter.2.cloned.1.call-done
  213.3 1.9 bitcast_convert_fusion.2
  (7 shorter events, 0.0 us)
Async XLA Ops:
  7.2 110.8 %all-gather.2.cloned.1.call-start = ((), (), s32[]{:S(2)}) async-start(), calls=%async_computation.1 | async-start | bytes 8912896 | tf_op jit(solution)/shard_map/all_gather | solution.py:229
  7.9 205.4 %reduce-scatter.2.cloned.1.call-start = ((), (), s32[]{:S(2)}) async-start(), calls=%async_computation.2 | async-start | bytes 6684672 | tf_op jit(solution)/shard_map/reduce_scatter | solution.py:267
  118.0 6.3 %copy-start.2 = (bf16[16,2,64,768]{3,2,1,0:T(8,128)(2,1)S(1)}, bf16[16,2,64,768]{3,2,1,0:T(8,128)(2,1)}, u32[]{:S(2)}) copy-start(bf16[16,2,64,768]{3,2,1,0:T(8,128)(2,1)} %get-tuple-element.13) | copy-start | bytes 9437188
  124.3 3.8 %copy-start = (bf16[16,128,2048]{2,1,0:T(8,128)(2,1)}, bf16[16,128,2048]{2,1,0:T(8,128)(2,1)S(1)}, u32[]{:S(2)}) copy-start(bf16[16,128,2048]{2,1,0:T(8,128)(2,1)S(1)} %fusion.23) | copy-start | bytes 25165828
  135.1 0.7 copy-start.1
Sparse Core Ops, SparseCore 0:
  10.4 107.5 all-gather.1
  135.2 63.7 reduce-scatter.1

commit v8 on v7

--- a/solution.py
+++ b/solution.py
@@ -134,6 +134,7 @@
 def return_kernel(owners, dy_ref, w_ref, back_ref, gbuf, own_sem, send_sem, recv_sem):
     me = lax.axis_index("dp")
     col = lax.axis_index("expert")
+    local_experts = w_ref.shape[0]
 
     barrier = pltpu.get_barrier_semaphore()
     for peer in range(owners - 1):
@@ -141,42 +142,52 @@
         pl.semaphore_signal(barrier, inc=1, device_id=(me, other), device_id_type=MESH)
     pl.semaphore_wait(barrier, owners - 1)
 
-    def send(source):
+    def send(source, j):
         return pltpu.make_async_remote_copy(
-            src_ref=gbuf.at[source],
-            dst_ref=back_ref.at[col],
-            send_sem=send_sem.at[source],
-            recv_sem=recv_sem.at[col],
+            src_ref=gbuf.at[source, j],
+            dst_ref=back_ref.at[col, j],
+            send_sem=send_sem.at[source, j],
+            recv_sem=recv_sem.at[col, j],
             device_id=(me, source),
             device_id_type=MESH,
         )
 
-    previous = None
-    for step in range(owners):
-        source = lax.rem(col + 1 + step, owners)
-        for j in range(w_ref.shape[0]):
+    def step(i, carry):
+        source = lax.rem(col + 1 + i, owners)
+        for j in range(local_experts):
             gbuf[source, j] = lax.dot_general(
                 dy_ref[source, j], w_ref[j], (((1,), (1,)), ((), ())),
                 preferred_element_type=jnp.float32,
             ).astype(gbuf.dtype)
-        if previous is not None:
-            send(previous).start()
-        previous = source
+
+        @pl.when(i > 0)
+        def _():
+            previous = lax.rem(col + i, owners)
+            for j in range(local_experts):
+                send(previous, j).start()
+
+        return carry
+
+    lax.fori_loop(0, owners, step, 0)
     own = pltpu.make_async_copy(gbuf.at[col], back_ref.at[col], own_sem)
     own.start()
 
-    for peer in range(owners - 1):
-        send(lax.rem(col + 1 + peer, owners)).wait_send()
-    for peer in range(owners - 1):
-        source = lax.rem(col + 1 + peer, owners)
-        pltpu.make_async_remote_copy(
-            src_ref=gbuf.at[source],
-            dst_ref=back_ref.at[source],
-            send_sem=send_sem.at[source],
-            recv_sem=recv_sem.at[source],
-            device_id=(me, source),
-            device_id_type=MESH,
-        ).wait_recv()
+    def finish(peer, carry):
+        other = lax.rem(col + 1 + peer, owners)
+        for j in range(local_experts):
+            send(other, j).wait_send()
+        for j in range(local_experts):
+            pltpu.make_async_remote_copy(
+                src_ref=gbuf.at[other, j],
+                dst_ref=back_ref.at[other, j],
+                send_sem=send_sem.at[other, j],
+                recv_sem=recv_sem.at[other, j],
+                device_id=(me, other),
+                device_id_type=MESH,
+            ).wait_recv()
+        return carry
+
+    lax.fori_loop(0, owners - 1, finish, 0)
     own.wait()
 
 
@@ -192,8 +203,8 @@
         scratch_shapes=[
             pltpu.VMEM(shape, dy.dtype),
             pltpu.SemaphoreType.DMA(()),
-            pltpu.SemaphoreType.DMA((owners,)),
-            pltpu.SemaphoreType.DMA((owners,)),
+            pltpu.SemaphoreType.DMA((owners, local_experts)),
+            pltpu.SemaphoreType.DMA((owners, local_experts)),
         ],
         compiler_params=pltpu.CompilerParams(
             collective_id=1, has_side_effects=True, vmem_limit_bytes=48 * 1024 * 1024

time: 225 us -> 226 us (level)
  transfers between devices with their start and end apart: 2 -> 2, of which waited for: 1 -> 1; matrix products, arithmetic and copies ran while one was open for 15% -> 15% of each run, Pallas kernels for 60% -> 61%
where the time goes in v8:
time: 226 us; the launch traced here: 223 us
  Pallas kernels  136 us (60%)
  other arithmetic  20.9 us (9%)
  waiting for transfers between devices  19.9 us (9%)
  local copies, waits for them, and re-layouts  17.9 us (8%)
  matrix products  14.2 us (6%)
  between operations  14.2 us (6%)
    pallas_call x1, Pallas kernels, exchange(): pl.pallas_call(lambda *refs: exchange_kernel(replicas, owners, pieces, *r...  69.6 us
    pallas_call x1, Pallas kernels, give_back(): pl.pallas_call(lambda *refs: return_kernel(owners, *refs), out_shape=jax....  66.7 us
    all_gather x1, waiting for transfers between devices, local(): cot_group = lax.all_gather(cotangent, 'expert', axis=0, tiled=True)  19.2 us
    gather x1, local copies, waits for them, and re-layouts, local(): scaled.reshape(routes, hidden_units)[route_of_slot]  9.4 us
    dot_general x2, matrix products, local(): jnp.einsum('scf,scd->fd', h_got[:, j], dy[:, j], preferred_element_type=j...  7.46 us
    dot_general x1, matrix products, local(): jnp.einsum('sct,std->scd', pick, cot_group.reshape(owners, tokens, width)...  6.24 us
    gather x1, local copies, waits for them, and re-layouts, local(): returned_rows = back.reshape(experts * capacity, hidden_units)[position]  5.21 us
  transfers between devices with their start and end apart: 2, of which 1 were waited for; matrix products, arithmetic and copies ran while one was open for 15% of the time, Pallas kernels for 61%

profile of v8, /device:TPU:64, one launch (start us, length us, event | category | flops | bytes accessed | tf_op | source)
XLA Modules:
  0.0 223.4 jit_solution(6661959149405502814)
XLA Ops:
  7.2 0.0 all-gather.2.cloned.1.call-start
  7.2 0.7 all-gather.2.cloned.1.call-update
  7.9 0.0 reduce-scatter.2.cloned.1.call-start
  7.9 0.8 copy.24
  8.7 0.8 copy.25
  9.5 0.1 reshape.176
  9.6 0.5 fusion.22
  10.2 1.0 fusion
  11.2 0.1 broadcast_in_dim.28
  11.3 0.9 select_reduce_fusion
  12.2 3.6 %fusion.16 = (bf16[1024,768]{1,0:T(8,128)(2,1)S(1)}, bf16[128,8,768]{2,1,0:T(8,128)(2,1)}) fusion(f32[128,8]{1,0:T(8,128)S(1)} %copy.24, bf16[128,8,1536]{2,1,0:T(8,128)(2,1)} %param.6), kind=kLoop, calls=%fused_computation.36 | loop fusion | flops 8650752 | bytes 6295552 | tf_op jit(solution)/shard_map/reshape | solution.py:257
  15.8 9.4 %gather_fusion = bf16[2048,768]{1,0:T(8,128)(2,1)} fusion(bf16[1024,768]{1,0:T(8,128)(2,1)S(1)} %get-tuple-element.25, s32[2048]{0:T(1024)S(1)} %broadcast_clamp_fusion), kind=kCustom, calls=%fused_computation | custom fusion | bytes 6299648 | tf_op jit(solution)/shard_map/gather | solution.py:257
  25.2 0.6 copy_select_fusion.refs_2_
  25.9 3.4 %broadcast_select_fusion.refs_1_ = bf16[16,2,64,768]{3,2,1,0:T(8,128)(2,1)} fusion(bf16[16,2,64,768]{3,2,1,0:T(8,128)(2,1)} %bitcast.54, pred[16,2,64]{2,1,0:T(4,128)(4,1)S(1)} %broadcast_in_dim.28), kind=kLoop, calls=%fused_computation.35 | loop fusion | flops 1572864 | bytes 6293504 | tf_op jit(solution)/shard_map/jit(_where)/select_n | solution.py:257
  29.3 69.6 %shard_map.76 = (bf16[2,16,48,2048]{3,2,1,0:T(8,128)(2,1)}, bf16[16,2,64,768]{3,2,1,0:T(8,128)(2,1)}, s32[16,1,128]{2,1,0:T(1,128)}) custom-call(bf16[2,48,2048]{2,1,0:T(8,128)(2,1)} %refs_0_.1, bf16[16,2,64,768]{3,2,1,0:T(8,128)(2,1)} %broadcast_select_fusion.refs_1_, s32[16,1,128]{2,1,0:T(1,128)} %copy_select_fusion.refs_2_), custom_call_target="tpu_custom_call" | custom-call | bytes 18874368 | tf_op jit(solution)/shard_map/pallas_call | solution.py:107
  98.9 19.2 %all-gather.2.cloned.1.call-done = bf16[2048,2048]{1,0:T(8,128)(2,1)} async-done(((bf16[128,2048]{1,0:T(8,128)(2,1)}), bf16[2048,2048]{1,0:T(8,128)(2,1)}) %all-gather.2.cloned.1.call-update) | async-done | bytes 8388624 | tf_op jit(solution)/shard_map/all_gather | solution.py:240
  118.1 0.0 copy-start.2
  118.1 6.2 %fusion.23 = bf16[16,128,2048]{2,1,0:T(8,128)(2,1)S(1)} fusion(bf16[16,128,2048]{2,1,0:T(8,128)(2,1)} %bitcast.50, s32[16,128]{1,0:T(8,128)} %bitcast.57), kind=kOutput, calls=%fused_computation.44 | convolution fusion | flops 1074003968 | bytes 16785408 | tf_op jit(solution)/shard_map/sct,std->scd/dot_general | solution.py:265
  124.4 0.0 copy-start
  124.4 0.0 copy-done.2
  124.4 3.7 %bitcast_convert_fusion = bf16[768,2048]{1,0:T(8,128)(2,1)S(1)} fusion(bf16[16,2,64,2048]{3,2,1,0:T(8,128)(2,1)S(1)} %bitcast.51, bf16[16,2,64,768]{3,2,1,0:T(8,128)(2,1)S(1)} %copy-done.2), kind=kOutput, calls=%fused_computation.6 | convolution fusion | flops 3222798336 | bytes 8912896 | tf_op jit(solution)/shard_map/scf,scd->fd/dot_general | solution.py:272
  128.1 0.0 copy-done
  128.1 3.7 %bitcast_convert_fusion.1 = bf16[768,2048]{1,0:T(8,128)(2,1)S(1)} fusion(bf16[16,2,64,2048]{3,2,1,0:T(8,128)(2,1)S(1)} %bitcast.52, bf16[16,2,64,768]{3,2,1,0:T(8,128)(2,1)S(1)} %copy-done.2), kind=kOutput, calls=%fused_computation.7 | convolution fusion | flops 3222798336 | bytes 8912896 | tf_op jit(solution)/shard_map/scf,scd->fd/dot_general | solution.py:272
  131.9 3.1 %pad_maximum_fusion = bf16[16,2,48,2048]{3,2,1,0:T(8,128)(2,1)} fusion(bf16[16,1,48,2048]{3,2,1,0:T(8,128)(2,1)S(1)} %bitcast.55, bf16[16,1,48,2048]{3,2,1,0:T(8,128)(2,1)S(1)} %bitcast.56), kind=kLoop, calls=%fused_computation.5 | loop fusion | flops 3145728 | bytes 12582912 | tf_op jit(solution)/shard_map/stack | solution.py:276
  135.0 0.0 copy-start.1
  135.0 0.0 reduce-scatter.2.cloned.1.call-update
  135.0 0.6 copy-done.1
  135.7 0.1 copy.29
  135.8 0.1 mul.74
  135.9 66.7 %shard_map.77 = bf16[16,2,64,768]{3,2,1,0:T(8,128)(2,1)S(1)} custom-call(bf16[16,2,64,2048]{3,2,1,0:T(8,128)(2,1)} %bitcast.53, bf16[2,768,2048]{2,1,0:T(8,128)(2,1)} %bitcast.64), custom_call_target="tpu_custom_call" | custom-call | flops 6442450944 | bytes 20971520 | tf_op jit(solution)/shard_map/pallas_call | solution.py:198
  202.6 5.2 %gather_fusion.1 = bf16[1024,768]{1,0:T(8,128)(2,1)} fusion(bf16[2048,768]{1,0:T(8,128)(2,1)S(1)} %bitcast.49, s32[1024]{0:T(1024)S(1)} %broadcast_clamp_fusion.1), kind=kCustom, calls=%fused_computation.1 | custom fusion | bytes 3149824 | tf_op jit(solution)/shard_map/gather | solution.py:281
  207.8 4.2 %fusion.9 = (bf16[128,8,768]{2,1,0:T(8,128)(2,1)S(1)}, bf16[128,8,768]{2,1,0:T(8,128)(2,1)S(1)}, f32[128,8]{1,0:T(8,128)S(1)}) fusion(bf16[1024,768]{1,0:T(8,128)(2,1)} %gather_fusion.1, f32[128,8]{1,0:T(8,128)S(1)} %copy.24, bf16[128,8,1536]{2,1,0:T(8,128)(2,1)} %param.6, bf16[128,8,768]{2,1,0:T(8,128)(2,1)} %get-tuple-element.26), kind=kLoop, calls=%fused_computation.27 | loop fusion | flops 15727616 | bytes 9445376 | tf_op jit(solution)/shard_map/convert.2
  212.1 0.7 copy.30
  212.8 1.9 pad_maximum_fusion.1
  214.7 0.0 reduce-scatter.2.cloned.1.call-done
  214.7 1.9 bitcast_convert_fusion.2
  (7 shorter events, 0.0 us)
Async XLA Ops:
  7.2 110.9 %all-gather.2.cloned.1.call-start = ((), (), s32[]{:S(2)}) async-start(), calls=%async_computation.1 | async-start | bytes 8912896 | tf_op jit(solution)/shard_map/all_gather | solution.py:240
  7.9 206.8 %reduce-scatter.2.cloned.1.call-start = ((), (), s32[]{:S(2)}) async-start(), calls=%async_computation.2 | async-start | bytes 6684672 | tf_op jit(solution)/shard_map/reduce_scatter | solution.py:278
  118.1 6.3 %copy-start.2 = (bf16[16,2,64,768]{3,2,1,0:T(8,128)(2,1)S(1)}, bf16[16,2,64,768]{3,2,1,0:T(8,128)(2,1)}, u32[]{:S(2)}) copy-start(bf16[16,2,64,768]{3,2,1,0:T(8,128)(2,1)} %get-tuple-element.13) | copy-start | bytes 9437188
  124.4 3.8 %copy-start = (bf16[16,128,2048]{2,1,0:T(8,128)(2,1)}, bf16[16,128,2048]{2,1,0:T(8,128)(2,1)S(1)}, u32[]{:S(2)}) copy-start(bf16[16,128,2048]{2,1,0:T(8,128)(2,1)S(1)} %fusion.23) | copy-start | bytes 25165828
  135.0 0.7 copy-start.1
Sparse Core Ops, SparseCore 0:
  10.4 107.6 all-gather.1
  135.1 64.0 reduce-scatter.1

commit v9 on v8

--- a/solution.py
+++ b/solution.py
@@ -131,7 +131,7 @@
     )(w_down, h_send, t_send)
 
 
-def return_kernel(owners, dy_ref, w_ref, back_ref, gbuf, own_sem, send_sem, recv_sem):
+def return_kernel(owners, pieces, dy_ref, w_ref, back_ref, gbuf, own_sem, send_sem, recv_sem):
     me = lax.axis_index("dp")
     col = lax.axis_index("expert")
     local_experts = w_ref.shape[0]
@@ -142,12 +142,15 @@
         pl.semaphore_signal(barrier, inc=1, device_id=(me, other), device_id_type=MESH)
     pl.semaphore_wait(barrier, owners - 1)
 
-    def send(source, j):
+    rows = gbuf.shape[2] // pieces
+
+    def send(source, j, piece):
+        part = pl.ds(piece * rows, rows)
         return pltpu.make_async_remote_copy(
-            src_ref=gbuf.at[source, j],
-            dst_ref=back_ref.at[col, j],
-            send_sem=send_sem.at[source, j],
-            recv_sem=recv_sem.at[col, j],
+            src_ref=gbuf.at[source, j, part],
+            dst_ref=back_ref.at[col, j, part],
+            send_sem=send_sem.at[source, j, piece],
+            recv_sem=recv_sem.at[col, j, piece],
             device_id=(me, source),
             device_id_type=MESH,
         )
@@ -164,7 +167,8 @@
         def _():
             previous = lax.rem(col + i, owners)
             for j in range(local_experts):
-                send(previous, j).start()
+                for piece in range(pieces):
+                    send(previous, j, piece).start()
 
         return carry
 
@@ -175,36 +179,39 @@
     def finish(peer, carry):
         other = lax.rem(col + 1 + peer, owners)
         for j in range(local_experts):
-            send(other, j).wait_send()
+            for piece in range(pieces):
+                send(other, j, piece).wait_send()
         for j in range(local_experts):
-            pltpu.make_async_remote_copy(
-                src_ref=gbuf.at[other, j],
-                dst_ref=back_ref.at[other, j],
-                send_sem=send_sem.at[other, j],
-                recv_sem=recv_sem.at[other, j],
-                device_id=(me, other),
-                device_id_type=MESH,
-            ).wait_recv()
+            for piece in range(pieces):
+                part = pl.ds(piece * rows, rows)
+                pltpu.make_async_remote_copy(
+                    src_ref=gbuf.at[other, j, part],
+                    dst_ref=back_ref.at[other, j, part],
+                    send_sem=send_sem.at[other, j, piece],
+                    recv_sem=recv_sem.at[other, j, piece],
+                    device_id=(me, other),
+                    device_id_type=MESH,
+                ).wait_recv()
         return carry
 
     lax.fori_loop(0, owners - 1, finish, 0)
     own.wait()
 
 
-def give_back(dy, full_down, owners):
+def give_back(dy, full_down, owners, pieces=2):
     sources, local_experts, capacity, width = dy.shape
     hidden_units = full_down.shape[1]
     shape = (sources, local_experts, capacity, hidden_units)
     return pl.pallas_call(
-        lambda *refs: return_kernel(owners, *refs),
+        lambda *refs: return_kernel(owners, pieces, *refs),
         out_shape=jax.ShapeDtypeStruct(shape, dy.dtype),
         in_specs=[pl.BlockSpec(memory_space=pltpu.VMEM)] * 2,
         out_specs=pl.BlockSpec(memory_space=pl.ANY),
         scratch_shapes=[
             pltpu.VMEM(shape, dy.dtype),
             pltpu.SemaphoreType.DMA(()),
-            pltpu.SemaphoreType.DMA((owners, local_experts)),
-            pltpu.SemaphoreType.DMA((owners, local_experts)),
+            pltpu.SemaphoreType.DMA((owners, local_experts, pieces)),
+            pltpu.SemaphoreType.DMA((owners, local_experts, pieces)),
         ],
         compiler_params=pltpu.CompilerParams(
             collective_id=1, has_side_effects=True, vmem_limit_bytes=48 * 1024 * 1024

time: 226 us -> 227 us (level)
  no operation moved by 1% of the time
where the time goes in v9:
time: 227 us; the launch traced here: 224 us
  Pallas kernels  137 us (60%)
  other arithmetic  20.9 us (9%)
  waiting for transfers between devices  19.9 us (9%)
  local copies, waits for them, and re-layouts  17.9 us (8%)
  matrix products  14.2 us (6%)
  between operations  14.2 us (6%)
    pallas_call x1, Pallas kernels, exchange(): pl.pallas_call(lambda *refs: exchange_kernel(replicas, owners, pieces, *r...  69.6 us
    pallas_call x1, Pallas kernels, give_back(): pl.pallas_call(lambda *refs: return_kernel(owners, pieces, *refs), out_sh...  67.3 us
    all_gather x1, waiting for transfers between devices, local(): cot_group = lax.all_gather(cotangent, 'expert', axis=0, tiled=True)  19.2 us
    gather x1, local copies, waits for them, and re-layouts, local(): scaled.reshape(routes, hidden_units)[route_of_slot]  9.4 us
    dot_general x2, matrix products, local(): jnp.einsum('scf,scd->fd', h_got[:, j], dy[:, j], preferred_element_type=j...  7.46 us
    dot_general x1, matrix products, local(): jnp.einsum('sct,std->scd', pick, cot_group.reshape(owners, tokens, width)...  6.24 us
    gather x1, local copies, waits for them, and re-layouts, local(): returned_rows = back.reshape(experts * capacity, hidden_units)[position]  5.21 us
  transfers between devices with their start and end apart: 2, of which 1 were waited for; matrix products, arithmetic and copies ran while one was open for 15% of the time, Pallas kernels for 61%

profile of v9, /device:TPU:64, one launch (start us, length us, event | category | flops | bytes accessed | tf_op | source)
XLA Modules:
  0.0 224.0 jit_solution(17678671721867654676)
XLA Ops:
  7.2 0.0 all-gather.2.cloned.1.call-start
  7.2 0.7 all-gather.2.cloned.1.call-update
  7.9 0.0 reduce-scatter.2.cloned.1.call-start
  7.9 0.8 copy.24
  8.7 0.8 copy.25
  9.5 0.1 reshape.176
  9.6 0.5 fusion.22
  10.2 1.0 fusion
  11.2 0.1 broadcast_in_dim.28
  11.3 0.9 select_reduce_fusion
  12.2 3.6 %fusion.16 = (bf16[1024,768]{1,0:T(8,128)(2,1)S(1)}, bf16[128,8,768]{2,1,0:T(8,128)(2,1)}) fusion(f32[128,8]{1,0:T(8,128)S(1)} %copy.24, bf16[128,8,1536]{2,1,0:T(8,128)(2,1)} %param.6), kind=kLoop, calls=%fused_computation.36 | loop fusion | flops 8650752 | bytes 6295552 | tf_op jit(solution)/shard_map/reshape | solution.py:264
  15.8 9.4 %gather_fusion = bf16[2048,768]{1,0:T(8,128)(2,1)} fusion(bf16[1024,768]{1,0:T(8,128)(2,1)S(1)} %get-tuple-element.25, s32[2048]{0:T(1024)S(1)} %broadcast_clamp_fusion), kind=kCustom, calls=%fused_computation | custom fusion | bytes 6299648 | tf_op jit(solution)/shard_map/gather | solution.py:264
  25.2 0.6 copy_select_fusion.refs_2_
  25.9 3.4 %broadcast_select_fusion.refs_1_ = bf16[16,2,64,768]{3,2,1,0:T(8,128)(2,1)} fusion(bf16[16,2,64,768]{3,2,1,0:T(8,128)(2,1)} %bitcast.54, pred[16,2,64]{2,1,0:T(4,128)(4,1)S(1)} %broadcast_in_dim.28), kind=kLoop, calls=%fused_computation.35 | loop fusion | flops 1572864 | bytes 6293504 | tf_op jit(solution)/shard_map/jit(_where)/select_n | solution.py:264
  29.3 69.6 %shard_map.76 = (bf16[2,16,48,2048]{3,2,1,0:T(8,128)(2,1)}, bf16[16,2,64,768]{3,2,1,0:T(8,128)(2,1)}, s32[16,1,128]{2,1,0:T(1,128)}) custom-call(bf16[2,48,2048]{2,1,0:T(8,128)(2,1)} %refs_0_.1, bf16[16,2,64,768]{3,2,1,0:T(8,128)(2,1)} %broadcast_select_fusion.refs_1_, s32[16,1,128]{2,1,0:T(1,128)} %copy_select_fusion.refs_2_), custom_call_target="tpu_custom_call" | custom-call | bytes 18874368 | tf_op jit(solution)/shard_map/pallas_call | solution.py:107
  98.9 19.2 %all-gather.2.cloned.1.call-done = bf16[2048,2048]{1,0:T(8,128)(2,1)} async-done(((bf16[128,2048]{1,0:T(8,128)(2,1)}), bf16[2048,2048]{1,0:T(8,128)(2,1)}) %all-gather.2.cloned.1.call-update) | async-done | bytes 8388624 | tf_op jit(solution)/shard_map/all_gather | solution.py:247
  118.1 0.0 copy-start.2
  118.1 6.2 %fusion.23 = bf16[16,128,2048]{2,1,0:T(8,128)(2,1)S(1)} fusion(bf16[16,128,2048]{2,1,0:T(8,128)(2,1)} %bitcast.50, s32[16,128]{1,0:T(8,128)} %bitcast.57), kind=kOutput, calls=%fused_computation.44 | convolution fusion | flops 1074003968 | bytes 16785408 | tf_op jit(solution)/shard_map/sct,std->scd/dot_general | solution.py:272
  124.4 0.0 copy-start
  124.4 0.0 copy-done.2
  124.4 3.7 %bitcast_convert_fusion = bf16[768,2048]{1,0:T(8,128)(2,1)S(1)} fusion(bf16[16,2,64,2048]{3,2,1,0:T(8,128)(2,1)S(1)} %bitcast.51, bf16[16,2,64,768]{3,2,1,0:T(8,128)(2,1)S(1)} %copy-done.2), kind=kOutput, calls=%fused_computation.6 | convolution fusion | flops 3222798336 | bytes 8912896 | tf_op jit(solution)/shard_map/scf,scd->fd/dot_general | solution.py:279
  128.1 0.0 copy-done
  128.1 3.7 %bitcast_convert_fusion.1 = bf16[768,2048]{1,0:T(8,128)(2,1)S(1)} fusion(bf16[16,2,64,2048]{3,2,1,0:T(8,128)(2,1)S(1)} %bitcast.52, bf16[16,2,64,768]{3,2,1,0:T(8,128)(2,1)S(1)} %copy-done.2), kind=kOutput, calls=%fused_computation.7 | convolution fusion | flops 3222798336 | bytes 8912896 | tf_op jit(solution)/shard_map/scf,scd->fd/dot_general | solution.py:279
  131.9 3.1 %pad_maximum_fusion = bf16[16,2,48,2048]{3,2,1,0:T(8,128)(2,1)} fusion(bf16[16,1,48,2048]{3,2,1,0:T(8,128)(2,1)S(1)} %bitcast.55, bf16[16,1,48,2048]{3,2,1,0:T(8,128)(2,1)S(1)} %bitcast.56), kind=kLoop, calls=%fused_computation.5 | loop fusion | flops 3145728 | bytes 12582912 | tf_op jit(solution)/shard_map/stack | solution.py:283
  135.0 0.0 copy-start.1
  135.0 0.0 reduce-scatter.2.cloned.1.call-update
  135.0 0.6 copy-done.1
  135.7 0.1 copy.29
  135.8 0.1 mul.74
  135.9 67.3 %shard_map.77 = bf16[16,2,64,768]{3,2,1,0:T(8,128)(2,1)S(1)} custom-call(bf16[16,2,64,2048]{3,2,1,0:T(8,128)(2,1)} %bitcast.53, bf16[2,768,2048]{2,1,0:T(8,128)(2,1)} %bitcast.64), custom_call_target="tpu_custom_call" | custom-call | flops 6442450944 | bytes 20971520 | tf_op jit(solution)/shard_map/pallas_call | solution.py:205
  203.2 5.2 %gather_fusion.1 = bf16[1024,768]{1,0:T(8,128)(2,1)} fusion(bf16[2048,768]{1,0:T(8,128)(2,1)S(1)} %bitcast.49, s32[1024]{0:T(1024)S(1)} %broadcast_clamp_fusion.1), kind=kCustom, calls=%fused_computation.1 | custom fusion | bytes 3149824 | tf_op jit(solution)/shard_map/gather | solution.py:288
  208.4 4.2 %fusion.9 = (bf16[128,8,768]{2,1,0:T(8,128)(2,1)S(1)}, bf16[128,8,768]{2,1,0:T(8,128)(2,1)S(1)}, f32[128,8]{1,0:T(8,128)S(1)}) fusion(bf16[1024,768]{1,0:T(8,128)(2,1)} %gather_fusion.1, f32[128,8]{1,0:T(8,128)S(1)} %copy.24, bf16[128,8,1536]{2,1,0:T(8,128)(2,1)} %param.6, bf16[128,8,768]{2,1,0:T(8,128)(2,1)} %get-tuple-element.26), kind=kLoop, calls=%fused_computation.27 | loop fusion | flops 15727616 | bytes 9445376 | tf_op jit(solution)/shard_map/convert.2
  212.7 0.7 copy.30
  213.4 1.9 pad_maximum_fusion.1
  215.3 0.0 reduce-scatter.2.cloned.1.call-done
  215.3 1.9 bitcast_convert_fusion.2
  (7 shorter events, 0.0 us)
Async XLA Ops:
  7.2 110.9 %all-gather.2.cloned.1.call-start = ((), (), s32[]{:S(2)}) async-start(), calls=%async_computation.1 | async-start | bytes 8912896 | tf_op jit(solution)/shard_map/all_gather | solution.py:247
  7.9 207.4 %reduce-scatter.2.cloned.1.call-start = ((), (), s32[]{:S(2)}) async-start(), calls=%async_computation.2 | async-start | bytes 6684672 | tf_op jit(solution)/shard_map/reduce_scatter | solution.py:285
  118.1 6.3 %copy-start.2 = (bf16[16,2,64,768]{3,2,1,0:T(8,128)(2,1)S(1)}, bf16[16,2,64,768]{3,2,1,0:T(8,128)(2,1)}, u32[]{:S(2)}) copy-start(bf16[16,2,64,768]{3,2,1,0:T(8,128)(2,1)} %get-tuple-element.13) | copy-start | bytes 9437188
  124.4 3.8 %copy-start = (bf16[16,128,2048]{2,1,0:T(8,128)(2,1)}, bf16[16,128,2048]{2,1,0:T(8,128)(2,1)S(1)}, u32[]{:S(2)}) copy-start(bf16[16,128,2048]{2,1,0:T(8,128)(2,1)S(1)} %fusion.23) | copy-start | bytes 25165828
  135.0 0.7 copy-start.1
Sparse Core Ops, SparseCore 0:
  10.4 107.6 all-gather.1
  135.1 64.0 reduce-scatter.1

commit v10 on v8

--- a/solution.py
+++ b/solution.py
@@ -281,10 +281,14 @@
     returned_rows = back.reshape(experts * capacity, hidden_units)[position]
     qf = returned_rows.reshape(tokens, top, hidden_units).astype(jnp.float32)
     route_grad = jnp.sum(qf * hidden.astype(jnp.float32), -1)
-    d_hidden = weights * qf
-    d_gate = d_hidden * up * sig * (1.0 + gate * (1.0 - sig))
-    d_up = d_hidden * act
-    grad_gate_up = jnp.concatenate([d_gate, d_up], -1).astype(jnp.bfloat16)
+    row = saved_gate_up.astype(jnp.float32)
+    partner = jnp.roll(row, hidden_units, axis=-1)
+    is_gate = jnp.arange(2 * hidden_units) < hidden_units
+    g = jnp.where(is_gate, row, partner)
+    u = jnp.where(is_gate, partner, row)
+    s_g = jax.nn.sigmoid(g)
+    d_both = weights * jnp.concatenate([qf, qf], -1)
+    grad_gate_up = jnp.where(is_gate, d_both * u * s_g * (1.0 + g * (1.0 - s_g)), d_both * (g * s_g)).astype(jnp.bfloat16)
     return (grad_gate_up, route_grad, grad_down)
 
 

time: 226 us -> 233 us (1.031)
  other arithmetic: 20.9 us -> 28.1 us
    convert_element_type x0 -> x2, other arithmetic: none -> 8.77 us  [the longest x1 6.86 us: local(): jnp.where(is_gate, d_both * u * s_g * (1.0 + g * (1.0 - s_g)), d_both * (...]
    slice x0 -> x1, other arithmetic: none -> 5.96 us  [local(): partner = jnp.roll(row, hidden_units, axis=-1)]
    another operation x1 -> x0, other arithmetic: 4.24 us -> none
    reshape x1 -> x0, other arithmetic: 3.58 us -> none  [local(): scaled.reshape(routes, hidden_units)[route_of_slot]]
    reduce_sum x0 -> x1, other arithmetic: none -> 2.36 us  [local(): route_grad = jnp.sum(qf * hidden.astype(jnp.float32), -1)]
  transfers between devices with their start and end apart: 2 -> 2, of which waited for: 1 -> 1; matrix products, arithmetic and copies ran while one was open for 15% -> 18% of each run, Pallas kernels for 61% -> 58%
where the time goes in v10:
time: 233 us; the launch traced here: 230 us
  Pallas kernels  134 us (58%)
  other arithmetic  28.1 us (12%)
  waiting for transfers between devices  21.8 us (9%)
  local copies, waits for them, and re-layouts  17.9 us (8%)
  matrix products  14.2 us (6%)
  between operations  14.2 us (6%)
    pallas_call x1, Pallas kernels, exchange(): pl.pallas_call(lambda *refs: exchange_kernel(replicas, owners, pieces, *r...  67.4 us
    pallas_call x1, Pallas kernels, give_back(): pl.pallas_call(lambda *refs: return_kernel(owners, *refs), out_shape=jax....  66.3 us
    all_gather x1, waiting for transfers between devices, local(): cot_group = lax.all_gather(cotangent, 'expert', axis=0, tiled=True)  21.1 us
    gather x1, local copies, waits for them, and re-layouts, local(): scaled.reshape(routes, hidden_units)[route_of_slot]  9.4 us
    dot_general x2, matrix products, local(): jnp.einsum('scf,scd->fd', h_got[:, j], dy[:, j], preferred_element_type=j...  7.46 us
    convert_element_type x1, other arithmetic, local(): jnp.where(is_gate, d_both * u * s_g * (1.0 + g * (1.0 - s_g)), d_both * (...  6.86 us
    dot_general x1, matrix products, local(): jnp.einsum('sct,std->scd', pick, cot_group.reshape(owners, tokens, width)...  6.24 us
    slice x1, other arithmetic, local(): partner = jnp.roll(row, hidden_units, axis=-1)  5.96 us
  transfers between devices with their start and end apart: 2, of which 1 were waited for; matrix products, arithmetic and copies ran while one was open for 18% of the time, Pallas kernels for 58%

profile of v10, /device:TPU:64, one launch (start us, length us, event | category | flops | bytes accessed | tf_op | source)
XLA Modules:
  0.0 230.0 jit_solution(2654833790239742090)
XLA Ops:
  7.2 0.0 all-gather.2.cloned.1.call-start
  7.2 0.7 all-gather.2.cloned.1.call-update
  7.9 0.0 reduce-scatter.2.cloned.1.call-start
  7.9 0.8 copy.28
  8.7 0.1 reshape.176
  8.8 0.8 copy.27
  9.6 0.5 fusion.23
  10.2 1.0 fusion
  11.2 0.1 broadcast_in_dim.50
  11.3 0.9 select_reduce_fusion
  12.2 6.0 %fusion.29 = (f32[128,8,768]{2,1,0:T(8,128)}, f32[128,8,768]{2,1,0:T(8,128)}, bf16[1024,768]{1,0:T(8,128)(2,1)S(1)}, bf16[128,8,768]{2,1,0:T(8,128)(2,1)}) fusion(bf16[128,8,1536]{2,1,0:T(8,128)(2,1)} %param.6, f32[128,8]{1,0:T(8,128)S(1)} %copy.27), kind=kLoop, calls=%fused_computation.61 | loop fusion | flops 8650752 | bytes 18878464 | tf_op jit(solution)/shard_map/jit(_roll_static)/slice | solution.py:285
  18.2 9.4 %gather_fusion = bf16[2048,768]{1,0:T(8,128)(2,1)} fusion(bf16[1024,768]{1,0:T(8,128)(2,1)S(1)} %get-tuple-element.29, s32[2048]{0:T(1024)S(1)} %broadcast_clamp_fusion), kind=kCustom, calls=%fused_computation | custom fusion | bytes 6299648 | tf_op jit(solution)/shard_map/gather | solution.py:257
  27.6 0.6 copy_select_fusion.refs_2_
  28.2 3.3 %broadcast_select_fusion.refs_1_ = bf16[16,2,64,768]{3,2,1,0:T(8,128)(2,1)} fusion(bf16[16,2,64,768]{3,2,1,0:T(8,128)(2,1)} %bitcast.54, pred[16,2,64]{2,1,0:T(4,128)(4,1)S(1)} %broadcast_in_dim.50), kind=kLoop, calls=%fused_computation.33 | loop fusion | flops 1572864 | bytes 6293504 | tf_op jit(solution)/shard_map/jit(_where)/select_n | solution.py:257
  31.5 67.4 %shard_map.76 = (bf16[2,16,48,2048]{3,2,1,0:T(8,128)(2,1)}, bf16[16,2,64,768]{3,2,1,0:T(8,128)(2,1)}, s32[16,1,128]{2,1,0:T(1,128)}) custom-call(bf16[2,48,2048]{2,1,0:T(8,128)(2,1)} %refs_0_.1, bf16[16,2,64,768]{3,2,1,0:T(8,128)(2,1)} %broadcast_select_fusion.refs_1_, s32[16,1,128]{2,1,0:T(1,128)} %copy_select_fusion.refs_2_), custom_call_target="tpu_custom_call" | custom-call | bytes 18874368 | tf_op jit(solution)/shard_map/pallas_call | solution.py:107
  98.9 21.1 %all-gather.2.cloned.1.call-done = bf16[2048,2048]{1,0:T(8,128)(2,1)} async-done(((bf16[128,2048]{1,0:T(8,128)(2,1)}), bf16[2048,2048]{1,0:T(8,128)(2,1)}) %all-gather.2.cloned.1.call-update) | async-done | bytes 8388624 | tf_op jit(solution)/shard_map/all_gather | solution.py:240
  120.0 0.0 copy-start.3
  120.0 6.2 %fusion.24 = bf16[16,128,2048]{2,1,0:T(8,128)(2,1)S(1)} fusion(bf16[16,128,2048]{2,1,0:T(8,128)(2,1)} %bitcast.50, s32[16,128]{1,0:T(8,128)} %bitcast.57), kind=kOutput, calls=%fused_computation.43 | convolution fusion | flops 1074003968 | bytes 16785408 | tf_op jit(solution)/shard_map/sct,std->scd/dot_general | solution.py:265
  126.3 0.0 copy-start.1
  126.3 0.0 copy-done.3
  126.3 3.7 %bitcast_convert_fusion.1 = bf16[768,2048]{1,0:T(8,128)(2,1)S(1)} fusion(bf16[16,2,64,2048]{3,2,1,0:T(8,128)(2,1)S(1)} %bitcast.51, bf16[16,2,64,768]{3,2,1,0:T(8,128)(2,1)S(1)} %copy-done.3), kind=kOutput, calls=%fused_computation.15 | convolution fusion | flops 3222798336 | bytes 8912896 | tf_op jit(solution)/shard_map/scf,scd->fd/dot_general | solution.py:272
  130.0 0.0 copy-done.1
  130.1 3.7 %bitcast_convert_fusion = bf16[768,2048]{1,0:T(8,128)(2,1)S(1)} fusion(bf16[16,2,64,2048]{3,2,1,0:T(8,128)(2,1)S(1)} %bitcast.52, bf16[16,2,64,768]{3,2,1,0:T(8,128)(2,1)S(1)} %copy-done.3), kind=kOutput, calls=%fused_computation.14 | convolution fusion | flops 3222798336 | bytes 8912896 | tf_op jit(solution)/shard_map/scf,scd->fd/dot_general | solution.py:272
  133.8 3.1 %pad_maximum_fusion = bf16[16,2,48,2048]{3,2,1,0:T(8,128)(2,1)} fusion(bf16[16,1,48,2048]{3,2,1,0:T(8,128)(2,1)S(1)} %bitcast.56, bf16[16,1,48,2048]{3,2,1,0:T(8,128)(2,1)S(1)} %bitcast.55), kind=kLoop, calls=%fused_computation.5 | loop fusion | flops 3145728 | bytes 12582912 | tf_op jit(solution)/shard_map/stack | solution.py:276
  136.9 0.0 copy-start.2
  136.9 0.0 reduce-scatter.2.cloned.1.call-update
  137.0 0.6 copy-done.2
  137.6 0.1 copy.33
  137.7 0.1 mul.80
  137.9 66.3 %shard_map.77 = bf16[16,2,64,768]{3,2,1,0:T(8,128)(2,1)S(1)} custom-call(bf16[16,2,64,2048]{3,2,1,0:T(8,128)(2,1)} %bitcast.53, bf16[2,768,2048]{2,1,0:T(8,128)(2,1)} %bitcast.64), custom_call_target="tpu_custom_call" | custom-call | flops 6442450944 | bytes 20971520 | tf_op jit(solution)/shard_map/pallas_call | solution.py:198
  204.2 5.2 %gather_fusion.1 = bf16[1024,768]{1,0:T(8,128)(2,1)} fusion(bf16[2048,768]{1,0:T(8,128)(2,1)S(1)} %bitcast.49, s32[1024]{0:T(1024)S(1)} %broadcast_clamp_fusion.1), kind=kCustom, calls=%fused_computation.1 | custom fusion | bytes 3149824 | tf_op jit(solution)/shard_map/gather | solution.py:281
  209.4 2.4 %fusion.15 = f32[128,8]{1,0:T(8,128)S(1)} fusion(bf16[128,8,768]{2,1,0:T(8,128)(2,1)} %get-tuple-element.30, bf16[1024,768]{1,0:T(8,128)(2,1)} %gather_fusion.1), kind=kLoop, calls=%fused_computation.31 | loop fusion | flops 3144704 | bytes 3149824 | tf_op jit(solution)/shard_map/reduce_sum | solution.py:283
  211.8 0.0 copy-start
  211.8 0.7 copy.34
  212.4 1.9 bitcast_convert_fusion.2
  214.4 0.0 copy-done
  214.4 6.9 %fusion.6 = bf16[128,8,1536]{2,1,0:T(8,128)(2,1)} fusion(f32[128,8,768]{2,1,0:T(8,128)S(1)} %bitcast_convert_fusion.2, f32[128,8,768]{2,1,0:T(8,128)} %get-tuple-element.28, f32[128,8,768]{2,1,0:T(8,128)} %get-tuple-element.27, f32[128,8]{1,0:T(8,128)S(1)} %copy.27, pred[1536]{0:T(1024)(128)(4,1)S(1)} %iota_compare_fusion.11, ...), kind=kLoop, calls=%fused_computation.12 | loop fusion | flops 29884416 | bytes 15734272 | tf_op jit(solution)/shard_map/convert_element_type | solution.py:291
  221.2 0.0 reduce-scatter.2.cloned.1.call-done
  221.2 1.9 bitcast_convert_fusion.3
  (8 shorter events, 0.0 us)
Async XLA Ops:
  7.2 112.9 %all-gather.2.cloned.1.call-start = ((), (), s32[]{:S(2)}) async-start(), calls=%async_computation.1 | async-start | bytes 8912896 | tf_op jit(solution)/shard_map/all_gather | solution.py:240
  7.9 213.3 %reduce-scatter.2.cloned.1.call-start = ((), (), s32[]{:S(2)}) async-start(), calls=%async_computation.2 | async-start | bytes 6684672 | tf_op jit(solution)/shard_map/reduce_scatter | solution.py:278
  120.0 6.3 %copy-start.3 = (bf16[16,2,64,768]{3,2,1,0:T(8,128)(2,1)S(1)}, bf16[16,2,64,768]{3,2,1,0:T(8,128)(2,1)}, u32[]{:S(2)}) copy-start(bf16[16,2,64,768]{3,2,1,0:T(8,128)(2,1)} %get-tuple-element.13) | copy-start | bytes 9437188
  126.3 3.8 %copy-start.1 = (bf16[16,128,2048]{2,1,0:T(8,128)(2,1)}, bf16[16,128,2048]{2,1,0:T(8,128)(2,1)S(1)}, u32[]{:S(2)}) copy-start(bf16[16,128,2048]{2,1,0:T(8,128)(2,1)S(1)} %fusion.24) | copy-start | bytes 25165828
  136.9 0.7 copy-start.2
  211.8 2.6 %copy-start = (bf16[128,8,1536]{2,1,0:T(8,128)(2,1)S(1)}, bf16[128,8,1536]{2,1,0:T(8,128)(2,1)}, u32[]{:S(2)}) copy-start(bf16[128,8,1536]{2,1,0:T(8,128)(2,1)} %param.6) | copy-start | bytes 9437188
Sparse Core Ops, SparseCore 0:
  10.4 109.5 all-gather.1
  137.1 64.2 reduce-scatter.1

commit v11 on v8

--- a/solution.py
+++ b/solution.py
@@ -278,8 +278,12 @@
     summed = lax.psum_scatter(stacked, "dp", scatter_dimension=0, tiled=True)
     grad_down = summed[0].astype(jnp.float32)
     back = give_back(dy, full_down.reshape(local_experts, hidden_units, width), owners)
-    returned_rows = back.reshape(experts * capacity, hidden_units)[position]
-    qf = returned_rows.reshape(tokens, top, hidden_units).astype(jnp.float32)
+    take = (position.reshape(tokens, top, 1)
+            == jnp.arange(experts * capacity, dtype=jnp.int32)[None, None, :]).astype(jnp.bfloat16)
+    qf = jnp.einsum(
+        "tkr,rf->tkf", take, back.reshape(experts * capacity, hidden_units),
+        preferred_element_type=jnp.float32,
+    )
     route_grad = jnp.sum(qf * hidden.astype(jnp.float32), -1)
     d_hidden = weights * qf
     d_gate = d_hidden * up * sig * (1.0 + gate * (1.0 - sig))

time: 226 us -> 224 us (level)
  other arithmetic: 20.9 us -> 13.5 us
  matrix products: 14.2 us -> 20.7 us
  Pallas kernels: 136 us -> 130 us
  waiting for transfers between devices: 19.9 us -> 24.2 us
    dot_general x0 -> x1, matrix products: none -> 6.51 us  [local(): jnp.einsum('tkr,rf->tkf', take, back.reshape(experts * capacity, hidden_u...]
    gather x1 -> x0, local copies, waits for them, and re-layouts: 5.21 us -> none  [local(): returned_rows = back.reshape(experts * capacity, hidden_units)[position]]
    all_gather x1, waiting for transfers between devices: 19.2 us -> 23.5 us  [local(): cot_group = lax.all_gather(cotangent, 'expert', axis=0, tiled=True)]
    another operation x1 -> x0, other arithmetic: 4.24 us -> none
    pallas_call x1, Pallas kernels: 66.7 us -> 62.9 us  [give_back(): pl.pallas_call(lambda *refs: return_kernel(owners, *refs), out_shape=jax....]
    reshape x1 -> x0, other arithmetic: 3.58 us -> none  [local(): scaled.reshape(routes, hidden_units)[route_of_slot]]
    pallas_call x1, Pallas kernels: 69.6 us -> 67.2 us  [exchange(): pl.pallas_call(lambda *refs: exchange_kernel(replicas, owners, pieces, *r...]
    unnamed x9 -> x16, local copies, waits for them, and re-layouts: 2.89 us -> 4.72 us
  transfers between devices with their start and end apart: 2 -> 2, of which waited for: 1 -> 1; matrix products, arithmetic and copies ran while one was open for 15% -> 15% of each run, Pallas kernels for 61% -> 59%
where the time goes in v11:
time: 224 us; the launch traced here: 220 us
  Pallas kernels  130 us (58%)
  waiting for transfers between devices  24.2 us (11%)
  matrix products  20.7 us (9%)
  local copies, waits for them, and re-layouts  17.4 us (8%)
  between operations  14.2 us (6%)
  other arithmetic  13.5 us (6%)
    pallas_call x1, Pallas kernels, exchange(): pl.pallas_call(lambda *refs: exchange_kernel(replicas, owners, pieces, *r...  67.2 us
    pallas_call x1, Pallas kernels, give_back(): pl.pallas_call(lambda *refs: return_kernel(owners, *refs), out_shape=jax....  62.9 us
    all_gather x1, waiting for transfers between devices, local(): cot_group = lax.all_gather(cotangent, 'expert', axis=0, tiled=True)  23.5 us
    gather x1, local copies, waits for them, and re-layouts, local(): scaled.reshape(routes, hidden_units)[route_of_slot]  9.4 us
    dot_general x2, matrix products, local(): jnp.einsum('scf,scd->fd', h_got[:, j], dy[:, j], preferred_element_type=j...  7.46 us
    dot_general x1, matrix products, local(): jnp.einsum('tkr,rf->tkf', take, back.reshape(experts * capacity, hidden_u...  6.51 us
    dot_general x1, matrix products, local(): jnp.einsum('sct,std->scd', pick, cot_group.reshape(owners, tokens, width)...  6.24 us
    unnamed x16, local copies, waits for them, and re-layouts  4.72 us
  transfers between devices with their start and end apart: 2, of which 1 were waited for; matrix products, arithmetic and copies ran while one was open for 15% of the time, Pallas kernels for 59%

profile of v11, /device:TPU:64, one launch (start us, length us, event | category | flops | bytes accessed | tf_op | source)
XLA Modules:
  0.0 220.2 jit_solution(4093791519567880619)
XLA Ops:
  7.2 0.0 all-gather.2.cloned.1.call-start
  7.2 0.7 all-gather.2.cloned.1.call-update
  7.9 0.0 reduce-scatter.2.cloned.1.call-start
  7.9 0.8 copy.35
  8.7 0.1 eq.56
  8.8 0.5 fusion.21
  9.4 1.0 fusion
  10.4 0.1 broadcast_in_dim.28
  10.5 0.0 copy-start.5
  10.5 2.1 fusion.27
  12.6 0.0 copy-start.1
  12.6 0.0 copy-done.5
  12.6 2.3 %fusion.10 = (bf16[128,8,768]{2,0,1:T(8,128)(2,1)S(1)}, bf16[128,8,768]{2,0,1:T(8,128)(2,1)}) fusion(f32[128,8]{0,1:T(8,128)S(1)} %copy-done.5, bf16[128,8,768]{2,1,0:T(8,128)(2,1)S(1)} %get-tuple-element.37, bf16[128,8,768]{2,1,0:T(8,128)(2,1)S(1)} %get-tuple-element.36), kind=kLoop, calls=%fused_computation.27 | loop fusion | flops 8650752 | bytes 6295552 | tf_op jit(solution)/shard_map/convert_element_type | solution.py:248
  14.9 0.0 copy-done.1
  14.9 0.9 copy.58
  15.7 0.9 select_reduce_fusion
  16.7 9.4 %gather_fusion = bf16[2048,768]{1,0:T(8,128)(2,1)} fusion(bf16[1024,768]{1,0:T(8,128)(2,1)S(1)} %bitcast.47, s32[2048]{0:T(1024)S(1)} %broadcast_clamp_fusion), kind=kCustom, calls=%fused_computation | custom fusion | bytes 6299648 | tf_op jit(solution)/shard_map/gather | solution.py:257
  26.1 0.6 copy_select_fusion.refs_2_
  26.8 3.3 %broadcast_select_fusion.refs_1_ = bf16[16,2,64,768]{3,2,1,0:T(8,128)(2,1)} fusion(bf16[16,2,64,768]{3,2,1,0:T(8,128)(2,1)} %bitcast.52, pred[16,2,64]{2,1,0:T(4,128)(4,1)S(1)} %broadcast_in_dim.28), kind=kLoop, calls=%fused_computation.35 | loop fusion | flops 1572864 | bytes 6293504 | tf_op jit(solution)/shard_map/jit(_where)/select_n | solution.py:257
  30.0 67.2 %shard_map.76 = (bf16[2,16,48,2048]{3,2,1,0:T(8,128)(2,1)}, bf16[16,2,64,768]{3,2,1,0:T(8,128)(2,1)}, s32[16,1,128]{2,1,0:T(1,128)}) custom-call(bf16[2,48,2048]{2,1,0:T(8,128)(2,1)} %refs_0_.1, bf16[16,2,64,768]{3,2,1,0:T(8,128)(2,1)} %broadcast_select_fusion.refs_1_, s32[16,1,128]{2,1,0:T(1,128)} %copy_select_fusion.refs_2_), custom_call_target="tpu_custom_call" | custom-call | bytes 18874368 | tf_op jit(solution)/shard_map/pallas_call | solution.py:107
  97.3 23.5 %all-gather.2.cloned.1.call-done = bf16[2048,2048]{1,0:T(8,128)(2,1)} async-done(((bf16[128,2048]{1,0:T(8,128)(2,1)}), bf16[2048,2048]{1,0:T(8,128)(2,1)}) %all-gather.2.cloned.1.call-update) | async-done | bytes 8388624 | tf_op jit(solution)/shard_map/all_gather | solution.py:240
  120.8 0.0 copy-start.6
  120.8 6.2 %fusion.22 = bf16[16,128,2048]{2,1,0:T(8,128)(2,1)S(1)} fusion(bf16[16,128,2048]{2,1,0:T(8,128)(2,1)} %bitcast.48, s32[16,128]{1,0:T(8,128)} %bitcast.55), kind=kOutput, calls=%fused_computation.44 | convolution fusion | flops 1074003968 | bytes 16785408 | tf_op jit(solution)/shard_map/sct,std->scd/dot_general | solution.py:265
  127.0 0.0 copy-start
  127.0 0.0 copy-done.6
  127.0 3.7 %bitcast_convert_fusion = bf16[768,2048]{1,0:T(8,128)(2,1)S(1)} fusion(bf16[16,2,64,2048]{3,2,1,0:T(8,128)(2,1)S(1)} %bitcast.49, bf16[16,2,64,768]{3,2,1,0:T(8,128)(2,1)S(1)} %copy-done.6), kind=kOutput, calls=%fused_computation.7 | convolution fusion | flops 3222798336 | bytes 8912896 | tf_op jit(solution)/shard_map/scf,scd->fd/dot_general | solution.py:272
  130.8 0.0 copy-done
  130.8 3.7 %bitcast_convert_fusion.1 = bf16[768,2048]{1,0:T(8,128)(2,1)S(1)} fusion(bf16[16,2,64,2048]{3,2,1,0:T(8,128)(2,1)S(1)} %bitcast.50, bf16[16,2,64,768]{3,2,1,0:T(8,128)(2,1)S(1)} %copy-done.6), kind=kOutput, calls=%fused_computation.8 | convolution fusion | flops 3222798336 | bytes 8912896 | tf_op jit(solution)/shard_map/scf,scd->fd/dot_general | solution.py:272
  134.5 3.1 %pad_maximum_fusion = bf16[16,2,48,2048]{3,2,1,0:T(8,128)(2,1)} fusion(bf16[16,1,48,2048]{3,2,1,0:T(8,128)(2,1)S(1)} %bitcast.53, bf16[16,1,48,2048]{3,2,1,0:T(8,128)(2,1)S(1)} %bitcast.54), kind=kLoop, calls=%fused_computation.6 | loop fusion | flops 3145728 | bytes 12582912 | tf_op jit(solution)/shard_map/stack | solution.py:276
  137.6 0.0 copy-start.4
  137.6 0.0 reduce-scatter.2.cloned.1.call-update
  137.7 0.1 convert_element_type.53
  137.8 0.5 copy-done.4
  138.3 0.0 copy-start.2
  138.3 0.0 copy-start.3
  138.3 62.9 %shard_map.77 = bf16[16,2,64,768]{3,2,1,0:T(8,128)(2,1)S(1)} custom-call(bf16[16,2,64,2048]{3,2,1,0:T(8,128)(2,1)} %bitcast.51, bf16[2,768,2048]{2,1,0:T(8,128)(2,1)} %bitcast.60), custom_call_target="tpu_custom_call" | custom-call | flops 6442450944 | bytes 20971520 | tf_op jit(solution)/shard_map/pallas_call | solution.py:198
  201.3 0.0 copy-done.2
  201.3 0.0 copy-done.3
  201.3 6.5 %fusion.9 = (bf16[128,8,768]{2,0,1:T(8,128)(2,1)S(1)}, bf16[128,8,768]{2,0,1:T(8,128)(2,1)S(1)}, f32[128,8]{0,1:T(8,128)}) fusion(f32[128,8]{0,1:T(8,128)S(1)} %copy-done.5, bf16[128,8,768]{2,1,0:T(8,128)(2,1)S(1)} %copy-done.2, bf16[128,8,768]{2,1,0:T(8,128)(2,1)S(1)} %get-tuple-element.36, bf16[128,8,768]{2,0,1:T(8,128)(2,1)S(1)} %copy-done.3, ...), kind=kOutput, calls=%fused_computation.26 | convolution fusion | flops 3238263808 | bytes 11022336 | tf_op jit(solution)/shard_map/tkr,rf->tkf/dot_general | solution.py:283
  207.8 0.3 pad_maximum_fusion.1
  208.1 3.4 %copy.43 = bf16[128,8,1536]{2,1,0:T(8,128)(2,1)} copy(bf16[128,8,1536]{2,0,1:T(8,128)(2,1)S(1)} %pad_maximum_fusion.1) | data formatting | bytes 6291456
  211.4 0.0 reduce-scatter.2.cloned.1.call-done
  211.4 1.9 bitcast_convert_fusion.2
  (6 shorter events, 0.1 us)
Async XLA Ops:
  7.2 113.6 %all-gather.2.cloned.1.call-start = ((), (), s32[]{:S(2)}) async-start(), calls=%async_computation.1 | async-start | bytes 8912896 | tf_op jit(solution)/shard_map/all_gather | solution.py:240
  7.9 203.5 %reduce-scatter.2.cloned.1.call-start = ((), (), s32[]{:S(2)}) async-start(), calls=%async_computation.2 | async-start | bytes 6684672 | tf_op jit(solution)/shard_map/reduce_scatter | solution.py:278
  10.5 2.1 copy-start.5
  12.6 2.3 %copy-start.1 = (bf16[128,8,768]{2,1,0:T(8,128)(2,1)}, bf16[128,8,768]{2,1,0:T(8,128)(2,1)S(1)}, u32[]{:S(2)}) copy-start(bf16[128,8,768]{2,1,0:T(8,128)(2,1)S(1)} %get-tuple-element.37) | copy-start | bytes 4718596
  120.8 6.3 %copy-start.6 = (bf16[16,2,64,768]{3,2,1,0:T(8,128)(2,1)S(1)}, bf16[16,2,64,768]{3,2,1,0:T(8,128)(2,1)}, u32[]{:S(2)}) copy-start(bf16[16,2,64,768]{3,2,1,0:T(8,128)(2,1)} %get-tuple-element.13) | copy-start | bytes 9437188
  127.0 3.8 %copy-start = (bf16[16,128,2048]{2,1,0:T(8,128)(2,1)}, bf16[16,128,2048]{2,1,0:T(8,128)(2,1)S(1)}, u32[]{:S(2)}) copy-start(bf16[16,128,2048]{2,1,0:T(8,128)(2,1)S(1)} %fusion.22) | copy-start | bytes 25165828
  137.6 0.7 copy-start.4
  138.3 62.9 %copy-start.2 = (bf16[128,8,768]{2,1,0:T(8,128)(2,1)S(1)}, bf16[128,8,768]{2,1,0:T(8,128)(2,1)}, u32[]{:S(2)}) copy-start(bf16[128,8,768]{2,1,0:T(8,128)(2,1)} %copy-done.1) | copy-start | bytes 4718596
  138.3 62.9 %copy-start.3 = (bf16[128,8,768]{2,0,1:T(8,128)(2,1)S(1)}, bf16[128,8,768]{2,0,1:T(8,128)(2,1)}, u32[]{:S(2)}) copy-start(bf16[128,8,768]{2,0,1:T(8,128)(2,1)} %get-tuple-element.32) | copy-start | bytes 4718596
Sparse Core Ops, SparseCore 0:
  10.4 110.2 all-gather.1
  137.8 62.9 reduce-scatter.1

commit v12 on v8

--- a/solution.py
+++ b/solution.py
@@ -278,8 +278,9 @@
     summed = lax.psum_scatter(stacked, "dp", scatter_dimension=0, tiled=True)
     grad_down = summed[0].astype(jnp.float32)
     back = give_back(dy, full_down.reshape(local_experts, hidden_units, width), owners)
-    returned_rows = back.reshape(experts * capacity, hidden_units)[position]
-    qf = returned_rows.reshape(tokens, top, hidden_units).astype(jnp.float32)
+    take = (position[:, None] == jnp.arange(experts * capacity, dtype=jnp.int32)[None, :]).astype(jnp.bfloat16)
+    rows = jnp.dot(take, back.reshape(experts * capacity, hidden_units), preferred_element_type=jnp.bfloat16)
+    qf = lax.optimization_barrier(rows).reshape(tokens, top, hidden_units).astype(jnp.float32)
     route_grad = jnp.sum(qf * hidden.astype(jnp.float32), -1)
     d_hidden = weights * qf
     d_gate = d_hidden * up * sig * (1.0 + gate * (1.0 - sig))

time: 226 us -> 226 us (level)
  waiting for transfers between devices: 19.9 us -> 26.2 us
  local copies, waits for them, and re-layouts: 17.9 us -> 11.8 us
  Pallas kernels: 136 us -> 132 us
  matrix products: 14.2 us -> 18 us
    all_gather x1, waiting for transfers between devices: 19.2 us -> 25.5 us  [local(): cot_group = lax.all_gather(cotangent, 'expert', axis=0, tiled=True)]
    pallas_call x1, Pallas kernels: 66.7 us -> 61.2 us  [give_back(): pl.pallas_call(lambda *refs: return_kernel(owners, *refs), out_shape=jax....]
    gather x1 -> x0, local copies, waits for them, and re-layouts: 5.21 us -> none  [local(): returned_rows = back.reshape(experts * capacity, hidden_units)[position]]
    dot_general x0 -> x1, matrix products: none -> 3.72 us  [local(): jnp.dot(take, back.reshape(experts * capacity, hidden_units), preferred_e...]
  transfers between devices with their start and end apart: 2 -> 2, of which waited for: 1 -> 1; matrix products, arithmetic and copies ran while one was open for 15% -> 14% of each run, Pallas kernels for 61% -> 59%
where the time goes in v12:
time: 226 us; the launch traced here: 223 us
  Pallas kernels  132 us (58%)
  waiting for transfers between devices  26.2 us (12%)
  other arithmetic  20.2 us (9%)
  matrix products  18 us (8%)
  between operations  14.2 us (6%)
  local copies, waits for them, and re-layouts  11.8 us (5%)
    pallas_call x1, Pallas kernels, exchange(): pl.pallas_call(lambda *refs: exchange_kernel(replicas, owners, pieces, *r...  71.2 us
    pallas_call x1, Pallas kernels, give_back(): pl.pallas_call(lambda *refs: return_kernel(owners, *refs), out_shape=jax....  61.2 us
    all_gather x1, waiting for transfers between devices, local(): cot_group = lax.all_gather(cotangent, 'expert', axis=0, tiled=True)  25.5 us
    gather x1, local copies, waits for them, and re-layouts, local(): scaled.reshape(routes, hidden_units)[route_of_slot]  9.4 us
    dot_general x2, matrix products, local(): jnp.einsum('scf,scd->fd', h_got[:, j], dy[:, j], preferred_element_type=j...  7.45 us
    dot_general x1, matrix products, local(): jnp.einsum('sct,std->scd', pick, cot_group.reshape(owners, tokens, width)...  6.24 us
  transfers between devices with their start and end apart: 2, of which 1 were waited for; matrix products, arithmetic and copies ran while one was open for 14% of the time, Pallas kernels for 59%

profile of v12, /device:TPU:64, one launch (start us, length us, event | category | flops | bytes accessed | tf_op | source)
XLA Modules:
  0.0 223.0 jit_solution(6798583913705726038)
XLA Ops:
  7.2 0.0 all-gather.2.cloned.1.call-start
  7.2 0.7 all-gather.2.cloned.1.call-update
  7.9 0.0 reduce-scatter.2.cloned.1.call-start
  7.9 0.8 copy.22
  8.7 0.8 copy.23
  9.5 0.1 reshape.153
  9.6 0.5 fusion.24
  10.2 1.0 fusion
  11.2 0.1 broadcast_in_dim.28
  11.3 0.9 select_reduce_fusion
  12.2 2.5 %fusion.18 = (bf16[1024,768]{1,0:T(8,128)(2,1)S(1)}, bf16[128,8,768]{2,1,0:T(8,128)(2,1)S(1)}) fusion(f32[128,8]{1,0:T(8,128)S(1)} %copy.22, bf16[128,8,1536]{2,1,0:T(8,128)(2,1)} %param.6), kind=kLoop, calls=%fused_computation.38 | loop fusion | flops 8650752 | bytes 6295552 | tf_op jit(solution)/shard_map/reshape | solution.py:257
  14.8 9.4 %gather_fusion = bf16[2048,768]{1,0:T(8,128)(2,1)} fusion(bf16[1024,768]{1,0:T(8,128)(2,1)S(1)} %get-tuple-element.25, s32[2048]{0:T(1024)S(1)} %broadcast_clamp_fusion), kind=kCustom, calls=%fused_computation | custom fusion | bytes 6299648 | tf_op jit(solution)/shard_map/gather | solution.py:257
  24.2 0.6 copy_select_fusion.refs_2_
  24.8 3.4 %broadcast_select_fusion.refs_1_ = bf16[16,2,64,768]{3,2,1,0:T(8,128)(2,1)} fusion(bf16[16,2,64,768]{3,2,1,0:T(8,128)(2,1)} %bitcast.53, pred[16,2,64]{2,1,0:T(4,128)(4,1)S(1)} %broadcast_in_dim.28), kind=kLoop, calls=%fused_computation.37 | loop fusion | flops 1572864 | bytes 6293504 | tf_op jit(solution)/shard_map/jit(_where)/select_n | solution.py:257
  28.2 71.2 %shard_map.76 = (bf16[2,16,48,2048]{3,2,1,0:T(8,128)(2,1)}, bf16[16,2,64,768]{3,2,1,0:T(8,128)(2,1)}, s32[16,1,128]{2,1,0:T(1,128)}) custom-call(bf16[2,48,2048]{2,1,0:T(8,128)(2,1)} %refs_0_.1, bf16[16,2,64,768]{3,2,1,0:T(8,128)(2,1)} %broadcast_select_fusion.refs_1_, s32[16,1,128]{2,1,0:T(1,128)} %copy_select_fusion.refs_2_), custom_call_target="tpu_custom_call" | custom-call | bytes 18874368 | tf_op jit(solution)/shard_map/pallas_call | solution.py:107
  99.5 25.5 %all-gather.2.cloned.1.call-done = bf16[2048,2048]{1,0:T(8,128)(2,1)} async-done(((bf16[128,2048]{1,0:T(8,128)(2,1)}), bf16[2048,2048]{1,0:T(8,128)(2,1)}) %all-gather.2.cloned.1.call-update) | async-done | bytes 8388624 | tf_op jit(solution)/shard_map/all_gather | solution.py:240
  125.0 0.0 copy-start.2
  125.0 6.2 %fusion.25 = bf16[16,128,2048]{2,1,0:T(8,128)(2,1)S(1)} fusion(bf16[16,128,2048]{2,1,0:T(8,128)(2,1)} %bitcast.49, s32[16,128]{1,0:T(8,128)} %bitcast.56), kind=kOutput, calls=%fused_computation.46 | convolution fusion | flops 1074003968 | bytes 16785408 | tf_op jit(solution)/shard_map/sct,std->scd/dot_general | solution.py:265
  131.3 0.0 copy-start
  131.3 0.0 copy-done.2
  131.3 3.7 %bitcast_convert_fusion = bf16[768,2048]{1,0:T(8,128)(2,1)S(1)} fusion(bf16[16,2,64,2048]{3,2,1,0:T(8,128)(2,1)S(1)} %bitcast.50, bf16[16,2,64,768]{3,2,1,0:T(8,128)(2,1)S(1)} %copy-done.2), kind=kOutput, calls=%fused_computation.7 | convolution fusion | flops 3222798336 | bytes 8912896 | tf_op jit(solution)/shard_map/scf,scd->fd/dot_general | solution.py:272
  135.0 0.0 copy-done
  135.0 3.7 %bitcast_convert_fusion.1 = bf16[768,2048]{1,0:T(8,128)(2,1)S(1)} fusion(bf16[16,2,64,2048]{3,2,1,0:T(8,128)(2,1)S(1)} %bitcast.51, bf16[16,2,64,768]{3,2,1,0:T(8,128)(2,1)S(1)} %copy-done.2), kind=kOutput, calls=%fused_computation.8 | convolution fusion | flops 3222798336 | bytes 8912896 | tf_op jit(solution)/shard_map/scf,scd->fd/dot_general | solution.py:272
  138.8 3.1 %pad_maximum_fusion = bf16[16,2,48,2048]{3,2,1,0:T(8,128)(2,1)} fusion(bf16[16,1,48,2048]{3,2,1,0:T(8,128)(2,1)S(1)} %bitcast.54, bf16[16,1,48,2048]{3,2,1,0:T(8,128)(2,1)S(1)} %bitcast.55), kind=kLoop, calls=%fused_computation.6 | loop fusion | flops 3145728 | bytes 12582912 | tf_op jit(solution)/shard_map/stack | solution.py:276
  141.9 0.0 reduce-scatter.2.cloned.1.call-update
  141.9 61.2 %shard_map.77 = bf16[16,2,64,768]{3,2,1,0:T(8,128)(2,1)S(1)} custom-call(bf16[16,2,64,2048]{3,2,1,0:T(8,128)(2,1)} %bitcast.52, bf16[2,768,2048]{2,1,0:T(8,128)(2,1)} %bitcast.61), custom_call_target="tpu_custom_call" | custom-call | flops 6442450944 | bytes 20971520 | tf_op jit(solution)/shard_map/pallas_call | solution.py:198
  203.2 0.0 copy-start.1
  203.2 3.7 %fusion.1 = bf16[1024,768]{1,0:T(8,128)(2,1)S(1)} fusion(bf16[2048,768]{1,0:T(8,128)(2,1)S(1)} %bitcast.48, s32[1024]{0:T(1024)S(1)} %convert_add_fusion), kind=kOutput, calls=%fused_computation.5 | convolution fusion | flops 3223322624 | bytes 4722688 | tf_op jit(solution)/shard_map/dot_general | solution.py:282
  206.9 0.0 copy-done.1
  206.9 3.3 %fusion.11 = (bf16[128,8,768]{2,1,0:T(8,128)(2,1)S(1)}, bf16[128,8,768]{2,1,0:T(8,128)(2,1)}, f32[128,8]{1,0:T(8,128)S(1)}) fusion(bf16[1024,768]{1,0:T(8,128)(2,1)S(1)} %fusion.1, f32[128,8]{1,0:T(8,128)S(1)} %copy.22, bf16[128,8,1536]{2,1,0:T(8,128)(2,1)S(1)} %copy-done.1, bf16[128,8,768]{2,1,0:T(8,128)(2,1)S(1)} %get-tuple-element.26), kind=kLoop, calls=%fused_computation.29 | loop fusion | flops 15727616 | bytes 9445376 | tf_op jit(solution)/shard_map/convert.2
  210.2 0.7 copy.27
  210.9 3.3 %pad_maximum_fusion.1 = bf16[128,8,1536]{2,1,0:T(8,128)(2,1)} fusion(bf16[128,8,768]{2,1,0:T(8,128)(2,1)} %get-tuple-element.28, bf16[128,8,768]{2,1,0:T(8,128)(2,1)S(1)} %get-tuple-element.27), kind=kLoop, calls=%fused_computation.36 | loop fusion | flops 6291456 | bytes 6291456 | tf_op jit(solution)/shard_map/concatenate | solution.py:288
  214.2 0.0 reduce-scatter.2.cloned.1.call-done
  214.2 1.9 bitcast_convert_fusion.2
  (3 shorter events, 0.0 us)
Async XLA Ops:
  7.2 117.8 %all-gather.2.cloned.1.call-start = ((), (), s32[]{:S(2)}) async-start(), calls=%async_computation.1 | async-start | bytes 8912896 | tf_op jit(solution)/shard_map/all_gather | solution.py:240
  7.9 206.3 %reduce-scatter.2.cloned.1.call-start = ((), (), s32[]{:S(2)}) async-start(), calls=%async_computation.2 | async-start | bytes 6684672 | tf_op jit(solution)/shard_map/reduce_scatter | solution.py:278
  125.0 6.3 %copy-start.2 = (bf16[16,2,64,768]{3,2,1,0:T(8,128)(2,1)S(1)}, bf16[16,2,64,768]{3,2,1,0:T(8,128)(2,1)}, u32[]{:S(2)}) copy-start(bf16[16,2,64,768]{3,2,1,0:T(8,128)(2,1)} %get-tuple-element.13) | copy-start | bytes 9437188
  131.3 3.8 %copy-start = (bf16[16,128,2048]{2,1,0:T(8,128)(2,1)}, bf16[16,128,2048]{2,1,0:T(8,128)(2,1)S(1)}, u32[]{:S(2)}) copy-start(bf16[16,128,2048]{2,1,0:T(8,128)(2,1)S(1)} %fusion.25) | copy-start | bytes 25165828
  203.2 3.7 %copy-start.1 = (bf16[128,8,1536]{2,1,0:T(8,128)(2,1)S(1)}, bf16[128,8,1536]{2,1,0:T(8,128)(2,1)}, u32[]{:S(2)}) copy-start(bf16[128,8,1536]{2,1,0:T(8,128)(2,1)} %param.6) | copy-start | bytes 9437188
Sparse Core Ops, SparseCore 0:
  10.4 114.5 all-gather.1
  142.0 58.6 reduce-scatter.1

commit v13 on v11

--- a/solution.py
+++ b/solution.py
@@ -136,6 +136,14 @@
     col = lax.axis_index("expert")
     local_experts = w_ref.shape[0]
 
+    def grads_of(source):
+        for j in range(local_experts):
+            gbuf[source, j] = lax.dot_general(
+                dy_ref[source, j], w_ref[j], (((1,), (1,)), ((), ())),
+                preferred_element_type=jnp.float32,
+            ).astype(gbuf.dtype)
+
+    grads_of(lax.rem(col + 1, owners))
     barrier = pltpu.get_barrier_semaphore()
     for peer in range(owners - 1):
         other = lax.rem(col + 1 + peer, owners)
@@ -153,22 +161,13 @@
         )
 
     def step(i, carry):
-        source = lax.rem(col + 1 + i, owners)
+        grads_of(lax.rem(col + 1 + i, owners))
+        previous = lax.rem(col + i, owners)
         for j in range(local_experts):
-            gbuf[source, j] = lax.dot_general(
-                dy_ref[source, j], w_ref[j], (((1,), (1,)), ((), ())),
-                preferred_element_type=jnp.float32,
-            ).astype(gbuf.dtype)
-
-        @pl.when(i > 0)
-        def _():
-            previous = lax.rem(col + i, owners)
-            for j in range(local_experts):
-                send(previous, j).start()
-
+            send(previous, j).start()
         return carry
 
-    lax.fori_loop(0, owners, step, 0)
+    lax.fori_loop(1, owners, step, 0)
     own = pltpu.make_async_copy(gbuf.at[col], back_ref.at[col], own_sem)
     own.start()
 

time: 224 us -> 224 us (level)
  no operation moved by 1% of the time
where the time goes in v13:
time: 224 us; the launch traced here: 220 us
  Pallas kernels  130 us (58%)
  waiting for transfers between devices  24.2 us (11%)
  matrix products  20.6 us (9%)
  local copies, waits for them, and re-layouts  17.4 us (8%)
  between operations  14.2 us (6%)
  other arithmetic  13.5 us (6%)
    pallas_call x1, Pallas kernels, exchange(): pl.pallas_call(lambda *refs: exchange_kernel(replicas, owners, pieces, *r...  67.2 us
    pallas_call x1, Pallas kernels, give_back(): pl.pallas_call(lambda *refs: return_kernel(owners, *refs), out_shape=jax....  62.9 us
    all_gather x1, waiting for transfers between devices, local(): cot_group = lax.all_gather(cotangent, 'expert', axis=0, tiled=True)  23.5 us
    gather x1, local copies, waits for them, and re-layouts, local(): scaled.reshape(routes, hidden_units)[route_of_slot]  9.4 us
    dot_general x2, matrix products, local(): jnp.einsum('scf,scd->fd', h_got[:, j], dy[:, j], preferred_element_type=j...  7.46 us
    dot_general x1, matrix products, local(): jnp.einsum('tkr,rf->tkf', take, back.reshape(experts * capacity, hidden_u...  6.33 us
    dot_general x1, matrix products, local(): jnp.einsum('sct,std->scd', pick, cot_group.reshape(owners, tokens, width)...  6.24 us
    unnamed x16, local copies, waits for them, and re-layouts  4.72 us
  transfers between devices with their start and end apart: 2, of which 1 were waited for; matrix products, arithmetic and copies ran while one was open for 15% of the time, Pallas kernels for 59%

profile of v13, /device:TPU:64, one launch (start us, length us, event | category | flops | bytes accessed | tf_op | source)
XLA Modules:
  0.0 220.1 jit_solution(16558382886771040463)
XLA Ops:
  7.2 0.0 all-gather.2.cloned.1.call-start
  7.2 0.7 all-gather.2.cloned.1.call-update
  7.9 0.0 reduce-scatter.2.cloned.1.call-start
  7.9 0.8 copy.35
  8.7 0.1 eq.56
  8.8 0.5 fusion.21
  9.4 1.0 fusion
  10.4 0.1 broadcast_in_dim.28
  10.5 0.0 copy-start.5
  10.5 2.1 fusion.27
  12.6 0.0 copy-start.1
  12.6 0.0 copy-done.5
  12.6 2.3 %fusion.10 = (bf16[128,8,768]{2,0,1:T(8,128)(2,1)S(1)}, bf16[128,8,768]{2,0,1:T(8,128)(2,1)}) fusion(f32[128,8]{0,1:T(8,128)S(1)} %copy-done.5, bf16[128,8,768]{2,1,0:T(8,128)(2,1)S(1)} %get-tuple-element.37, bf16[128,8,768]{2,1,0:T(8,128)(2,1)S(1)} %get-tuple-element.36), kind=kLoop, calls=%fused_computation.27 | loop fusion | flops 8650752 | bytes 6295552 | tf_op jit(solution)/shard_map/convert_element_type | solution.py:247
  14.9 0.0 copy-done.1
  14.9 0.9 copy.58
  15.7 0.9 select_reduce_fusion
  16.7 9.4 %gather_fusion = bf16[2048,768]{1,0:T(8,128)(2,1)} fusion(bf16[1024,768]{1,0:T(8,128)(2,1)S(1)} %bitcast.47, s32[2048]{0:T(1024)S(1)} %broadcast_clamp_fusion), kind=kCustom, calls=%fused_computation | custom fusion | bytes 6299648 | tf_op jit(solution)/shard_map/gather | solution.py:256
  26.1 0.6 copy_select_fusion.refs_2_
  26.8 3.3 %broadcast_select_fusion.refs_1_ = bf16[16,2,64,768]{3,2,1,0:T(8,128)(2,1)} fusion(bf16[16,2,64,768]{3,2,1,0:T(8,128)(2,1)} %bitcast.52, pred[16,2,64]{2,1,0:T(4,128)(4,1)S(1)} %broadcast_in_dim.28), kind=kLoop, calls=%fused_computation.35 | loop fusion | flops 1572864 | bytes 6293504 | tf_op jit(solution)/shard_map/jit(_where)/select_n | solution.py:256
  30.0 67.2 %shard_map.76 = (bf16[2,16,48,2048]{3,2,1,0:T(8,128)(2,1)}, bf16[16,2,64,768]{3,2,1,0:T(8,128)(2,1)}, s32[16,1,128]{2,1,0:T(1,128)}) custom-call(bf16[2,48,2048]{2,1,0:T(8,128)(2,1)} %refs_0_.1, bf16[16,2,64,768]{3,2,1,0:T(8,128)(2,1)} %broadcast_select_fusion.refs_1_, s32[16,1,128]{2,1,0:T(1,128)} %copy_select_fusion.refs_2_), custom_call_target="tpu_custom_call" | custom-call | bytes 18874368 | tf_op jit(solution)/shard_map/pallas_call | solution.py:107
  97.3 23.5 %all-gather.2.cloned.1.call-done = bf16[2048,2048]{1,0:T(8,128)(2,1)} async-done(((bf16[128,2048]{1,0:T(8,128)(2,1)}), bf16[2048,2048]{1,0:T(8,128)(2,1)}) %all-gather.2.cloned.1.call-update) | async-done | bytes 8388624 | tf_op jit(solution)/shard_map/all_gather | solution.py:239
  120.8 0.0 copy-start.6
  120.8 6.2 %fusion.22 = bf16[16,128,2048]{2,1,0:T(8,128)(2,1)S(1)} fusion(bf16[16,128,2048]{2,1,0:T(8,128)(2,1)} %bitcast.48, s32[16,128]{1,0:T(8,128)} %bitcast.55), kind=kOutput, calls=%fused_computation.44 | convolution fusion | flops 1074003968 | bytes 16785408 | tf_op jit(solution)/shard_map/sct,std->scd/dot_general | solution.py:264
  127.0 0.0 copy-start
  127.0 0.0 copy-done.6
  127.0 3.7 %bitcast_convert_fusion = bf16[768,2048]{1,0:T(8,128)(2,1)S(1)} fusion(bf16[16,2,64,2048]{3,2,1,0:T(8,128)(2,1)S(1)} %bitcast.49, bf16[16,2,64,768]{3,2,1,0:T(8,128)(2,1)S(1)} %copy-done.6), kind=kOutput, calls=%fused_computation.7 | convolution fusion | flops 3222798336 | bytes 8912896 | tf_op jit(solution)/shard_map/scf,scd->fd/dot_general | solution.py:271
  130.8 0.0 copy-done
  130.8 3.7 %bitcast_convert_fusion.1 = bf16[768,2048]{1,0:T(8,128)(2,1)S(1)} fusion(bf16[16,2,64,2048]{3,2,1,0:T(8,128)(2,1)S(1)} %bitcast.50, bf16[16,2,64,768]{3,2,1,0:T(8,128)(2,1)S(1)} %copy-done.6), kind=kOutput, calls=%fused_computation.8 | convolution fusion | flops 3222798336 | bytes 8912896 | tf_op jit(solution)/shard_map/scf,scd->fd/dot_general | solution.py:271
  134.5 3.1 %pad_maximum_fusion = bf16[16,2,48,2048]{3,2,1,0:T(8,128)(2,1)} fusion(bf16[16,1,48,2048]{3,2,1,0:T(8,128)(2,1)S(1)} %bitcast.53, bf16[16,1,48,2048]{3,2,1,0:T(8,128)(2,1)S(1)} %bitcast.54), kind=kLoop, calls=%fused_computation.6 | loop fusion | flops 3145728 | bytes 12582912 | tf_op jit(solution)/shard_map/stack | solution.py:275
  137.6 0.0 copy-start.4
  137.6 0.0 reduce-scatter.2.cloned.1.call-update
  137.7 0.1 convert_element_type.53
  137.8 0.5 copy-done.4
  138.3 0.0 copy-start.2
  138.3 0.0 copy-start.3
  138.3 62.9 %shard_map.77 = bf16[16,2,64,768]{3,2,1,0:T(8,128)(2,1)S(1)} custom-call(bf16[16,2,64,2048]{3,2,1,0:T(8,128)(2,1)} %bitcast.51, bf16[2,768,2048]{2,1,0:T(8,128)(2,1)} %bitcast.60), custom_call_target="tpu_custom_call" | custom-call | flops 6442450944 | bytes 20971520 | tf_op jit(solution)/shard_map/pallas_call | solution.py:197
  201.3 0.0 copy-done.2
  201.3 0.0 copy-done.3
  201.3 6.3 %fusion.9 = (bf16[128,8,768]{2,0,1:T(8,128)(2,1)S(1)}, bf16[128,8,768]{2,0,1:T(8,128)(2,1)S(1)}, f32[128,8]{0,1:T(8,128)}) fusion(f32[128,8]{0,1:T(8,128)S(1)} %copy-done.5, bf16[128,8,768]{2,1,0:T(8,128)(2,1)S(1)} %copy-done.2, bf16[128,8,768]{2,1,0:T(8,128)(2,1)S(1)} %get-tuple-element.36, bf16[128,8,768]{2,0,1:T(8,128)(2,1)S(1)} %copy-done.3, ...), kind=kOutput, calls=%fused_computation.26 | convolution fusion | flops 3238263808 | bytes 11022336 | tf_op jit(solution)/shard_map/tkr,rf->tkf/dot_general | solution.py:282
  207.6 0.3 pad_maximum_fusion.1
  207.9 3.4 %copy.43 = bf16[128,8,1536]{2,1,0:T(8,128)(2,1)} copy(bf16[128,8,1536]{2,0,1:T(8,128)(2,1)S(1)} %pad_maximum_fusion.1) | data formatting | bytes 6291456
  211.3 0.0 reduce-scatter.2.cloned.1.call-done
  211.3 1.9 bitcast_convert_fusion.2
  (6 shorter events, 0.1 us)
Async XLA Ops:
  7.2 113.6 %all-gather.2.cloned.1.call-start = ((), (), s32[]{:S(2)}) async-start(), calls=%async_computation.1 | async-start | bytes 8912896 | tf_op jit(solution)/shard_map/all_gather | solution.py:239
  7.9 203.4 %reduce-scatter.2.cloned.1.call-start = ((), (), s32[]{:S(2)}) async-start(), calls=%async_computation.2 | async-start | bytes 6684672 | tf_op jit(solution)/shard_map/reduce_scatter | solution.py:277
  10.5 2.1 copy-start.5
  12.6 2.3 %copy-start.1 = (bf16[128,8,768]{2,1,0:T(8,128)(2,1)}, bf16[128,8,768]{2,1,0:T(8,128)(2,1)S(1)}, u32[]{:S(2)}) copy-start(bf16[128,8,768]{2,1,0:T(8,128)(2,1)S(1)} %get-tuple-element.37) | copy-start | bytes 4718596
  120.8 6.3 %copy-start.6 = (bf16[16,2,64,768]{3,2,1,0:T(8,128)(2,1)S(1)}, bf16[16,2,64,768]{3,2,1,0:T(8,128)(2,1)}, u32[]{:S(2)}) copy-start(bf16[16,2,64,768]{3,2,1,0:T(8,128)(2,1)} %get-tuple-element.13) | copy-start | bytes 9437188
  127.0 3.8 %copy-start = (bf16[16,128,2048]{2,1,0:T(8,128)(2,1)}, bf16[16,128,2048]{2,1,0:T(8,128)(2,1)S(1)}, u32[]{:S(2)}) copy-start(bf16[16,128,2048]{2,1,0:T(8,128)(2,1)S(1)} %fusion.22) | copy-start | bytes 25165828
  137.6 0.7 copy-start.4
  138.3 63.0 %copy-start.2 = (bf16[128,8,768]{2,1,0:T(8,128)(2,1)S(1)}, bf16[128,8,768]{2,1,0:T(8,128)(2,1)}, u32[]{:S(2)}) copy-start(bf16[128,8,768]{2,1,0:T(8,128)(2,1)} %copy-done.1) | copy-start | bytes 4718596
  138.3 63.0 %copy-start.3 = (bf16[128,8,768]{2,0,1:T(8,128)(2,1)S(1)}, bf16[128,8,768]{2,0,1:T(8,128)(2,1)}, u32[]{:S(2)}) copy-start(bf16[128,8,768]{2,0,1:T(8,128)(2,1)} %get-tuple-element.32) | copy-start | bytes 4718596
Sparse Core Ops, SparseCore 0:
  10.4 110.2 all-gather.1
  137.8 62.9 reduce-scatter.1

commit v14 on v13

--- a/solution.py
+++ b/solution.py
@@ -277,12 +277,9 @@
     summed = lax.psum_scatter(stacked, "dp", scatter_dimension=0, tiled=True)
     grad_down = summed[0].astype(jnp.float32)
     back = give_back(dy, full_down.reshape(local_experts, hidden_units, width), owners)
-    take = (position.reshape(tokens, top, 1)
-            == jnp.arange(experts * capacity, dtype=jnp.int32)[None, None, :]).astype(jnp.bfloat16)
-    qf = jnp.einsum(
-        "tkr,rf->tkf", take, back.reshape(experts * capacity, hidden_units),
-        preferred_element_type=jnp.float32,
-    )
+    take = (position[:, None] == jnp.arange(experts * capacity, dtype=jnp.int32)[None, :]).astype(jnp.bfloat16)
+    rows = jnp.dot(take, back.reshape(experts * capacity, hidden_units), preferred_element_type=jnp.bfloat16)
+    qf = lax.optimization_barrier(rows).reshape(tokens, top, hidden_units).astype(jnp.float32)
     route_grad = jnp.sum(qf * hidden.astype(jnp.float32), -1)
     d_hidden = weights * qf
     d_gate = d_hidden * up * sig * (1.0 + gate * (1.0 - sig))

time: 224 us -> 226 us (level)
  other arithmetic: 13.5 us -> 20.4 us
  local copies, waits for them, and re-layouts: 17.4 us -> 11.8 us
  Pallas kernels: 130 us -> 133 us
  matrix products: 20.6 us -> 18 us
    pallas_call x1, Pallas kernels: 67.2 us -> 70.8 us  [exchange(): pl.pallas_call(lambda *refs: exchange_kernel(replicas, owners, pieces, *r...]
    another operation x0 -> x1, other arithmetic: none -> 3.29 us
    concatenate x1, other arithmetic: 0.26 us -> 3.29 us  [local(): grad_gate_up = jnp.concatenate([d_gate, d_up], -1).astype(jnp.bfloat16)]
    reshape x0 -> x1, other arithmetic: none -> 2.69 us  [local(): scaled.reshape(routes, hidden_units)[route_of_slot]]
    dot_general x1, matrix products: 6.33 us -> 3.72 us  [local(): jnp.dot(take, back.reshape(experts * capacity, hidden_units), preferred_e...]
    unnamed x16 -> x9, local copies, waits for them, and re-layouts: 4.72 us -> 2.25 us
  transfers between devices with their start and end apart: 2 -> 2, of which waited for: 1 -> 1; matrix products, arithmetic and copies ran while one was open for 15% -> 14% of each run, Pallas kernels for 59% -> 60%
where the time goes in v14:
time: 226 us; the launch traced here: 222 us
  Pallas kernels  133 us (59%)
  waiting for transfers between devices  25.5 us (11%)
  other arithmetic  20.4 us (9%)
  matrix products  18 us (8%)
  between operations  14.2 us (6%)
  local copies, waits for them, and re-layouts  11.8 us (5%)
    pallas_call x1, Pallas kernels, exchange(): pl.pallas_call(lambda *refs: exchange_kernel(replicas, owners, pieces, *r...  70.8 us
    pallas_call x1, Pallas kernels, give_back(): pl.pallas_call(lambda *refs: return_kernel(owners, *refs), out_shape=jax....  61.8 us
    all_gather x1, waiting for transfers between devices, local(): cot_group = lax.all_gather(cotangent, 'expert', axis=0, tiled=True)  24.8 us
    gather x1, local copies, waits for them, and re-layouts, local(): scaled.reshape(routes, hidden_units)[route_of_slot]  9.4 us
    dot_general x2, matrix products, local(): jnp.einsum('scf,scd->fd', h_got[:, j], dy[:, j], preferred_element_type=j...  7.46 us
    dot_general x1, matrix products, local(): jnp.einsum('sct,std->scd', pick, cot_group.reshape(owners, tokens, width)...  6.24 us
  transfers between devices with their start and end apart: 2, of which 1 were waited for; matrix products, arithmetic and copies ran while one was open for 14% of the time, Pallas kernels for 60%

profile of v14, /device:TPU:64, one launch (start us, length us, event | category | flops | bytes accessed | tf_op | source)
XLA Modules:
  0.0 222.5 jit_solution(5790856396632654455)
XLA Ops:
  7.2 0.0 all-gather.2.cloned.1.call-start
  7.2 0.7 all-gather.2.cloned.1.call-update
  7.9 0.0 reduce-scatter.2.cloned.1.call-start
  7.9 0.8 copy.22
  8.7 0.8 copy.23
  9.5 0.1 reshape.153
  9.6 0.5 fusion.24
  10.2 1.0 fusion
  11.2 0.1 broadcast_in_dim.28
  11.3 0.9 select_reduce_fusion
  12.2 2.7 %fusion.18 = (bf16[1024,768]{1,0:T(8,128)(2,1)S(1)}, bf16[128,8,768]{2,1,0:T(8,128)(2,1)S(1)}) fusion(f32[128,8]{1,0:T(8,128)S(1)} %copy.22, bf16[128,8,1536]{2,1,0:T(8,128)(2,1)} %param.6), kind=kLoop, calls=%fused_computation.38 | loop fusion | flops 8650752 | bytes 6295552 | tf_op jit(solution)/shard_map/reshape | solution.py:256
  14.9 9.4 %gather_fusion = bf16[2048,768]{1,0:T(8,128)(2,1)} fusion(bf16[1024,768]{1,0:T(8,128)(2,1)S(1)} %get-tuple-element.25, s32[2048]{0:T(1024)S(1)} %broadcast_clamp_fusion), kind=kCustom, calls=%fused_computation | custom fusion | bytes 6299648 | tf_op jit(solution)/shard_map/gather | solution.py:256
  24.4 0.6 copy_select_fusion.refs_2_
  25.0 3.4 %broadcast_select_fusion.refs_1_ = bf16[16,2,64,768]{3,2,1,0:T(8,128)(2,1)} fusion(bf16[16,2,64,768]{3,2,1,0:T(8,128)(2,1)} %bitcast.53, pred[16,2,64]{2,1,0:T(4,128)(4,1)S(1)} %broadcast_in_dim.28), kind=kLoop, calls=%fused_computation.37 | loop fusion | flops 1572864 | bytes 6293504 | tf_op jit(solution)/shard_map/jit(_where)/select_n | solution.py:256
  28.4 70.8 %shard_map.76 = (bf16[2,16,48,2048]{3,2,1,0:T(8,128)(2,1)}, bf16[16,2,64,768]{3,2,1,0:T(8,128)(2,1)}, s32[16,1,128]{2,1,0:T(1,128)}) custom-call(bf16[2,48,2048]{2,1,0:T(8,128)(2,1)} %refs_0_.1, bf16[16,2,64,768]{3,2,1,0:T(8,128)(2,1)} %broadcast_select_fusion.refs_1_, s32[16,1,128]{2,1,0:T(1,128)} %copy_select_fusion.refs_2_), custom_call_target="tpu_custom_call" | custom-call | bytes 18874368 | tf_op jit(solution)/shard_map/pallas_call | solution.py:107
  99.2 24.8 %all-gather.2.cloned.1.call-done = bf16[2048,2048]{1,0:T(8,128)(2,1)} async-done(((bf16[128,2048]{1,0:T(8,128)(2,1)}), bf16[2048,2048]{1,0:T(8,128)(2,1)}) %all-gather.2.cloned.1.call-update) | async-done | bytes 8388624 | tf_op jit(solution)/shard_map/all_gather | solution.py:239
  124.0 0.0 copy-start.2
  124.0 6.2 %fusion.25 = bf16[16,128,2048]{2,1,0:T(8,128)(2,1)S(1)} fusion(bf16[16,128,2048]{2,1,0:T(8,128)(2,1)} %bitcast.49, s32[16,128]{1,0:T(8,128)} %bitcast.56), kind=kOutput, calls=%fused_computation.46 | convolution fusion | flops 1074003968 | bytes 16785408 | tf_op jit(solution)/shard_map/sct,std->scd/dot_general | solution.py:264
  130.2 0.0 copy-start
  130.2 0.0 copy-done.2
  130.2 3.7 %bitcast_convert_fusion = bf16[768,2048]{1,0:T(8,128)(2,1)S(1)} fusion(bf16[16,2,64,2048]{3,2,1,0:T(8,128)(2,1)S(1)} %bitcast.50, bf16[16,2,64,768]{3,2,1,0:T(8,128)(2,1)S(1)} %copy-done.2), kind=kOutput, calls=%fused_computation.7 | convolution fusion | flops 3222798336 | bytes 8912896 | tf_op jit(solution)/shard_map/scf,scd->fd/dot_general | solution.py:271
  134.0 0.0 copy-done
  134.0 3.7 %bitcast_convert_fusion.1 = bf16[768,2048]{1,0:T(8,128)(2,1)S(1)} fusion(bf16[16,2,64,2048]{3,2,1,0:T(8,128)(2,1)S(1)} %bitcast.51, bf16[16,2,64,768]{3,2,1,0:T(8,128)(2,1)S(1)} %copy-done.2), kind=kOutput, calls=%fused_computation.8 | convolution fusion | flops 3222798336 | bytes 8912896 | tf_op jit(solution)/shard_map/scf,scd->fd/dot_general | solution.py:271
  137.7 3.1 %pad_maximum_fusion = bf16[16,2,48,2048]{3,2,1,0:T(8,128)(2,1)} fusion(bf16[16,1,48,2048]{3,2,1,0:T(8,128)(2,1)S(1)} %bitcast.54, bf16[16,1,48,2048]{3,2,1,0:T(8,128)(2,1)S(1)} %bitcast.55), kind=kLoop, calls=%fused_computation.6 | loop fusion | flops 3145728 | bytes 12582912 | tf_op jit(solution)/shard_map/stack | solution.py:275
  140.9 0.0 reduce-scatter.2.cloned.1.call-update
  140.9 61.8 %shard_map.77 = bf16[16,2,64,768]{3,2,1,0:T(8,128)(2,1)S(1)} custom-call(bf16[16,2,64,2048]{3,2,1,0:T(8,128)(2,1)} %bitcast.52, bf16[2,768,2048]{2,1,0:T(8,128)(2,1)} %bitcast.61), custom_call_target="tpu_custom_call" | custom-call | flops 6442450944 | bytes 20971520 | tf_op jit(solution)/shard_map/pallas_call | solution.py:197
  202.7 0.0 copy-start.1
  202.7 3.7 %fusion.1 = bf16[1024,768]{1,0:T(8,128)(2,1)S(1)} fusion(bf16[2048,768]{1,0:T(8,128)(2,1)S(1)} %bitcast.48, s32[1024]{0:T(1024)S(1)} %convert_add_fusion), kind=kOutput, calls=%fused_computation.5 | convolution fusion | flops 3223322624 | bytes 4722688 | tf_op jit(solution)/shard_map/dot_general | solution.py:281
  206.4 0.0 copy-done.1
  206.5 3.3 %fusion.11 = (bf16[128,8,768]{2,1,0:T(8,128)(2,1)S(1)}, bf16[128,8,768]{2,1,0:T(8,128)(2,1)}, f32[128,8]{1,0:T(8,128)S(1)}) fusion(bf16[1024,768]{1,0:T(8,128)(2,1)S(1)} %fusion.1, f32[128,8]{1,0:T(8,128)S(1)} %copy.22, bf16[128,8,1536]{2,1,0:T(8,128)(2,1)S(1)} %copy-done.1, bf16[128,8,768]{2,1,0:T(8,128)(2,1)S(1)} %get-tuple-element.26), kind=kLoop, calls=%fused_computation.29 | loop fusion | flops 15727616 | bytes 9445376 | tf_op jit(solution)/shard_map/convert.2
  209.7 0.7 copy.27
  210.4 3.3 %pad_maximum_fusion.1 = bf16[128,8,1536]{2,1,0:T(8,128)(2,1)} fusion(bf16[128,8,768]{2,1,0:T(8,128)(2,1)} %get-tuple-element.28, bf16[128,8,768]{2,1,0:T(8,128)(2,1)S(1)} %get-tuple-element.27), kind=kLoop, calls=%fused_computation.36 | loop fusion | flops 6291456 | bytes 6291456 | tf_op jit(solution)/shard_map/concatenate | solution.py:287
  213.7 0.0 reduce-scatter.2.cloned.1.call-done
  213.7 1.9 bitcast_convert_fusion.2
  (3 shorter events, 0.0 us)
Async XLA Ops:
  7.2 116.8 %all-gather.2.cloned.1.call-start = ((), (), s32[]{:S(2)}) async-start(), calls=%async_computation.1 | async-start | bytes 8912896 | tf_op jit(solution)/shard_map/all_gather | solution.py:239
  7.9 205.8 %reduce-scatter.2.cloned.1.call-start = ((), (), s32[]{:S(2)}) async-start(), calls=%async_computation.2 | async-start | bytes 6684672 | tf_op jit(solution)/shard_map/reduce_scatter | solution.py:277
  124.0 6.3 %copy-start.2 = (bf16[16,2,64,768]{3,2,1,0:T(8,128)(2,1)S(1)}, bf16[16,2,64,768]{3,2,1,0:T(8,128)(2,1)}, u32[]{:S(2)}) copy-start(bf16[16,2,64,768]{3,2,1,0:T(8,128)(2,1)} %get-tuple-element.13) | copy-start | bytes 9437188
  130.2 3.8 %copy-start = (bf16[16,128,2048]{2,1,0:T(8,128)(2,1)}, bf16[16,128,2048]{2,1,0:T(8,128)(2,1)S(1)}, u32[]{:S(2)}) copy-start(bf16[16,128,2048]{2,1,0:T(8,128)(2,1)S(1)} %fusion.25) | copy-start | bytes 25165828
  202.7 3.7 %copy-start.1 = (bf16[128,8,1536]{2,1,0:T(8,128)(2,1)S(1)}, bf16[128,8,1536]{2,1,0:T(8,128)(2,1)}, u32[]{:S(2)}) copy-start(bf16[128,8,1536]{2,1,0:T(8,128)(2,1)} %param.6) | copy-start | bytes 9437188
Sparse Core Ops, SparseCore 0:
  10.4 113.5 all-gather.1
  141.0 59.3 reduce-scatter.1

commit v15 on v13

--- a/solution.py
+++ b/solution.py
@@ -253,7 +253,8 @@
     match = position[None, :] == slot_ids[:, None]
     route_of_slot = jnp.sum(jnp.where(match, jnp.arange(routes, dtype=jnp.int32)[None, :], 0), axis=1)
     filled = jnp.any(match, axis=1)
-    h_rows = jnp.where(filled[:, None], scaled.reshape(routes, hidden_units)[route_of_slot], jnp.zeros((), jnp.bfloat16))
+    h_rows = jnp.dot(match.astype(jnp.bfloat16), scaled.reshape(routes, hidden_units),
+                     preferred_element_type=jnp.bfloat16)
     h_send = h_rows.reshape(owners, local_experts, capacity, hidden_units)
 
     t_send = jnp.where(filled, route_of_slot // top, -1).reshape(owners, 1, local_experts * capacity)

time: 224 us -> 231 us (1.031)
  waiting for transfers between devices: 24.2 us -> 43.3 us
  local copies, waits for them, and re-layouts: 17.4 us -> 7.02 us
  matrix products: 20.6 us -> 26.3 us
  Pallas kernels: 130 us -> 126 us
  other arithmetic: 13.5 us -> 10.4 us
    all_gather x1, waiting for transfers between devices: 23.5 us -> 42.6 us  [local(): cot_group = lax.all_gather(cotangent, 'expert', axis=0, tiled=True)]
    gather x1 -> x0, local copies, waits for them, and re-layouts: 9.4 us -> none  [local(): scaled.reshape(routes, hidden_units)[route_of_slot]]
    dot_general x0 -> x1, matrix products: none -> 5.73 us  [local(): jnp.dot(match.astype(jnp.bfloat16), scaled.reshape(routes, hidden_units),...]
    select_n x2 -> x0, other arithmetic: 3.29 us -> none  [the longest x1 3.28 us: local(): jnp.where(filled[:, None], scaled.reshape(routes, hidden_units)[route_of_...]
    pallas_call x1, Pallas kernels: 67.2 us -> 64.7 us  [exchange(): pl.pallas_call(lambda *refs: exchange_kernel(replicas, owners, pieces, *r...]
    unnamed x16 -> x12, local copies, waits for them, and re-layouts: 4.72 us -> 4.71 us
  transfers between devices with their start and end apart: 2 -> 2, of which waited for: 1 -> 1; matrix products, arithmetic and copies ran while one was open for 15% -> 11% of each run, Pallas kernels for 59% -> 55%
where the time goes in v15:
time: 231 us; the launch traced here: 228 us
  Pallas kernels  126 us (55%)
  waiting for transfers between devices  43.3 us (19%)
  matrix products  26.3 us (11%)
  between operations  14.2 us (6%)
  other arithmetic  10.4 us (5%)
  local copies, waits for them, and re-layouts  7.02 us (3%)
    pallas_call x1, Pallas kernels, exchange(): pl.pallas_call(lambda *refs: exchange_kernel(replicas, owners, pieces, *r...  64.7 us
    pallas_call x1, Pallas kernels, give_back(): pl.pallas_call(lambda *refs: return_kernel(owners, *refs), out_shape=jax....  61.6 us
    all_gather x1, waiting for transfers between devices, local(): cot_group = lax.all_gather(cotangent, 'expert', axis=0, tiled=True)  42.6 us
    dot_general x2, matrix products, local(): jnp.einsum('scf,scd->fd', h_got[:, j], dy[:, j], preferred_element_type=j...  7.46 us
    dot_general x1, matrix products, local(): jnp.einsum('tkr,rf->tkf', take, back.reshape(experts * capacity, hidden_u...  6.33 us
    dot_general x1, matrix products, local(): jnp.einsum('sct,std->scd', pick, cot_group.reshape(owners, tokens, width)...  6.24 us
    dot_general x1, matrix products, local(): jnp.dot(match.astype(jnp.bfloat16), scaled.reshape(routes, hidden_units),...  5.73 us
    unnamed x12, local copies, waits for them, and re-layouts  4.71 us
  transfers between devices with their start and end apart: 2, of which 1 were waited for; matrix products, arithmetic and copies ran while one was open for 11% of the time, Pallas kernels for 55%

profile of v15, /device:TPU:64, one launch (start us, length us, event | category | flops | bytes accessed | tf_op | source)
XLA Modules:
  0.0 227.6 jit_solution(11677449494358257916)
XLA Ops:
  7.2 0.0 all-gather.2.cloned.1.call-start
  7.2 0.7 all-gather.2.cloned.1.call-update
  7.9 0.0 reduce-scatter.2.cloned.1.call-start
  7.9 0.8 copy.35
  8.7 0.1 eq.79
  8.8 0.5 fusion.27
  9.4 1.0 fusion
  10.4 0.9 select_reduce_fusion
  11.4 0.6 copy_select_fusion.refs_2_
  12.0 0.0 copy-start.3
  12.0 2.1 fusion.33
  14.1 0.0 copy-done.3
  14.1 2.4 %fusion.14 = (bf16[128,8,768]{2,0,1:T(8,128)(2,1)S(1)}, bf16[128,8,768]{2,0,1:T(8,128)(2,1)}) fusion(f32[128,8]{0,1:T(8,128)S(1)} %copy-done.3, bf16[128,8,768]{2,1,0:T(8,128)(2,1)S(1)} %get-tuple-element.37, bf16[128,8,768]{2,1,0:T(8,128)(2,1)S(1)} %get-tuple-element.36), kind=kLoop, calls=%fused_computation.30 | loop fusion | flops 8650752 | bytes 6295552 | tf_op jit(solution)/shard_map/convert_element_type | solution.py:247
  16.5 5.7 %fusion.2.refs_1_ = bf16[16,2,64,768]{3,2,1,0:T(8,128)(2,1)} fusion(s32[16,2,64]{2,1,0:T(2,128)S(1)} %multiply_add_fusion, s32[1024]{0:T(1024)S(1)} %multiply_add_fusion.1, bf16[128,8,768]{2,0,1:T(8,128)(2,1)S(1)} %get-tuple-element.31), kind=kOutput, calls=%fused_computation.5 | convolution fusion | flops 3223322624 | bytes 4730880 | tf_op jit(solution)/shard_map/dot_general | solution.py:256
  22.3 64.7 %shard_map.76 = (bf16[2,16,48,2048]{3,2,1,0:T(8,128)(2,1)}, bf16[16,2,64,768]{3,2,1,0:T(8,128)(2,1)}, s32[16,1,128]{2,1,0:T(1,128)}) custom-call(bf16[2,48,2048]{2,1,0:T(8,128)(2,1)} %refs_0_.1, bf16[16,2,64,768]{3,2,1,0:T(8,128)(2,1)} %fusion.2.refs_1_, s32[16,1,128]{2,1,0:T(1,128)} %copy_select_fusion.refs_2_), custom_call_target="tpu_custom_call" | custom-call | bytes 18874368 | tf_op jit(solution)/shard_map/pallas_call | solution.py:107
  87.0 42.6 %all-gather.2.cloned.1.call-done = bf16[2048,2048]{1,0:T(8,128)(2,1)} async-done(((bf16[128,2048]{1,0:T(8,128)(2,1)}), bf16[2048,2048]{1,0:T(8,128)(2,1)}) %all-gather.2.cloned.1.call-update) | async-done | bytes 8388624 | tf_op jit(solution)/shard_map/all_gather | solution.py:239
  129.6 0.0 copy-start.4
  129.6 6.2 %fusion.28 = bf16[16,128,2048]{2,1,0:T(8,128)(2,1)S(1)} fusion(bf16[16,128,2048]{2,1,0:T(8,128)(2,1)} %bitcast.48, s32[16,128]{1,0:T(8,128)} %bitcast.54), kind=kOutput, calls=%fused_computation.47 | convolution fusion | flops 1074003968 | bytes 16785408 | tf_op jit(solution)/shard_map/sct,std->scd/dot_general | solution.py:265
  135.9 0.0 copy-start
  135.9 0.0 copy-done.4
  135.9 3.7 %bitcast_convert_fusion = bf16[768,2048]{1,0:T(8,128)(2,1)S(1)} fusion(bf16[16,2,64,2048]{3,2,1,0:T(8,128)(2,1)S(1)} %bitcast.49, bf16[16,2,64,768]{3,2,1,0:T(8,128)(2,1)S(1)} %copy-done.4), kind=kOutput, calls=%fused_computation.8 | convolution fusion | flops 3222798336 | bytes 8912896 | tf_op jit(solution)/shard_map/scf,scd->fd/dot_general | solution.py:272
  139.6 0.0 copy-done
  139.6 3.7 %bitcast_convert_fusion.1 = bf16[768,2048]{1,0:T(8,128)(2,1)S(1)} fusion(bf16[16,2,64,2048]{3,2,1,0:T(8,128)(2,1)S(1)} %bitcast.50, bf16[16,2,64,768]{3,2,1,0:T(8,128)(2,1)S(1)} %copy-done.4), kind=kOutput, calls=%fused_computation.9 | convolution fusion | flops 3222798336 | bytes 8912896 | tf_op jit(solution)/shard_map/scf,scd->fd/dot_general | solution.py:272
  143.4 3.1 %pad_maximum_fusion = bf16[16,2,48,2048]{3,2,1,0:T(8,128)(2,1)} fusion(bf16[16,1,48,2048]{3,2,1,0:T(8,128)(2,1)S(1)} %bitcast.52, bf16[16,1,48,2048]{3,2,1,0:T(8,128)(2,1)S(1)} %bitcast.53), kind=kLoop, calls=%fused_computation.7 | loop fusion | flops 3145728 | bytes 12582912 | tf_op jit(solution)/shard_map/stack | solution.py:276
  146.5 0.0 copy-start.2
  146.5 0.0 reduce-scatter.2.cloned.1.call-update
  146.6 0.1 convert_element_type.54
  146.7 0.5 copy-done.2
  147.2 0.0 copy-start.1
  147.2 61.6 %shard_map.77 = bf16[16,2,64,768]{3,2,1,0:T(8,128)(2,1)S(1)} custom-call(bf16[16,2,64,2048]{3,2,1,0:T(8,128)(2,1)} %bitcast.51, bf16[2,768,2048]{2,1,0:T(8,128)(2,1)} %bitcast.57), custom_call_target="tpu_custom_call" | custom-call | flops 6442450944 | bytes 20971520 | tf_op jit(solution)/shard_map/pallas_call | solution.py:197
  208.8 0.0 copy-done.1
  208.8 6.3 %fusion.13 = (bf16[128,8,768]{2,0,1:T(8,128)(2,1)S(1)}, bf16[128,8,768]{2,0,1:T(8,128)(2,1)S(1)}, f32[128,8]{0,1:T(8,128)}) fusion(f32[128,8]{0,1:T(8,128)S(1)} %copy-done.3, bf16[128,8,768]{2,1,0:T(8,128)(2,1)S(1)} %get-tuple-element.37, bf16[128,8,768]{2,1,0:T(8,128)(2,1)S(1)} %get-tuple-element.36, bf16[128,8,768]{2,0,1:T(8,128)(2,1)S(1)} %copy-done.1, ...), kind=kOutput, calls=%fused_computation.29 | convolution fusion | flops 3238263808 | bytes 11022336 | tf_op jit(solution)/shard_map/tkr,rf->tkf/dot_general | solution.py:283
  215.1 0.3 pad_maximum_fusion.1
  215.4 3.4 %copy.43 = bf16[128,8,1536]{2,1,0:T(8,128)(2,1)} copy(bf16[128,8,1536]{2,0,1:T(8,128)(2,1)S(1)} %pad_maximum_fusion.1) | data formatting | bytes 6291456
  218.8 0.0 reduce-scatter.2.cloned.1.call-done
  218.8 1.9 bitcast_convert_fusion.2
  (5 shorter events, 0.1 us)
Async XLA Ops:
  7.2 122.5 %all-gather.2.cloned.1.call-start = ((), (), s32[]{:S(2)}) async-start(), calls=%async_computation.1 | async-start | bytes 8912896 | tf_op jit(solution)/shard_map/all_gather | solution.py:239
  7.9 210.9 %reduce-scatter.2.cloned.1.call-start = ((), (), s32[]{:S(2)}) async-start(), calls=%async_computation.2 | async-start | bytes 6684672 | tf_op jit(solution)/shard_map/reduce_scatter | solution.py:278
  12.0 2.1 copy-start.3
  129.6 6.3 %copy-start.4 = (bf16[16,2,64,768]{3,2,1,0:T(8,128)(2,1)S(1)}, bf16[16,2,64,768]{3,2,1,0:T(8,128)(2,1)}, u32[]{:S(2)}) copy-start(bf16[16,2,64,768]{3,2,1,0:T(8,128)(2,1)} %get-tuple-element.13) | copy-start | bytes 9437188
  135.9 3.8 %copy-start = (bf16[16,128,2048]{2,1,0:T(8,128)(2,1)}, bf16[16,128,2048]{2,1,0:T(8,128)(2,1)S(1)}, u32[]{:S(2)}) copy-start(bf16[16,128,2048]{2,1,0:T(8,128)(2,1)S(1)} %fusion.28) | copy-start | bytes 25165828
  146.5 0.7 copy-start.2
  147.2 61.6 %copy-start.1 = (bf16[128,8,768]{2,0,1:T(8,128)(2,1)S(1)}, bf16[128,8,768]{2,0,1:T(8,128)(2,1)}, u32[]{:S(2)}) copy-start(bf16[128,8,768]{2,0,1:T(8,128)(2,1)} %get-tuple-element.32) | copy-start | bytes 4718596
Sparse Core Ops, SparseCore 0:
  10.4 119.1 all-gather.1
  146.7 61.5 reduce-scatter.1
